TPU v7x, 32 devices: a whole 2x2x4 slice. The times are simulated.
32 devices in a mesh: site: 8 (over z, y), mode: 4 (over x, core).
Axes of the slice: x: 2, y: 2, z: 4, core: 2. Of those that a mesh axis runs over, the one named last changes fastest.
Arguments:
- basis: bfloat16 [64, 400, 512], P('site', 'mode'), may hold values from -6 to 6
- images: bfloat16 [64, 400, 496], P('site', 'mode'), may hold values from -6 to 6
- hops: bfloat16 [64, 9, 400, 400], P('site', None, 'mode'), may hold values from -0.09375 to 0.09375
- neighbours: int32 [64, 8], P('site'), may hold values from 0 to 47, as said below
- rotation: bfloat16 [512, 512], replicated, may hold values from -0.25 to 0.25
Outputs:
- projected: float32 [512, 512], replicated
- rotated_basis: bfloat16 [64, 400, 512], P('site', 'mode')
- rotated_images: bfloat16 [64, 400, 512], P('site', 'mode')
Inputs may be any that keep to these rules, and one draw needn't show every extreme that they name: `neighbours`: the blocks form a periodic 4 x 4 x 4 x 64/64 lattice. Group s = 8 t + 4 gx + 2 gy + gz holds the 2 x 2 x 2 cube of time slice t at spatial offsets 2 gx, 2 gy, 2 gz, stored in its own order.
All inputs are finite; a program needn't handle non-finite values.
Results may differ from a plain program's by a relative error of at most 0.0026.
Values may be sent and summed in bfloat16 or wider, within the bound.
No kernel may reach another device: no remote copies, remote signals or barrier semaphores. Data moves between devices by JAX's collectives and lax.ppermute only.
A program may use at most 64 MiB of HBM per device.

v0:
```python
import math

import jax
import jax.numpy as jnp
from jax import lax
from jax.sharding import PartitionSpec as P

OLD = 496


def swapped(block, axis, distance):
    count = lax.axis_size(axis)
    route = []
    for low in range(count):
        high = low | 1 << distance
        if high != low and high < count:
            route += [(low, high), (high, low)]
    return lax.ppermute(block, axis, route)


def from_behind(block, axis, distance):
    devices = range(lax.axis_size(axis))
    route = [((i - distance) % len(devices), i) for i in devices]
    return lax.ppermute(block, axis, route)


def local(basis, images, hops, neighbours, rotation):
    local_blocks = basis.shape[0]
    modes_here = basis.shape[1]
    nvec = basis.shape[2]
    site_count = lax.axis_size("site")
    norm_scale = 1.0 / math.sqrt(site_count * local_blocks * modes_here * lax.axis_size("mode"))
    old_part = jnp.einsum("bci,bcj->ij", basis, images, preferred_element_type=jnp.float32)
    old_sum = lax.psum(old_part, ("site", "mode"))
    newest = jnp.transpose(basis[:, :, OLD:], (0, 2, 1))
    pieces = [newest]
    for bit in (2, 1, 0):
        pieces.append(swapped(newest, "site", bit))
    for offset in (-8, 8):
        if site_count > 8:
            pieces.append(from_behind(newest, "site", offset))
        else:
            pieces.append(newest)
    stacked = jnp.concatenate(pieces, axis=0)
    widened = lax.all_gather(stacked, "mode", axis=2, tiled=True)
    own_rows = jnp.arange(local_blocks, dtype=jnp.int32)
    row_index = jnp.concatenate([own_rows[:, None], neighbours], axis=1)
    gathered = widened[row_index]
    stencil = jnp.einsum("bdoi,bdki->bok", hops, gathered, preferred_element_type=jnp.float32)
    image_new = stencil.astype(jnp.bfloat16)
    images_all = jnp.concatenate([images, image_new], axis=2)
    new_part = jnp.einsum("bci,bck->ik", basis, image_new, preferred_element_type=jnp.float32)
    new_sum = lax.psum(new_part, ("site", "mode"))
    projected = jnp.concatenate([old_sum, new_sum], axis=1) * norm_scale
    flat_basis = basis.reshape(local_blocks * modes_here, nvec)
    flat_images = images_all.reshape(local_blocks * modes_here, nvec)
    rotated_basis = jnp.dot(flat_basis, rotation, preferred_element_type=jnp.float32).astype(
        jnp.bfloat16
    )
    rotated_images = jnp.dot(flat_images, rotation, preferred_element_type=jnp.float32).astype(
        jnp.bfloat16
    )
    return (
        projected,
        rotated_basis.reshape(local_blocks, modes_here, nvec),
        rotated_images.reshape(local_blocks, modes_here, nvec),
    )


def solution(mesh):
    placed = (
        P("site", "mode", None),
        P("site", "mode", None),
        P("site", None, "mode", None),
        P("site", None),
        P(),
    )
    return jax.shard_map(
        local,
        mesh=mesh,
        in_specs=placed,
        out_specs=(P(), P("site", "mode", None), P("site", "mode", None)),
        check_vma=False,
    )
```

profile of v0, /device:TPU:0, one launch (start us, length us, event | category | flops | bytes accessed | tf_op | source)
XLA Modules:
  0.0 156.1 jit_solution(4232743305024800474)
XLA Ops:
  7.2 0.0 all-reduce.2.cloned.1.call-start
  7.2 1.1 slice.3
  8.3 0.2 copy.50
  8.5 4.1 %collective-permute-start = (bf16[8,16,100]{2,1,0:T(8,128)(2,1)S(1)}, bf16[8,16,100]{2,1,0:T(8,128)(2,1)S(1)}, u32[]{:S(2)}, u32[]{:S(2)}) collective-permute-start(bf16[8,16,100]{2,1,0:T(8,128)(2,1)S(1)} %bitcast.32), channel_id=1, source_target_pairs={{0,16},{16,0},{4,20},{20,4},{8,24},{24,8},{12,28},{28,12},{1,17},{... | collective-permute-start | bytes 76808 | tf_op jit(solution)/shard_map/ppermute | solution.py:18
  12.6 1.6 %collective-permute-start.1 = (bf16[8,16,100]{2,1,0:T(8,128)(2,1)S(1)}, bf16[8,16,100]{2,1,0:T(8,128)(2,1)S(1)}, u32[]{:S(2)}, u32[]{:S(2)}) collective-permute-start(bf16[8,16,100]{2,1,0:T(8,128)(2,1)S(1)} %bitcast.33), channel_id=1, source_target_pairs={{0,8},{8,0},{4,12},{12,4},{16,24},{24,16},{20,28},{28,20},{1,9},{9... | collective-permute-start | bytes 76808 | tf_op jit(solution)/shard_map/ppermute | solution.py:18
  14.2 1.5 collective-permute-start.2
  15.7 3.1 %convolution_bitcast_fusion = f32[512,496]{0,1:T(8,128)} fusion(bf16[8,100,512]{2,0,1:T(8,128)(2,1)} %param.5, bf16[8,100,496]{2,0,1:T(8,128)(2,1)} %param.6), kind=kOutput, calls=%fused_computation.5 | convolution fusion | flops 406323200 | bytes 2628608 | tf_op jit(solution)/shard_map/bci,bcj->ij/dot_general | solution.py:33
  18.9 0.2 copy.42
  19.1 0.4 copy-done.4
  19.5 0.1 compare_select_fusion
  19.6 0.1 reshape.89
  19.7 0.1 reshape.83
  19.8 0.6 convolution_convert_fusion.1
  20.4 0.1 reshape.84
  20.6 1.1 copy.47
  21.8 0.4 copy.39
  22.3 14.5 %all_gather.3 = bf16[48,16,400]{0,1,2:T(8,128)(2,1)S(1)} all-gather(bf16[48,16,100]{0,1,2:T(8,128)(2,1)S(1)} %copy.39), channel_id=1, replica_groups=mesh['site'=8,'mode'=4] {'mode'}, dimensions={2}, use_global_device_ids=true | all-gather | bytes 768000 | tf_op jit(solution)/shard_map/all_gather | solution.py:45
  36.7 2.1 %copy.40 = bf16[48,16,400]{2,1,0:T(8,128)(2,1)S(1)} copy(bf16[48,16,400]{0,1,2:T(8,128)(2,1)S(1)} %all_gather.3) | data formatting | bytes 1228800 | tf_op jit(solution)/shard_map/all_gather | solution.py:45
  38.8 0.7 gather_fusion
  39.5 5.3 %fusion.8 = bf16[8,100,16]{1,2,0:T(8,128)(2,1)S(1)} fusion(bf16[8,9,16,400]{3,2,1,0:T(8,128)(2,1)S(1)} %bitcast.31, bf16[8,9,100,400]{3,0,2,1:T(8,128)(2,1)} %param.7), kind=kOutput, calls=%fused_computation.8 | convolution fusion | flops 92172800 | bytes 6707200 | tf_op jit(solution)/shard_map/bdoi,bdki->bok/dot_general | solution.py:49
  44.8 0.2 copy.44
  45.0 0.2 pad_maximum_fusion
  45.2 0.2 copy.45
  45.5 0.1 reshape.85
  45.6 0.6 convolution_convert_fusion
  46.2 0.1 reshape.86
  46.4 1.1 copy.48
  47.5 0.4 convolution_bitcast_fusion.1
  47.9 38.0 %psum.15 = f32[512,16]{0,1:T(8,128)S(1)} all-reduce(f32[512,16]{0,1:T(8,128)S(1)} %convolution_bitcast_fusion.1), channel_id=1, replica_groups=mesh['site'=8,'mode'=4] {'site','mode'}, use_global_device_ids=true, to_apply=%region_1.0 | all-reduce | flops 8192 | bytes 65536 | tf_op jit(solution)/shard_map/psum | solution.py:53
  85.9 60.7 %all-reduce.2.cloned.1.call-done = f32[512,496]{0,1:T(8,128)} async-done(((f32[512,496]{0,1:T(8,128)}), f32[512,496]{0,1:T(8,128)}) %all-reduce.2.cloned.1.call-update) | async-done | bytes 1015824 | tf_op jit(solution)/shard_map/psum | solution.py:34
  146.6 1.3 maximum_multiply_fusion
  147.9 1.3 copy.46
  (21 shorter events, 0.1 us)
Async XLA Ops:
  7.2 12.7 %copy-start = (bf16[512,512]{1,0:T(8,128)(2,1)S(1)}, bf16[512,512]{1,0:T(8,128)(2,1)}, u32[]{:S(2)}) copy-start(bf16[512,512]{1,0:T(8,128)(2,1)} %param.9) | copy-start | bytes 1572868
  7.2 139.4 %all-reduce.2.cloned.1.call-start = ((), (), s32[]{:S(2)}) async-start(), calls=%async_computation | async-start | bytes 2031616 | tf_op jit(solution)/shard_map/psum | solution.py:34
  8.5 10.3 %copy-start.1 = (bf16[8,100,512]{2,0,1:T(8,128)(2,1)S(1)}, bf16[8,100,512]{2,0,1:T(8,128)(2,1)}, u32[]{:S(2)}) copy-start(bf16[8,100,512]{2,0,1:T(8,128)(2,1)} %param.5) | copy-start | bytes 2457604
  8.5 13.2 %collective-permute-start = (bf16[8,16,100]{2,1,0:T(8,128)(2,1)S(1)}, bf16[8,16,100]{2,1,0:T(8,128)(2,1)S(1)}, u32[]{:S(2)}, u32[]{:S(2)}) collective-permute-start(bf16[8,16,100]{2,1,0:T(8,128)(2,1)S(1)} %bitcast.32), channel_id=1, source_target_pairs={{0,16},{16,0},{4,20},{20,4},{8,24},{24,8},{12,28},{28,12},{1,17},{... | collective-permute-start | bytes 76808 | tf_op jit(solution)/shard_map/ppermute | solution.py:18
  12.6 9.1 %collective-permute-start.1 = (bf16[8,16,100]{2,1,0:T(8,128)(2,1)S(1)}, bf16[8,16,100]{2,1,0:T(8,128)(2,1)S(1)}, u32[]{:S(2)}, u32[]{:S(2)}) collective-permute-start(bf16[8,16,100]{2,1,0:T(8,128)(2,1)S(1)} %bitcast.33), channel_id=1, source_target_pairs={{0,8},{8,0},{4,12},{12,4},{16,24},{24,16},{20,28},{28,20},{1,9},{9... | collective-permute-start | bytes 76808 | tf_op jit(solution)/shard_map/ppermute | solution.py:18
  14.2 7.5 %collective-permute-start.2 = (bf16[8,16,100]{2,1,0:T(8,128)(2,1)S(1)}, bf16[8,16,100]{2,1,0:T(8,128)(2,1)S(1)}, u32[]{:S(2)}, u32[]{:S(2)}) collective-permute-start(bf16[8,16,100]{2,1,0:T(8,128)(2,1)S(1)} %bitcast.34), channel_id=1, source_target_pairs={{0,4},{4,0},{8,12},{12,8},{16,20},{20,16},{24,28},{28,24},{1,5},{5... | collective-permute-start | bytes 76808 | tf_op jit(solution)/shard_map/ppermute | solution.py:18
  18.8 0.7 copy-start.4
  39.5 5.5 %copy-start.3 = (bf16[8,100,496]{2,0,1:T(8,128)(2,1)S(1)}, bf16[8,100,496]{2,0,1:T(8,128)(2,1)}, u32[]{:S(2)}) copy-start(bf16[8,100,496]{2,0,1:T(8,128)(2,1)} %param.6) | copy-start | bytes 2380804
  46.2 1.3 copy-start.2
Sparse Core Ops, SparseCore 0:
  19.0 127.5 all-reduce.1
where the time goes:
time: 156 us
  waiting for transfers between devices  60.7 us (39%)
  blocking collectives  52.5 us (34%)
  between operations  14.2 us (9%)
  matrix products  9.92 us (6%)
  local copies, waits for them, and re-layouts  9.89 us (6%)
  starting transfers between devices  7.26 us (5%)
  other arithmetic  1.57 us (1%)
    psum x1, waiting for transfers between devices, local(): old_sum = lax.psum(old_part, ('site', 'mode'))  60.7 us
    psum x1, blocking collectives, local(): new_sum = lax.psum(new_part, ('site', 'mode'))  38 us
    all_gather x1, blocking collectives, local(): widened = lax.all_gather(stacked, 'mode', axis=2, tiled=True)  14.5 us
    ppermute x3, starting transfers between devices, swapped(): return lax.ppermute(block, axis, route)  7.22 us
    dot_general x1, matrix products, local(): jnp.einsum('bdoi,bdki->bok', hops, gathered, preferred_element_type=jnp.f...  5.31 us
    unnamed x20, local copies, waits for them, and re-layouts  4.45 us
  transfers between devices with their start and end apart: 4, of which 1 were waited for; matrix products, arithmetic and copies ran while one was open for 11% of the time, Pallas kernels for 0%

commit v1 on v0

v1 whole, which is shorter than its diff:
```python
import functools
import math

import jax
import jax.numpy as jnp
from jax import lax
from jax.experimental import pallas as pl
from jax.experimental.pallas import tpu as pltpu
from jax.sharding import PartitionSpec as P

F32 = jnp.float32
BF16 = jnp.bfloat16
BOTH = ("site", "mode")
LANES = 128


def dot_nn(a, b):
    return lax.dot_general(a, b, (((1,), (0,)), ((), ())), preferred_element_type=F32)


def dot_tn(a, b):
    return lax.dot_general(a, b, (((0,), (0,)), ((), ())), preferred_element_type=F32)


def dot_nt(a, b):
    return lax.dot_general(a, b, (((1,), (1,)), ((), ())), preferred_element_type=F32)


def onehot(shape, test):
    rows = lax.broadcasted_iota(jnp.int32, shape, 0)
    cols = lax.broadcasted_iota(jnp.int32, shape, 1)
    return jnp.where(test(rows, cols), 1.0, 0.0).astype(BF16)


def split(x):
    high = x.astype(BF16)
    low = (x - high.astype(F32)).astype(BF16)
    return high, low


def place():
    mode = lax.axis_index("mode")
    site = lax.axis_index("site")
    core = lax.rem(mode, 2)
    half = lax.div(mode, 2)
    y = lax.rem(site, 2)
    z0 = lax.rem(lax.div(site, 2), 2)
    z1 = lax.rem(lax.div(site, 4), 2)
    return core, half, y, z0, z1


def pick(core, first, second):
    return first * (1 - core) + second * core


def rows_at(index, count):
    return pl.ds(pl.multiple_of(index * count, count), count)


def call(kernel, outs, *args, scratch=(), flops=10**8, moved=2 * 10**6):
    vmem = pl.BlockSpec(memory_space=pltpu.VMEM)
    return pl.pallas_call(
        kernel,
        out_shape=outs,
        in_specs=[vmem] * len(args),
        out_specs=jax.tree.map(lambda _: vmem, outs),
        scratch_shapes=scratch,
        compiler_params=pltpu.CompilerParams(vmem_limit_bytes=48 * 2**20),
        cost_estimate=pl.CostEstimate(flops=flops, bytes_accessed=moved, transcendentals=0),
    )(*args)


def shaped(rows, cols, dtype):
    return jax.ShapeDtypeStruct((rows, cols), dtype)


def first_kernel(nb, basis, images, pay):
    rows, nvec = basis.shape
    old = images.shape[1]
    blk = nvec - old
    core = place()[0]
    top = nvec // 2
    keep = basis[:, pl.ds(pl.multiple_of((1 - core) * top, top), top)]
    part = dot_tn(keep, images[...])
    high, low = split(part)
    pay[:top, :old] = high
    pay[:top, old:] = jnp.zeros((top, blk), BF16)
    pay[top : 2 * top, :old] = low
    pay[top : 2 * top, old:] = jnp.zeros((top, blk), BF16)
    wide = nb * blk
    last = basis[:, nvec - LANES :]
    spread = onehot((LANES, wide), lambda r, c: r - (LANES - blk) == lax.rem(c, blk))
    tiled = dot_nn(last, spread)
    row = lax.broadcasted_iota(jnp.int32, (rows, wide), 0)
    col = lax.broadcasted_iota(jnp.int32, (rows, wide), 1)
    tiled = jnp.where(lax.rem(row, nb) == lax.div(col, blk), tiled, 0.0).astype(BF16)
    gather = onehot((rows, LANES), lambda r, c: lax.div(r, nb) == c)
    flipped = dot_tn(tiled, gather).astype(BF16)
    groups = nvec // LANES
    each = wide // groups
    for g in range(groups):
        pay[2 * top :, g * LANES : (g + 1) * LANES] = flipped[g * each : (g + 1) * each]


def keep_kernel(basis, images, kept):
    nvec = basis.shape[1]
    old = images.shape[1]
    core = place()[0]
    top = nvec // 2
    mine = basis[:, pl.ds(pl.multiple_of(core * top, top), top)]
    kept[:, :old] = dot_tn(mine, images[...])
    kept[:, old:] = jnp.zeros((top, nvec - old), F32)


def rotate_kernel(basis, rotation, out):
    out[...] = dot_nn(basis[...], rotation[...]).astype(BF16)


def joined(kept, got, start, count):
    whole = kept.shape[0]
    rows = pl.ds(pl.multiple_of(start, count), count)
    lows = pl.ds(pl.multiple_of(start + whole, count), count)
    return kept[rows, :] + (got[rows, :].astype(F32) + got[lows, :].astype(F32))


def second_kernel(kept, got, pay, out, rest):
    core, half, y, z0, z1 = place()
    whole = kept.shape[0]
    n = whole // 2
    bit = pick(core, half, y)
    out[:n, :], out[n : 2 * n, :] = split(joined(kept, got, (1 - bit) * n, n))
    rest[...] = joined(kept, got, bit * n, n)
    each = got.shape[0] - 2 * whole
    out[pl.ds(pl.multiple_of(2 * n + core * each, each), each), :] = pay[2 * whole :, :]
    out[pl.ds(pl.multiple_of(2 * n + (1 - core) * each, each), each), :] = got[2 * whole :, :]


def third_kernel(kept, got, pay, out, rest):
    core, half, y, z0, z1 = place()
    whole = kept.shape[0]
    n = whole // 2
    bit = pick(core, y, half)
    out[:n, :], out[n : 2 * n, :] = split(joined(kept, got, (1 - bit) * n, n))
    rest[...] = joined(kept, got, bit * n, n)
    each = got.shape[0] - 2 * whole
    at = pick(core, half, 0)
    out[pl.ds(pl.multiple_of(2 * n + at * each, each), each), :] = pay[2 * whole :, :]
    out[pl.ds(pl.multiple_of(2 * n + (1 - at) * each, each), each), :] = got[2 * whole :, :]


def fourth_kernel(kept, got, pay, out, rest, side, hold):
    core, half, y, z0, z1 = place()
    whole = kept.shape[0]
    n = whole // 2
    bit = pick(core, z0, z1)
    out[:n, :], out[n : 2 * n, :] = split(joined(kept, got, (1 - bit) * n, n))
    rest[...] = joined(kept, got, bit * n, n)
    area = got.shape[0] - 2 * whole
    each = area // 2
    hold[:area, :] = pay[2 * whole :, :]
    hold[area:, :] = got[2 * whole :, :]
    for j in range(2):
        other = j * (1 - half) + (1 - j) * half
        own = pick(core, j, 2 * other)
        near = pick(core, 2 + j, 1 + 2 * other)
        out[2 * n + j * each : 2 * n + (j + 1) * each, :] = hold[rows_at(own, each), :]
        side[j * each : (j + 1) * each, :] = hold[rows_at(near, each), :]


def fifth_kernel(kept, got, out):
    n = kept.shape[0]
    total = kept[...] + (got[:n, :].astype(F32) + got[n : 2 * n, :].astype(F32))
    out[:n, :], out[n:, :] = split(total)


def assemble(area, spots, coarse):
    rows, nvec = area.shape
    groups = nvec // LANES
    modes = spots
    each = rows // modes
    share = coarse // modes
    lines = []
    for g in range(groups):
        lines.append(
            jnp.concatenate(
                [area[m * each : (m + 1) * each, g * LANES : (g + 1) * LANES] for m in range(modes)],
                axis=1,
            )
        )
    flat = jnp.concatenate(lines, axis=0)
    shift = onehot(
        (modes * LANES, coarse),
        lambda r, c: (lax.rem(r, LANES) < share) & (lax.div(r, LANES) * share + lax.rem(r, LANES) == c),
    )
    return dot_nn(flat, shift).astype(BF16)


def weights(table, step_hop, store, mixed, nb, blk):
    for b in range(nb):
        entry = table[b, step_hop]
        mixed[b * blk : (b + 1) * blk, :] = store[pl.ds(pl.multiple_of(entry * blk, blk), blk), :]


def stencil_near(order, table, nb, blk, spots, own_ref, side_ref, hops, total, own_out, store, mixed):
    step = pl.program_id(0)
    coarse = store.shape[1]
    wide = nb * blk

    @pl.when(step == 0)
    def _():
        own = assemble(own_ref[...], spots, coarse)
        own_out[...] = own
        near = assemble(side_ref[...], spots, coarse)
        for k in (0, 1, 2, 4, 5):
            store[k * wide : (k + 1) * wide, :] = own
        store[3 * wide : 4 * wide, :] = near

    weights(table, order[step], store, mixed, nb, blk)
    part = dot_nt(hops[...], mixed[...])

    @pl.when(step == 0)
    def _():
        total[...] = part

    @pl.when(step > 0)
    def _():
        total[...] += part


def run_near(order, table, own, side, hops, nb, blk, spots):
    count, rows, coarse = hops.shape
    wide = nb * blk
    steps = len(order)

    def kernel(order_ref, table_ref, own_ref, side_ref, hops_ref, total, own_out, store, mixed):
        stencil_near(
            order_ref, table_ref, nb, blk, spots, own_ref, side_ref, hops_ref, total, own_out, store, mixed
        )

    spec = pltpu.PrefetchScalarGridSpec(
        num_scalar_prefetch=2,
        grid=(steps,),
        in_specs=[
            pl.BlockSpec(own.shape, lambda i, o, t: (0, 0)),
            pl.BlockSpec(side.shape, lambda i, o, t: (0, 0)),
            pl.BlockSpec((None, rows, coarse), lambda i, o, t: (o[i], 0, 0)),
        ],
        out_specs=[
            pl.BlockSpec((rows, wide), lambda i, o, t: (0, 0)),
            pl.BlockSpec((wide, coarse), lambda i, o, t: (0, 0)),
        ],
        scratch_shapes=[pltpu.VMEM((6 * wide, coarse), BF16), pltpu.VMEM((wide, coarse), BF16)],
    )
    return pl.pallas_call(
        kernel,
        grid_spec=spec,
        out_shape=[shaped(rows, wide, F32), shaped(wide, coarse, BF16)],
        compiler_params=pltpu.CompilerParams(vmem_limit_bytes=32 * 2**20),
        cost_estimate=pl.CostEstimate(
            flops=2 * steps * rows * coarse * wide, bytes_accessed=2 * steps * rows * coarse, transcendentals=0
        ),
    )(jnp.array(order, jnp.int32), table, own, side, hops)


def run_far(order, table, own, mine, other, times, total, basis, old, hops, nb, blk, spots):
    count, rows, coarse = hops.shape
    wide = nb * blk
    steps = len(order)
    nvec = basis.shape[1]
    nold = old.shape[0]
    n_times = len(times)

    def kernel(order_ref, table_ref, own_ref, mine_ref, other_ref, *refs):
        time_refs = refs[:n_times]
        total_ref, basis_ref, old_ref, hops_ref, masked, pay, store, mixed, acc = refs[n_times:]
        step = pl.program_id(0)
        core = place()[0]

        @pl.when(step == 0)
        def _():
            own = own_ref[...]
            for k in (0, 3, 4, 5):
                store[k * wide : (k + 1) * wide, :] = own
            first = assemble(mine_ref[...], spots, coarse)
            second = assemble(other_ref[...], spots, coarse)
            store[rows_at(2 - core, wide), :] = first
            store[rows_at(1 + core, wide), :] = second
            for k, ref in enumerate(time_refs):
                store[(4 + k) * wide : (5 + k) * wide, :] = assemble(ref[...], spots, coarse)

        weights(table_ref, order_ref[step], store, mixed, nb, blk)
        part = dot_nt(hops_ref[...], mixed[...])

        @pl.when(step == 0)
        def _():
            acc[...] = total_ref[...] + part

        @pl.when(step > 0)
        def _():
            acc[...] += part

        @pl.when(step == steps - 1)
        def _():
            row = lax.broadcasted_iota(jnp.int32, (rows, wide), 0)
            col = lax.broadcasted_iota(jnp.int32, (rows, wide), 1)
            chosen = jnp.where(lax.rem(row, nb) == lax.div(col, blk), acc[...], 0.0).astype(BF16)
            masked[...] = chosen
            fold = onehot((blk, wide), lambda r, c: lax.rem(c, blk) == r)
            flat = dot_nt(fold, chosen).astype(BF16)
            new = dot_nn(flat, basis_ref[...])
            pay[:nold, :] = old_ref[...]
            pay[nold : nold + blk, :], pay[nold + blk :, :] = split(new)

    spec = pltpu.PrefetchScalarGridSpec(
        num_scalar_prefetch=2,
        grid=(steps,),
        in_specs=[pl.BlockSpec(a.shape, lambda i, o, t: (0, 0)) for a in (own, mine, other, *times, total, basis, old)]
        + [pl.BlockSpec((None, rows, coarse), lambda i, o, t: (o[i], 0, 0))],
        out_specs=[
            pl.BlockSpec((rows, wide), lambda i, o, t: (0, 0)),
            pl.BlockSpec((nold + 2 * blk, nvec), lambda i, o, t: (0, 0)),
        ],
        scratch_shapes=[
            pltpu.VMEM((6 * wide, coarse), BF16),
            pltpu.VMEM((wide, coarse), BF16),
            pltpu.VMEM((rows, wide), F32),
        ],
    )
    return pl.pallas_call(
        kernel,
        grid_spec=spec,
        out_shape=[shaped(rows, wide, BF16), shaped(nold + 2 * blk, nvec, BF16)],
        compiler_params=pltpu.CompilerParams(vmem_limit_bytes=32 * 2**20),
        cost_estimate=pl.CostEstimate(
            flops=2 * steps * rows * coarse * wide, bytes_accessed=2 * steps * rows * coarse, transcendentals=0
        ),
    )(jnp.array(order, jnp.int32), table, own, mine, other, *times, total, basis, old, hops)


def turn_kernel(nb, images, masked, rotation, out):
    old = images.shape[1]
    tail = rotation[old:, :]
    deep = jnp.concatenate([tail] * nb, axis=0)
    out[...] = (dot_nn(images[...], rotation[:old, :]) + dot_nn(masked[...], deep)).astype(BF16)


def value(ref, start, count):
    return ref[start : start + count, :].astype(F32) + ref[start + count : start + 2 * count, :].astype(F32)


def extra_kernel(n, blk, pay, got, out):
    out[:n, :], out[n : 2 * n, :] = split(value(pay, 0, n) + value(got, 0, n))
    out[2 * n : 2 * n + blk, :], out[2 * n + blk :, :] = split(value(pay, 2 * n, blk) + value(got, 2 * n, blk))


def settle_kernel(n, blk, scale, pay, got, out):
    out[:n, :] = ((value(pay, 0, n) + value(got, 0, n)) * scale).astype(BF16)
    out[n : n + blk, :], out[n + blk :, :] = split(value(pay, 2 * n, blk) + value(got, 2 * n, blk))


def grow_kernel(n, blk, chooser, pay, got, out):
    bit = chooser(*place())
    out[rows_at(bit, n), :] = pay[:n, :]
    out[rows_at(1 - bit, n), :] = got[:n, :]
    out[2 * n : 2 * n + blk, :], out[2 * n + blk :, :] = split(value(pay, n, blk) + value(got, n, blk))


def final_kernel(n, blk, scale, pay, got, out):
    nvec = out.shape[1]
    core = place()[0]
    out[rows_at(core, n), :] = pay[:n, :].astype(F32)
    out[rows_at(1 - core, n), :] = got[:n, :].astype(F32)
    new = (value(pay, n, blk) + value(got, n, blk)) * scale
    tall = jnp.concatenate([jnp.zeros((LANES - blk, nvec), F32), new], axis=0)
    flipped = tall.T
    lane = lax.broadcasted_iota(jnp.int32, (nvec, LANES), 1)
    out[:, nvec - LANES :] = jnp.where(lane < LANES - blk, out[:, nvec - LANES :], flipped)


def local(basis, images, hops, neighbours, rotation):
    nb, modes_here, nvec = basis.shape
    old = images.shape[2]
    blk = nvec - old
    sites = lax.axis_size("site")
    spots = lax.axis_size("mode")
    count = sites * spots
    rows = nb * modes_here
    coarse = hops.shape[3]
    wide = nb * blk
    chunk = wide * LANES // nvec
    scale = 1.0 / math.sqrt(count * rows)

    def send(x, first, second):
        pairs = [(d, d ^ (second if d % 2 else first)) for d in range(count)]
        return lax.ppermute(x, BOTH, pairs)

    core_hop, x_hop, y_hop, z0_hop, z1_hop = 1, 2, spots, 2 * spots, 4 * spots

    flat_basis = jnp.transpose(basis, (1, 0, 2)).reshape(rows, nvec)
    flat_images = jnp.transpose(images, (1, 0, 2)).reshape(rows, old)
    flat_hops = jnp.transpose(hops, (1, 2, 0, 3)).reshape(hops.shape[1], rows, coarse)
    own_rows = jnp.arange(nb, dtype=jnp.int32)
    table = jnp.concatenate([own_rows[:, None], neighbours], axis=1)

    half = nvec // 2
    pay0 = call(functools.partial(first_kernel, nb), shaped(nvec + chunk, nvec, BF16), flat_basis, flat_images)
    got0 = send(pay0, core_hop, core_hop)
    kept0 = call(keep_kernel, shaped(half, nvec, F32), flat_basis, flat_images)
    pay1, kept1 = call(
        second_kernel,
        (shaped(half + 2 * chunk, nvec, BF16), shaped(half // 2, nvec, F32)),
        kept0,
        got0,
        pay0,
    )
    got1 = send(pay1, x_hop, y_hop)
    turned_basis = call(rotate_kernel, shaped(rows, nvec, BF16), flat_basis, rotation)
    pay2, kept2 = call(
        third_kernel,
        (shaped(half // 2 + 4 * chunk, nvec, BF16), shaped(half // 4, nvec, F32)),
        kept1,
        got1,
        pay1,
    )
    got2 = send(pay2, y_hop, x_hop)
    pay3, kept3, side = call(
        fourth_kernel,
        (shaped(half // 4 + 4 * chunk, nvec, BF16), shaped(half // 8, nvec, F32), shaped(4 * chunk, nvec, BF16)),
        kept2,
        got2,
        pay2,
        scratch=[pltpu.VMEM((8 * chunk, nvec), BF16)],
    )
    n = half // 8
    got3 = send(pay3, z0_hop, z1_hop)
    own = pay3[2 * n :, :]
    times = []
    near_order = [0, 3, 6]
    far_order = [1, 4, 2, 5]
    if sites > 8:
        step = 8 * spots
        times = [
            lax.ppermute(own, BOTH, [((d + sign * step) % count, d) for d in range(count)]) for sign in (1, -1)
        ]
        far_order = far_order + [7, 8]
    else:
        near_order = near_order + [7, 8]
    total, own_flat = run_near(near_order, table, own, side, flat_hops, nb, blk, spots)
    mine = got3[2 * n :, :]
    other = send(mine, core_hop, core_hop)
    old_pay = call(fifth_kernel, shaped(2 * n, nvec, BF16), kept3, got3)
    masked, payc = run_far(
        far_order, table, own_flat, mine, other, times, total, flat_basis, old_pay, flat_hops, nb, blk, spots
    )
    gotc = send(payc, z1_hop, z0_hop)
    turned_images = call(functools.partial(turn_kernel, nb), shaped(rows, nvec, BF16), flat_images, masked, rotation)
    hop = 8 * spots
    while hop < count:
        payc = call(functools.partial(extra_kernel, n, blk), shaped(2 * n + 2 * blk, nvec, BF16), payc, gotc)
        gotc = send(payc, hop, hop)
        hop *= 2
    payc = call(functools.partial(settle_kernel, n, blk, scale), shaped(n + 2 * blk, nvec, BF16), payc, gotc)
    gotc = send(payc, z0_hop, z1_hop)
    payc = call(
        functools.partial(grow_kernel, n, blk, lambda core, half, y, z0, z1: pick(core, z0, z1)),
        shaped(2 * n + 2 * blk, nvec, BF16),
        payc,
        gotc,
    )
    gotc = send(payc, y_hop, x_hop)
    payc = call(
        functools.partial(grow_kernel, 2 * n, blk, lambda core, half, y, z0, z1: pick(core, y, half)),
        shaped(4 * n + 2 * blk, nvec, BF16),
        payc,
        gotc,
    )
    gotc = send(payc, x_hop, y_hop)
    payc = call(
        functools.partial(grow_kernel, 4 * n, blk, lambda core, half, y, z0, z1: pick(core, half, y)),
        shaped(8 * n + 2 * blk, nvec, BF16),
        payc,
        gotc,
    )
    gotc = send(payc, core_hop, core_hop)
    projected = call(functools.partial(final_kernel, 8 * n, blk, scale), shaped(nvec, nvec, F32), payc, gotc)

    def back(x):
        return jnp.transpose(x.reshape(modes_here, nb, nvec), (1, 0, 2))

    return projected, back(turned_basis), back(turned_images)


def solution(mesh):
    placed = (
        P("site", "mode", None),
        P("site", "mode", None),
        P("site", None, "mode", None),
        P("site", None),
        P(),
    )
    return jax.shard_map(
        local,
        mesh=mesh,
        in_specs=placed,
        out_specs=(P(), P("site", "mode", None), P("site", "mode", None)),
        check_vma=False,
    )
```

time: 156 us -> 60.8 us (0.39)
  blocking collectives: 52.5 us -> 0 us
  waiting for transfers between devices: 60.7 us -> 26.4 us
  between operations: 14.2 us -> 0.83 us
  Pallas kernels: 0 us -> 12.1 us
  starting transfers between devices: 7.26 us -> 18.5 us
  matrix products: 9.92 us -> 0 us
  local copies, waits for them, and re-layouts: 9.89 us -> 2.72 us
    psum x1 -> x0, waiting for transfers between devices: 60.7 us -> none  [local(): old_sum = lax.psum(old_part, ('site', 'mode'))]
    psum x1 -> x0, blocking collectives: 38 us -> none  [local(): new_sum = lax.psum(new_part, ('site', 'mode'))]
    ppermute x3 -> x10, waiting for transfers between devices: 0.01 us -> 26.4 us  [send(): return lax.ppermute(x, BOTH, pairs)]
    all_gather x1 -> x0, blocking collectives: 14.5 us -> none  [local(): widened = lax.all_gather(stacked, 'mode', axis=2, tiled=True)]
    pallas_call x0 -> x15, Pallas kernels: none -> 12.1 us  [the longest x13 5.89 us: call(): pl.pallas_call(kernel, out_shape=outs, in_specs=[vmem] * len(args), out_s...]
    ppermute x3 -> x10, starting transfers between devices: 7.22 us -> 18.5 us  [send(): return lax.ppermute(x, BOTH, pairs)]
    dot_general x5 -> x0, matrix products: 9.92 us -> none  [the longest x1 5.31 us: local(): jnp.einsum('bdoi,bdki->bok', hops, gathered, preferred_element_type=jnp.f...]
    all_gather x1 -> x0, local copies, waits for them, and re-layouts: 2.12 us -> none  [local(): widened = lax.all_gather(stacked, 'mode', axis=2, tiled=True)]
  transfers between devices with their start and end apart: 4 -> 10, of which waited for: 1 -> 8; matrix products, arithmetic and copies ran while one was open for 11% -> 0% of each run, Pallas kernels for 0% -> 11%
where the time goes in v1:
time: 60.8 us; the launch traced here: 60.7 us
  waiting for transfers between devices  26.4 us (43%)
  starting transfers between devices  18.5 us (30%)
  Pallas kernels  12.1 us (20%)
  local copies, waits for them, and re-layouts  2.72 us (4%)
  between operations  0.83 us (1%)
    ppermute x10, waiting for transfers between devices, send(): return lax.ppermute(x, BOTH, pairs)  26.4 us
    ppermute x10, starting transfers between devices, send(): return lax.ppermute(x, BOTH, pairs)  18.5 us
    pallas_call x13, Pallas kernels, call(): pl.pallas_call(kernel, out_shape=outs, in_specs=[vmem] * len(args), out_s...  5.89 us
    pallas_call x1, Pallas kernels, run_near(): pl.pallas_call(kernel, grid_spec=spec, out_shape=[shaped(rows, wide, F32)...  3.13 us
    pallas_call x1, Pallas kernels, run_far(): pl.pallas_call(kernel, grid_spec=spec, out_shape=[shaped(rows, wide, BF16...  3.11 us
    unnamed x18, local copies, waits for them, and re-layouts  2.7 us
  transfers between devices with their start and end apart: 10, of which 8 were waited for; matrix products, arithmetic and copies ran while one was open for 0% of the time, Pallas kernels for 11%

profile of v1, /device:TPU:0, one launch (start us, length us, event | category | flops | bytes accessed | tf_op | source)
XLA Modules:
  0.0 60.7 jit_solution(7234979286587727561)
XLA Ops:
  0.6 0.0 copy-start.7
  0.7 1.3 %copy-done.1 = bf16[8,100,512]{2,0,1:T(8,128)(2,1)S(1)} copy-done((bf16[8,100,512]{2,0,1:T(8,128)(2,1)S(1)}, bf16[8,100,512]{2,0,1:T(8,128)(2,1)}, u32[]{:S(2)}) %copy-start.1) | copy-done | bytes 819224
  2.0 1.4 %copy-done.3 = bf16[8,100,496]{2,0,1:T(8,128)(2,1)S(1)} copy-done((bf16[8,100,496]{2,0,1:T(8,128)(2,1)S(1)}, bf16[8,100,496]{2,0,1:T(8,128)(2,1)}, u32[]{:S(2)}) %copy-start.3) | copy-done | bytes 793624
  3.3 0.8 %shard_map.95.pay = bf16[544,512]{1,0:T(8,128)(2,1)S(1)} custom-call(bf16[800,512]{1,0:T(8,128)(2,1)S(1)} %bitcast.17, bf16[800,496]{1,0:T(8,128)(2,1)S(1)} %bitcast.21), custom_call_target="tpu_custom_call" | custom-call | flops 100000000 | bytes 2000000 | tf_op jit(solution)/shard_map/pallas_call | solution.py:62
  4.1 0.6 collective-permute-start
  4.7 0.5 shard_map.94.kept
  5.2 1.1 %collective-permute-done.got = bf16[544,512]{1,0:T(8,128)(2,1)S(1)} collective-permute-done((bf16[544,512]{1,0:T(8,128)(2,1)S(1)}, bf16[544,512]{1,0:T(8,128)(2,1)S(1)}, u32[]{:S(2)}, u32[]{:S(2)}) %collective-permute-start) | collective-permute-done | bytes 557088 | tf_op jit(solution)/shard_map/ppermute | solution.py:395
  6.3 0.1 shard_map.96
  6.4 2.9 %collective-permute-start.1 = (bf16[320,512]{1,0:T(8,128)(2,1)S(1)}, bf16[320,512]{1,0:T(8,128)(2,1)S(1)}, u32[]{:S(2)}, u32[]{:S(2)}) collective-permute-start(bf16[320,512]{1,0:T(8,128)(2,1)S(1)} %get-tuple-element.15.pay), channel_id=1, source_target_pairs={{0,2},{1,5},{2,0},{3,7},{4,6},{5,1},{6,4},{7,3},{8,10},{9,13},{10,... | collective-permute-start | bytes 983048 | tf_op jit(solution)/shard_map/ppermute | solution.py:395
  9.3 5.1 %collective-permute-done.1.got = bf16[320,512]{1,0:T(8,128)(2,1)S(1)} collective-permute-done((bf16[320,512]{1,0:T(8,128)(2,1)S(1)}, bf16[320,512]{1,0:T(8,128)(2,1)S(1)}, u32[]{:S(2)}, u32[]{:S(2)}) %collective-permute-start.1) | collective-permute-done | bytes 327712 | tf_op jit(solution)/shard_map/ppermute | solution.py:395
  14.4 0.1 shard_map.97
  14.4 2.1 %collective-permute-start.2 = (bf16[256,512]{1,0:T(8,128)(2,1)S(1)}, bf16[256,512]{1,0:T(8,128)(2,1)S(1)}, u32[]{:S(2)}, u32[]{:S(2)}) collective-permute-start(bf16[256,512]{1,0:T(8,128)(2,1)S(1)} %get-tuple-element.17.pay), channel_id=1, source_target_pairs={{0,4},{1,3},{2,6},{3,1},{4,0},{5,7},{6,2},{7,5},{8,12},{9,11},{10,... | collective-permute-start | bytes 786440 | tf_op jit(solution)/shard_map/ppermute | solution.py:395
  16.5 4.4 %collective-permute-done.2.got = bf16[256,512]{1,0:T(8,128)(2,1)S(1)} collective-permute-done((bf16[256,512]{1,0:T(8,128)(2,1)S(1)}, bf16[256,512]{1,0:T(8,128)(2,1)S(1)}, u32[]{:S(2)}, u32[]{:S(2)}) %collective-permute-start.2) | collective-permute-done | bytes 262176 | tf_op jit(solution)/shard_map/ppermute | solution.py:395
  20.9 0.1 shard_map.98
  20.9 2.1 %collective-permute-start.3 = (bf16[192,512]{1,0:T(8,128)(2,1)S(1)}, bf16[192,512]{1,0:T(8,128)(2,1)S(1)}, u32[]{:S(2)}, u32[]{:S(2)}) collective-permute-start(bf16[192,512]{1,0:T(8,128)(2,1)S(1)} %get-tuple-element.18), channel_id=1, source_target_pairs={{0,8},{1,17},{2,10},{3,19},{4,12},{5,21},{6,14},{7,23},{8,0},{9,25... | collective-permute-start | bytes 589832 | tf_op jit(solution)/shard_map/ppermute | solution.py:395
  23.1 3.8 %collective-permute-done.3.got = bf16[192,512]{1,0:T(8,128)(2,1)S(1)} collective-permute-done((bf16[192,512]{1,0:T(8,128)(2,1)S(1)}, bf16[192,512]{1,0:T(8,128)(2,1)S(1)}, u32[]{:S(2)}, u32[]{:S(2)}) %collective-permute-start.3) | collective-permute-done | bytes 196640 | tf_op jit(solution)/shard_map/ppermute | solution.py:395
  26.9 0.7 %collective-permute-start.4 = (bf16[128,512]{1,0:T(8,128)(2,1)S(1)}, bf16[128,512]{1,0:T(8,128)(2,1)S(1)}, u32[]{:S(2)}, u32[]{:S(2)}) collective-permute-start(bf16[128,512]{1,0:T(8,128)(2,1)S(1)} %slice.8.mine_ref), channel_id=1, source_target_pairs={{0,1},{1,0},{2,3},{3,2},{4,5},{5,4},{6,7},{7,6},{8,9},{9,8},{10,11... | collective-permute-start | bytes 393224 | tf_op jit(solution)/shard_map/ppermute | solution.py:395
  27.6 0.1 pad_add_fusion.table_ref
  27.7 3.1 %shard_map.99 = (f32[800,128]{1,0:T(8,128)S(1)}, bf16[128,400]{1,0:T(8,128)(2,1)S(1)}) custom-call(s32[5]{0:T(128)S(1)} %copy-done.7, s32[8,9]{1,0:T(8,128)S(1)} %pad_add_fusion.table_ref, bf16[128,512]{1,0:T(8,128)(2,1)S(1)} %slice.6.own_ref, bf16[128,512]{1,0:T(8,128)(2,1)S(1)} %get-tuple-element.19.side_ref, bf16[9,800,400]{2,1,0:T(8,128)(2,1)S(1)} %bitcast.15), custom_call_target="tpu_custom_call" | custom-call | flops 409600000 | bytes 3200000 | tf_op jit(solution)/shard_map/pallas_call | solution.py:254
  30.9 3.1 %shard_map.101 = (bf16[800,128]{1,0:T(8,128)(2,1)S(1)}, bf16[96,512]{1,0:T(8,128)(2,1)S(1)}) custom-call(s32[4]{0:T(128)S(1)} %copy-done.6, s32[8,9]{1,0:T(8,128)S(1)} %pad_add_fusion.table_ref, bf16[128,400]{1,0:T(8,128)(2,1)S(1)} %get-tuple-element.20.own_ref, bf16[128,512]{1,0:T(8,128)(2,1)S(1)} %slice.8.mine_ref, ...), custom_call_target="tpu_custom_call" | custom-call | flops 327680000 | bytes 2560000 | tf_op jit(solution)/shard_map/pallas_call | solution.py:329
  34.0 3.4 %collective-permute-start.5 = (bf16[96,512]{1,0:T(8,128)(2,1)S(1)}, bf16[96,512]{1,0:T(8,128)(2,1)S(1)}, u32[]{:S(2)}, u32[]{:S(2)}) collective-permute-start(bf16[96,512]{1,0:T(8,128)(2,1)S(1)} %get-tuple-element.23.pay), channel_id=1, source_target_pairs={{0,16},{1,9},{2,18},{3,11},{4,20},{5,13},{6,22},{7,15},{8,24},{9,1... | collective-permute-start | bytes 294920 | tf_op jit(solution)/shard_map/ppermute | solution.py:395
  37.5 2.6 %collective-permute-done.5.got = bf16[96,512]{1,0:T(8,128)(2,1)S(1)} collective-permute-done((bf16[96,512]{1,0:T(8,128)(2,1)S(1)}, bf16[96,512]{1,0:T(8,128)(2,1)S(1)}, u32[]{:S(2)}, u32[]{:S(2)}) %collective-permute-start.5) | collective-permute-done | bytes 98336 | tf_op jit(solution)/shard_map/ppermute | solution.py:395
  40.1 3.4 %collective-permute-start.6 = (bf16[64,512]{1,0:T(8,128)(2,1)S(1)}, bf16[64,512]{1,0:T(8,128)(2,1)S(1)}, u32[]{:S(2)}, u32[]{:S(2)}) collective-permute-start(bf16[64,512]{1,0:T(8,128)(2,1)S(1)} %shard_map.102.pay), channel_id=1, source_target_pairs={{0,8},{1,17},{2,10},{3,19},{4,12},{5,21},{6,14},{7,23},{8,0},{9,25... | collective-permute-start | bytes 196616 | tf_op jit(solution)/shard_map/ppermute | solution.py:395
  43.5 2.6 %collective-permute-done.6.got = bf16[64,512]{1,0:T(8,128)(2,1)S(1)} collective-permute-done((bf16[64,512]{1,0:T(8,128)(2,1)S(1)}, bf16[64,512]{1,0:T(8,128)(2,1)S(1)}, u32[]{:S(2)}, u32[]{:S(2)}) %collective-permute-start.6) | collective-permute-done | bytes 65568 | tf_op jit(solution)/shard_map/ppermute | solution.py:395
  46.1 1.6 %collective-permute-start.7 = (bf16[96,512]{1,0:T(8,128)(2,1)S(1)}, bf16[96,512]{1,0:T(8,128)(2,1)S(1)}, u32[]{:S(2)}, u32[]{:S(2)}) collective-permute-start(bf16[96,512]{1,0:T(8,128)(2,1)S(1)} %shard_map.103.pay), channel_id=1, source_target_pairs={{0,4},{1,3},{2,6},{3,1},{4,0},{5,7},{6,2},{7,5},{8,12},{9,11},{10,... | collective-permute-start | bytes 294920 | tf_op jit(solution)/shard_map/ppermute | solution.py:395
  47.7 3.1 %collective-permute-done.7.got = bf16[96,512]{1,0:T(8,128)(2,1)S(1)} collective-permute-done((bf16[96,512]{1,0:T(8,128)(2,1)S(1)}, bf16[96,512]{1,0:T(8,128)(2,1)S(1)}, u32[]{:S(2)}, u32[]{:S(2)}) %collective-permute-start.7) | collective-permute-done | bytes 98336 | tf_op jit(solution)/shard_map/ppermute | solution.py:395
  50.9 1.6 %collective-permute-start.8 = (bf16[160,512]{1,0:T(8,128)(2,1)S(1)}, bf16[160,512]{1,0:T(8,128)(2,1)S(1)}, u32[]{:S(2)}, u32[]{:S(2)}) collective-permute-start(bf16[160,512]{1,0:T(8,128)(2,1)S(1)} %shard_map.104.pay), channel_id=1, source_target_pairs={{0,2},{1,5},{2,0},{3,7},{4,6},{5,1},{6,4},{7,3},{8,10},{9,13},{10,... | collective-permute-start | bytes 491528 | tf_op jit(solution)/shard_map/ppermute | solution.py:395
  52.4 3.8 %collective-permute-done.8.got = bf16[160,512]{1,0:T(8,128)(2,1)S(1)} collective-permute-done((bf16[160,512]{1,0:T(8,128)(2,1)S(1)}, bf16[160,512]{1,0:T(8,128)(2,1)S(1)}, u32[]{:S(2)}, u32[]{:S(2)}) %collective-permute-start.8) | collective-permute-done | bytes 163872 | tf_op jit(solution)/shard_map/ppermute | solution.py:395
  56.3 0.1 collective-permute-start.9
  56.4 1.5 %shard_map.107 = bf16[800,512]{1,0:T(8,128)(2,1)} custom-call(bf16[800,512]{1,0:T(8,128)(2,1)S(1)} %bitcast.20, bf16[512,512]{1,0:T(8,128)(2,1)S(1)} %copy-done.5), custom_call_target="tpu_custom_call" | custom-call | flops 100000000 | bytes 2000000 | tf_op jit(solution)/shard_map/pallas_call | solution.py:62
  57.9 1.7 %shard_map.108 = bf16[800,512]{1,0:T(8,128)(2,1)} custom-call(bf16[800,496]{1,0:T(8,128)(2,1)S(1)} %bitcast.23, bf16[800,128]{1,0:T(8,128)(2,1)S(1)} %get-tuple-element.24.masked, bf16[512,512]{1,0:T(8,128)(2,1)S(1)} %copy-done.5), custom_call_target="tpu_custom_call" | custom-call | flops 100000000 | bytes 2000000 | tf_op jit(solution)/shard_map/pallas_call | solution.py:62
  59.5 1.1 %shard_map.106 = f32[512,512]{1,0:T(8,128)} custom-call(bf16[288,512]{1,0:T(8,128)(2,1)S(1)} %shard_map.105.pay, bf16[288,512]{1,0:T(8,128)(2,1)S(1)} %collective-permute-done.9.got), custom_call_target="tpu_custom_call" | custom-call | flops 100000000 | bytes 2000000 | tf_op jit(solution)/shard_map/pallas_call | solution.py:62
  (25 shorter events, 0.2 us)
Async XLA Ops:
  0.6 27.0 %copy-start.7 = (s32[5]{0:T(128)S(1)}, s32[5]{0:T(128)}, u32[]{:S(2)}) copy-start(s32[5]{0:T(128)} %constant.4.clone.order_ref) | copy-start | bytes 64
  0.6 27.0 %copy-start = (bf16[8,9,100,400]{3,0,2,1:T(8,128)(2,1)S(1)}, bf16[8,9,100,400]{3,0,2,1:T(8,128)(2,1)}, u32[]{:S(2)}) copy-start(bf16[8,9,100,400]{3,0,2,1:T(8,128)(2,1)} %param.9) | copy-start | bytes 17280004
  0.7 1.3 %copy-start.1 = (bf16[8,100,512]{2,0,1:T(8,128)(2,1)S(1)}, bf16[8,100,512]{2,0,1:T(8,128)(2,1)}, u32[]{:S(2)}) copy-start(bf16[8,100,512]{2,0,1:T(8,128)(2,1)} %param.7) | copy-start | bytes 2457604
  2.0 1.4 %copy-start.3 = (bf16[8,100,496]{2,0,1:T(8,128)(2,1)S(1)}, bf16[8,100,496]{2,0,1:T(8,128)(2,1)}, u32[]{:S(2)}) copy-start(bf16[8,100,496]{2,0,1:T(8,128)(2,1)} %param.8) | copy-start | bytes 2380804
  3.3 24.3 %copy-start.8 = (s32[8,8]{1,0:T(8,128)S(1)}, s32[8,8]{1,0:T(8,128)}, u32[]{:S(2)}) copy-start(s32[8,8]{1,0:T(8,128)} %param.10) | copy-start | bytes 772
  4.1 26.8 %copy-start.2 = (bf16[8,100,512]{2,0,1:T(8,128)(2,1)S(1)}, bf16[8,100,512]{2,0,1:T(8,128)(2,1)}, u32[]{:S(2)}) copy-start(bf16[8,100,512]{2,0,1:T(8,128)(2,1)} %param.7) | copy-start | bytes 2457604
  4.1 26.8 %copy-start.6 = (s32[4]{0:T(128)S(1)}, s32[4]{0:T(128)}, u32[]{:S(2)}) copy-start(s32[4]{0:T(128)} %constant.5.clone.order_ref) | copy-start | bytes 52
  4.1 2.1 %collective-permute-start = (bf16[544,512]{1,0:T(8,128)(2,1)S(1)}, bf16[544,512]{1,0:T(8,128)(2,1)S(1)}, u32[]{:S(2)}, u32[]{:S(2)}) collective-permute-start(bf16[544,512]{1,0:T(8,128)(2,1)S(1)} %shard_map.95.pay), channel_id=1, source_target_pairs={{0,1},{1,0},{2,3},{3,2},{4,5},{5,4},{6,7},{7,6},{8,9},{9,8},{10,11... | collective-permute-start | bytes 1671176 | tf_op jit(solution)/shard_map/ppermute | solution.py:395
  6.4 8.0 %collective-permute-start.1 = (bf16[320,512]{1,0:T(8,128)(2,1)S(1)}, bf16[320,512]{1,0:T(8,128)(2,1)S(1)}, u32[]{:S(2)}, u32[]{:S(2)}) collective-permute-start(bf16[320,512]{1,0:T(8,128)(2,1)S(1)} %get-tuple-element.15.pay), channel_id=1, source_target_pairs={{0,2},{1,5},{2,0},{3,7},{4,6},{5,1},{6,4},{7,3},{8,10},{9,13},{10,... | collective-permute-start | bytes 983048 | tf_op jit(solution)/shard_map/ppermute | solution.py:395
  14.4 6.5 %collective-permute-start.2 = (bf16[256,512]{1,0:T(8,128)(2,1)S(1)}, bf16[256,512]{1,0:T(8,128)(2,1)S(1)}, u32[]{:S(2)}, u32[]{:S(2)}) collective-permute-start(bf16[256,512]{1,0:T(8,128)(2,1)S(1)} %get-tuple-element.17.pay), channel_id=1, source_target_pairs={{0,4},{1,3},{2,6},{3,1},{4,0},{5,7},{6,2},{7,5},{8,12},{9,11},{10,... | collective-permute-start | bytes 786440 | tf_op jit(solution)/shard_map/ppermute | solution.py:395
  20.9 5.9 %collective-permute-start.3 = (bf16[192,512]{1,0:T(8,128)(2,1)S(1)}, bf16[192,512]{1,0:T(8,128)(2,1)S(1)}, u32[]{:S(2)}, u32[]{:S(2)}) collective-permute-start(bf16[192,512]{1,0:T(8,128)(2,1)S(1)} %get-tuple-element.18), channel_id=1, source_target_pairs={{0,8},{1,17},{2,10},{3,19},{4,12},{5,21},{6,14},{7,23},{8,0},{9,25... | collective-permute-start | bytes 589832 | tf_op jit(solution)/shard_map/ppermute | solution.py:395
  26.9 4.0 %collective-permute-start.4 = (bf16[128,512]{1,0:T(8,128)(2,1)S(1)}, bf16[128,512]{1,0:T(8,128)(2,1)S(1)}, u32[]{:S(2)}, u32[]{:S(2)}) collective-permute-start(bf16[128,512]{1,0:T(8,128)(2,1)S(1)} %slice.8.mine_ref), channel_id=1, source_target_pairs={{0,1},{1,0},{2,3},{3,2},{4,5},{5,4},{6,7},{7,6},{8,9},{9,8},{10,11... | collective-permute-start | bytes 393224 | tf_op jit(solution)/shard_map/ppermute | solution.py:395
  30.8 25.5 %copy-start.5 = (bf16[512,512]{1,0:T(8,128)(2,1)S(1)}, bf16[512,512]{1,0:T(8,128)(2,1)}, u32[]{:S(2)}) copy-start(bf16[512,512]{1,0:T(8,128)(2,1)} %rotation.3) | copy-start | bytes 1572868
  30.8 27.0 %copy-start.4 = (bf16[8,100,496]{2,0,1:T(8,128)(2,1)S(1)}, bf16[8,100,496]{2,0,1:T(8,128)(2,1)}, u32[]{:S(2)}) copy-start(bf16[8,100,496]{2,0,1:T(8,128)(2,1)} %param.8) | copy-start | bytes 2380804
  34.0 6.0 %collective-permute-start.5 = (bf16[96,512]{1,0:T(8,128)(2,1)S(1)}, bf16[96,512]{1,0:T(8,128)(2,1)S(1)}, u32[]{:S(2)}, u32[]{:S(2)}) collective-permute-start(bf16[96,512]{1,0:T(8,128)(2,1)S(1)} %get-tuple-element.23.pay), channel_id=1, source_target_pairs={{0,16},{1,9},{2,18},{3,11},{4,20},{5,13},{6,22},{7,15},{8,24},{9,1... | collective-permute-start | bytes 294920 | tf_op jit(solution)/shard_map/ppermute | solution.py:395
  40.1 6.0 %collective-permute-start.6 = (bf16[64,512]{1,0:T(8,128)(2,1)S(1)}, bf16[64,512]{1,0:T(8,128)(2,1)S(1)}, u32[]{:S(2)}, u32[]{:S(2)}) collective-permute-start(bf16[64,512]{1,0:T(8,128)(2,1)S(1)} %shard_map.102.pay), channel_id=1, source_target_pairs={{0,8},{1,17},{2,10},{3,19},{4,12},{5,21},{6,14},{7,23},{8,0},{9,25... | collective-permute-start | bytes 196616 | tf_op jit(solution)/shard_map/ppermute | solution.py:395
  46.1 4.7 %collective-permute-start.7 = (bf16[96,512]{1,0:T(8,128)(2,1)S(1)}, bf16[96,512]{1,0:T(8,128)(2,1)S(1)}, u32[]{:S(2)}, u32[]{:S(2)}) collective-permute-start(bf16[96,512]{1,0:T(8,128)(2,1)S(1)} %shard_map.103.pay), channel_id=1, source_target_pairs={{0,4},{1,3},{2,6},{3,1},{4,0},{5,7},{6,2},{7,5},{8,12},{9,11},{10,... | collective-permute-start | bytes 294920 | tf_op jit(solution)/shard_map/ppermute | solution.py:395
  50.9 5.4 %collective-permute-start.8 = (bf16[160,512]{1,0:T(8,128)(2,1)S(1)}, bf16[160,512]{1,0:T(8,128)(2,1)S(1)}, u32[]{:S(2)}, u32[]{:S(2)}) collective-permute-start(bf16[160,512]{1,0:T(8,128)(2,1)S(1)} %shard_map.104.pay), channel_id=1, source_target_pairs={{0,2},{1,5},{2,0},{3,7},{4,6},{5,1},{6,4},{7,3},{8,10},{9,13},{10,... | collective-permute-start | bytes 491528 | tf_op jit(solution)/shard_map/ppermute | solution.py:395
  56.3 3.2 %collective-permute-start.9 = (bf16[288,512]{1,0:T(8,128)(2,1)S(1)}, bf16[288,512]{1,0:T(8,128)(2,1)S(1)}, u32[]{:S(2)}, u32[]{:S(2)}) collective-permute-start(bf16[288,512]{1,0:T(8,128)(2,1)S(1)} %shard_map.105.pay), channel_id=1, source_target_pairs={{0,1},{1,0},{2,3},{3,2},{4,5},{5,4},{6,7},{7,6},{8,9},{9,8},{10,11... | collective-permute-start | bytes 884744 | tf_op jit(solution)/shard_map/ppermute | solution.py:395

commit v2 on v0

v2 whole, which is shorter than its diff:
```python
import functools
import math

import jax
import jax.numpy as jnp
from jax import lax
from jax.experimental import pallas as pl
from jax.experimental.pallas import tpu as pltpu
from jax.sharding import PartitionSpec as P


F32 = jnp.float32
BF16 = jnp.bfloat16
BOTH = ("site", "mode")
LANES = 128


def dot_nn(a, b):
    return lax.dot_general(a, b, (((1,), (0,)), ((), ())), preferred_element_type=F32)


def dot_tn(a, b):
    return lax.dot_general(a, b, (((0,), (0,)), ((), ())), preferred_element_type=F32)


def onehot(shape, test):
    rows = lax.broadcasted_iota(jnp.int32, shape, 0)
    cols = lax.broadcasted_iota(jnp.int32, shape, 1)
    return jnp.where(test(rows, cols), 1.0, 0.0).astype(BF16)


def split(x):
    high = x.astype(BF16)
    low = (x - high.astype(F32)).astype(BF16)
    return high, low


def place():
    mode = lax.axis_index("mode")
    site = lax.axis_index("site")
    core = lax.rem(mode, 2)
    half = lax.div(mode, 2)
    y = lax.rem(site, 2)
    z0 = lax.rem(lax.div(site, 2), 2)
    z1 = lax.rem(lax.div(site, 4), 2)
    return core, half, y, z0, z1


def pick(core, first, second):
    return first * (1 - core) + second * core


def rows_at(index, count):
    return pl.ds(pl.multiple_of(index * count, count), count)


def call(kernel, outs, *args, scratch=(), flops=10**8, moved=2 * 10**6, smem=()):
    vmem = pl.BlockSpec(memory_space=pltpu.VMEM)
    scalars = pl.BlockSpec(memory_space=pltpu.SMEM)
    return pl.pallas_call(
        kernel,
        out_shape=outs,
        in_specs=[scalars if i in smem else vmem for i in range(len(args))],
        out_specs=jax.tree.map(lambda _: vmem, outs),
        scratch_shapes=scratch,
        compiler_params=pltpu.CompilerParams(vmem_limit_bytes=16 * 2**20),
        cost_estimate=pl.CostEstimate(flops=flops, bytes_accessed=moved, transcendentals=0),
    )(*args)


def shaped(rows, cols, dtype):
    return jax.ShapeDtypeStruct((rows, cols), dtype)


def first_kernel(nb, basis, images, pay):
    rows, nvec = basis.shape
    old = images.shape[1]
    blk = nvec - old
    core = place()[0]
    top = nvec // 2
    keep = basis[:, pl.ds(pl.multiple_of((1 - core) * top, top), top)]
    part = dot_tn(keep, images[...])
    high, low = split(part)
    pay[:top, :old] = high
    pay[:top, old:] = jnp.zeros((top, blk), BF16)
    pay[top : 2 * top, :old] = low
    pay[top : 2 * top, old:] = jnp.zeros((top, blk), BF16)
    wide = nb * blk
    last = basis[:, nvec - LANES :]
    spread = onehot((LANES, wide), lambda r, c: r - (LANES - blk) == lax.rem(c, blk))
    tiled = dot_nn(last, spread)
    row = lax.broadcasted_iota(jnp.int32, (rows, wide), 0)
    col = lax.broadcasted_iota(jnp.int32, (rows, wide), 1)
    tiled = jnp.where(lax.rem(row, nb) == lax.div(col, blk), tiled, 0.0).astype(BF16)
    gather = onehot((LANES, rows), lambda r, c: lax.div(c, nb) == r)
    merged = dot_nn(gather, tiled).astype(BF16)
    groups = nvec // LANES
    each = LANES // groups
    for g in range(groups):
        pay[2 * top :, g * LANES : (g + 1) * LANES] = merged[g * each : (g + 1) * each]


def keep_kernel(basis, images, kept):
    nvec = basis.shape[1]
    old = images.shape[1]
    core = place()[0]
    top = nvec // 2
    mine = basis[:, pl.ds(pl.multiple_of(core * top, top), top)]
    kept[:, :old] = dot_tn(mine, images[...])
    kept[:, old:] = jnp.zeros((top, nvec - old), F32)


def rotate_kernel(basis, rotation, out):
    out[...] = dot_nn(basis[...], rotation[...]).astype(BF16)


def joined(kept, got, start, count):
    whole = kept.shape[0]
    rows = pl.ds(pl.multiple_of(start, count), count)
    lows = pl.ds(pl.multiple_of(start + whole, count), count)
    return kept[rows, :] + (got[rows, :].astype(F32) + got[lows, :].astype(F32))


def second_kernel(kept, got, pay, out, rest, pair):
    core, half, y, _, _ = place()
    whole = kept.shape[0]
    n = whole // 2
    bit = pick(core, half, y)
    out[:n, :], out[n : 2 * n, :] = split(joined(kept, got, (1 - bit) * n, n))
    rest[...] = joined(kept, got, bit * n, n)
    each = got.shape[0] - 2 * whole
    pair[rows_at(core, each), :] = pay[2 * whole :, :]
    pair[rows_at(1 - core, each), :] = got[2 * whole :, :]
    out[2 * n :, :] = pair[...]


def third_kernel(kept, got, pair, far, out, rest):
    core, half, _, z0, _ = place()
    whole = kept.shape[0]
    n = whole // 2
    bit = pick(core, z0, half)
    out[:n, :], out[n : 2 * n, :] = split(joined(kept, got, (1 - bit) * n, n))
    rest[...] = joined(kept, got, bit * n, n)
    each = pair.shape[0]
    at = pick(core, 1 - half, 0)
    out[pl.ds(pl.multiple_of(2 * n + at * each, each), each), :] = got[2 * whole :, :]
    out[pl.ds(pl.multiple_of(2 * n + (1 - at) * each, each), each), :] = jnp.where(
        core == 0, pair[...], far[...]
    )


def fourth_kernel(kept, got, far, out, rest, cross):
    core, _, _, z0, z1 = place()
    whole = kept.shape[0]
    n = whole // 2
    bit = pick(core, z1, z0)
    out[:n, :], out[n:, :] = split(joined(kept, got, (1 - bit) * n, n))
    rest[...] = joined(kept, got, bit * n, n)
    area = got.shape[0] - 2 * whole
    cross[:area, :] = got[2 * whole :, :]
    cross[area:, :] = far[...]


def setup_kernel(near, nb, blk, spots, table, perms, shift):
    hops = perms.shape[0]
    wide = nb * blk
    coarse = shift.shape[0]
    share = coarse // spots
    row = lax.broadcasted_iota(jnp.int32, (2 * wide, wide), 0)
    col = lax.broadcasted_iota(jnp.int32, (2 * wide, wide), 1)
    for hop in range(hops):
        wanted = lax.rem(col, blk)
        for b in range(nb):
            entry = table[b, hop]
            q = lax.rem(entry, nb)
            base = q * blk
            if hop not in near:
                base = base + jnp.where(entry >= nb, wide, 0)
            wanted = wanted + jnp.where(lax.div(col, blk) == b, base, 0)
        perms[hop] = jnp.where(row == wanted, 1.0, 0.0).astype(BF16)
    shift[...] = onehot(
        (coarse, spots * LANES),
        lambda r, c: (lax.rem(c, LANES) < share) & (lax.div(c, LANES) * share + lax.rem(c, LANES) == r),
    )


def stack(ref, at, piece):
    rows, nvec = piece.shape
    groups = nvec // LANES
    each = LANES // groups
    chunks = rows // each
    parts = [
        piece[m * each : (m + 1) * each, g * LANES : (g + 1) * LANES] for m in range(chunks) for g in range(groups)
    ]
    ref[rows_at(at, chunks * LANES), :] = jnp.concatenate(parts, axis=0)


def near_kernel(order, pair, got, crossed, hops, perms, shift, total, own_out, column):
    core, half, _, _, _ = place()
    each = pair.shape[0]
    wide = own_out.shape[1]
    area = got.shape[0]
    stack(column, half, pair[...])
    stack(column, 1 - half, jnp.where(core == 0, got[area - each :, :], crossed[...]))
    own = dot_nn(shift[...], column[...]).astype(BF16)
    own_out[...] = own
    rows = total.shape[0]
    mixed = [dot_nn(own, perms[hop, :wide, :]).astype(BF16) for hop in order]
    step = rows // 2
    for r in range(2):
        span = pl.ds(r * step, step)
        part = dot_nn(hops[order[0], span, :], mixed[0])
        for i in range(1, len(order)):
            part = part + dot_nn(hops[order[i], span, :], mixed[i])
        total[span, :] = part


def far_kernel(nb, blk, own, got2, cross, far, got1, crossed, total, basis, hops, perms, shift, *refs):
    times, (masked, new_out, column) = refs[:-3], refs[-3:]
    core, half, _, _, _ = place()
    each = far.shape[0]
    wide = own.shape[1]
    rows = basis.shape[0]
    nvec = basis.shape[1]
    first = core == 0
    mine = got2[got2.shape[0] - 2 * each :, :]
    theirs = cross[: 2 * each, :]
    sites = []
    one = jnp.where(first, theirs, mine)
    two = jnp.where(first, mine, theirs)
    stack(column.at[0], half, jnp.where(first, crossed[...], got1[got1.shape[0] - each :, :]))
    stack(column.at[0], 1 - half, one[:each])
    stack(column.at[1], half, jnp.where(first, cross[2 * each :, :], far[...]))
    stack(column.at[1], 1 - half, one[each:])
    stack(column.at[2], 0, two)
    near_site = dot_nn(shift[...], column[0]).astype(BF16)
    long_site = dot_nn(shift[...], column[1]).astype(BF16)
    mid_site = dot_nn(shift[...], column[2]).astype(BF16)
    sites = {1: long_site, 4: long_site, 2: mid_site, 5: mid_site, 3: near_site, 6: near_site}
    for k, ref in enumerate(times):
        sites[7 + k] = ref[...]
    order = sorted(sites)
    mixed = [
        (dot_nn(own[...], perms[hop, :wide, :]) + dot_nn(sites[hop], perms[hop, wide:, :])).astype(BF16)
        for hop in order
    ]
    step = rows // 2
    sums = jnp.zeros((wide, nvec), F32)
    for r in range(2):
        span = pl.ds(r * step, step)
        part = total[span, :]
        for i, hop in enumerate(order):
            part = part + dot_nn(hops[hop, span, :], mixed[i])
        row = lax.broadcasted_iota(jnp.int32, (step, wide), 0)
        col = lax.broadcasted_iota(jnp.int32, (step, wide), 1)
        chosen = jnp.where(lax.rem(row, nb) == lax.div(col, blk), part, 0.0).astype(BF16)
        masked[span, :] = chosen
        sums = sums + dot_tn(chosen, basis[span, :])
    new = sums[:blk]
    for b in range(1, nb):
        new = new + sums[b * blk : (b + 1) * blk]
    new_out[:blk, :], new_out[blk:, :] = split(new)


def join_kernel(kept, got, new, out):
    n = kept.shape[0]
    total = kept[...] + (got[:n, :].astype(F32) + got[n:, :].astype(F32))
    out[:n, :], out[n : 2 * n, :] = split(total)
    out[2 * n :, :] = new[...]


def turn_kernel(nb, images, masked, rotation, out):
    old = images.shape[1]
    tail = rotation[old:, :]
    deep = jnp.concatenate([tail] * nb, axis=0)
    out[...] = (dot_nn(images[...], rotation[:old, :]) + dot_nn(masked[...], deep)).astype(BF16)


def value(ref, start, count):
    return ref[start : start + count, :].astype(F32) + ref[start + count : start + 2 * count, :].astype(F32)


def extra_kernel(n, blk, pay, got, out):
    out[:n, :], out[n : 2 * n, :] = split(value(pay, 0, n) + value(got, 0, n))
    out[2 * n : 2 * n + blk, :], out[2 * n + blk :, :] = split(value(pay, 2 * n, blk) + value(got, 2 * n, blk))


def settle_kernel(n, blk, scale, pay, got, out):
    out[:n, :] = ((value(pay, 0, n) + value(got, 0, n)) * scale).astype(BF16)
    out[n : n + blk, :], out[n + blk :, :] = split(value(pay, 2 * n, blk) + value(got, 2 * n, blk))


def grow_kernel(n, blk, chooser, pay, got, out):
    bit = chooser(*place())
    out[rows_at(bit, n), :] = pay[:n, :]
    out[rows_at(1 - bit, n), :] = got[:n, :]
    out[2 * n : 2 * n + blk, :], out[2 * n + blk :, :] = split(value(pay, n, blk) + value(got, n, blk))


def final_kernel(n, blk, scale, pay, got, out):
    nvec = out.shape[1]
    core = place()[0]
    out[rows_at(core, n), :] = pay[:n, :].astype(F32)
    out[rows_at(1 - core, n), :] = got[:n, :].astype(F32)
    new = (value(pay, n, blk) + value(got, n, blk)) * scale
    tall = jnp.concatenate([jnp.zeros((LANES - blk, nvec), F32), new], axis=0)
    flipped = tall.T
    lane = lax.broadcasted_iota(jnp.int32, (nvec, LANES), 1)
    out[:, nvec - LANES :] = jnp.where(lane < LANES - blk, out[:, nvec - LANES :], flipped)


def program(basis, images, hops, neighbours, rotation):
    nb, modes_here, nvec = basis.shape
    old = images.shape[2]
    blk = nvec - old
    sites = lax.axis_size("site")
    spots = lax.axis_size("mode")
    count = sites * spots
    rows = nb * modes_here
    coarse = hops.shape[3]
    wide = nb * blk
    chunk = wide * LANES // nvec
    scale = 1.0 / math.sqrt(count * rows)

    def send(x, first, second):
        pairs = [(d, d ^ hop) for d in range(count) for hop in [second if d % 2 else first] if hop]
        return lax.ppermute(x, BOTH, pairs)

    core_hop, x_hop, y_hop, z0_hop, z1_hop = 1, 2, spots, 2 * spots, 4 * spots

    flat_basis = jnp.transpose(basis, (1, 0, 2)).reshape(rows, nvec)
    flat_images = jnp.transpose(images, (1, 0, 2)).reshape(rows, old)
    flat_hops = jnp.transpose(hops, (1, 2, 0, 3)).reshape(hops.shape[1], rows, coarse)
    own_rows = jnp.arange(nb, dtype=jnp.int32)
    table = jnp.concatenate([own_rows[:, None], neighbours], axis=1)
    near_order = [0] if sites > 8 else [0, 7, 8]

    half = nvec // 2
    n = half // 8
    pay0 = call(functools.partial(first_kernel, nb), shaped(nvec + chunk, nvec, BF16), flat_basis, flat_images)
    got0 = send(pay0, core_hop, core_hop)
    kept0 = call(keep_kernel, shaped(half, nvec, F32), flat_basis, flat_images)
    pay1, kept1, pair = call(
        second_kernel,
        (shaped(half + 2 * chunk, nvec, BF16), shaped(half // 2, nvec, F32), shaped(2 * chunk, nvec, BF16)),
        kept0,
        got0,
        pay0,
    )
    got1 = send(pay1, x_hop, y_hop)
    far = send(pair, 0, z1_hop)
    perms, shift = call(
        functools.partial(setup_kernel, near_order, nb, blk, spots),
        (
            jax.ShapeDtypeStruct((hops.shape[1], 2 * wide, wide), BF16),
            shaped(coarse, spots * LANES, BF16),
        ),
        table,
        smem=(0,),
    )
    turned_basis = call(rotate_kernel, shaped(rows, nvec, BF16), flat_basis, rotation)
    pay2, kept2 = call(
        third_kernel,
        (shaped(half // 2 + 4 * chunk, nvec, BF16), shaped(half // 4, nvec, F32)),
        kept1,
        got1,
        pair,
        far,
    )
    got2 = send(pay2, z0_hop, x_hop)
    crossed = send(got1[half:, :], core_hop, core_hop)
    total, own = call(
        functools.partial(near_kernel, near_order),
        (shaped(rows, wide, F32), shaped(coarse, wide, BF16)),
        pair,
        got1,
        crossed,
        flat_hops,
        perms,
        shift,
        scratch=[pltpu.VMEM((spots * LANES, wide), BF16)],
    )
    times = []
    if sites > 8:
        gap = 8 * spots
        times = [lax.ppermute(own, BOTH, [((d + sign * gap) % count, d) for d in range(count)]) for sign in (1, -1)]
    pay3, kept3, cross_pay = call(
        fourth_kernel,
        (shaped(half // 4, nvec, BF16), shaped(half // 8, nvec, F32), shaped(6 * chunk, nvec, BF16)),
        kept2,
        got2,
        far,
    )
    cross = send(cross_pay, core_hop, core_hop)
    got3 = send(pay3, z1_hop, z0_hop)
    masked, new = call(
        functools.partial(far_kernel, nb, blk),
        (shaped(rows, wide, BF16), shaped(2 * blk, nvec, BF16)),
        own,
        got2,
        cross,
        far,
        got1,
        crossed,
        total,
        flat_basis,
        flat_hops,
        perms,
        shift,
        *times,
        scratch=[pltpu.VMEM((3, spots * LANES, wide), BF16)],
    )
    payc = call(join_kernel, shaped(2 * n + 2 * blk, nvec, BF16), kept3, got3, new)
    gotc = send(payc, y_hop, z1_hop)
    turned_images = call(functools.partial(turn_kernel, nb), shaped(rows, nvec, BF16), flat_images, masked, rotation)
    hop = 8 * spots
    while hop < count:
        payc = call(functools.partial(extra_kernel, n, blk), shaped(2 * n + 2 * blk, nvec, BF16), payc, gotc)
        gotc = send(payc, hop, hop)
        hop *= 2
    payc = call(functools.partial(settle_kernel, n, blk, scale), shaped(n + 2 * blk, nvec, BF16), payc, gotc)
    steps = (
        (z1_hop, z0_hop, lambda core, half, y, z0, z1: pick(core, z1, z0)),
        (z0_hop, x_hop, lambda core, half, y, z0, z1: pick(core, z0, half)),
        (x_hop, y_hop, lambda core, half, y, z0, z1: pick(core, half, y)),
    )
    for first, second, chooser in steps:
        gotc = send(payc, first, second)
        payc = call(
            functools.partial(grow_kernel, n, blk, chooser), shaped(2 * n + 2 * blk, nvec, BF16), payc, gotc
        )
        n *= 2
    gotc = send(payc, core_hop, core_hop)
    projected = call(functools.partial(final_kernel, n, blk, scale), shaped(nvec, nvec, F32), payc, gotc)

    def back(x):
        return jnp.transpose(x.reshape(modes_here, nb, nvec), (1, 0, 2))

    return projected, back(turned_basis), back(turned_images)


def solution(mesh):
    placed = (
        P("site", "mode", None),
        P("site", "mode", None),
        P("site", None, "mode", None),
        P("site", None),
        P(),
    )
    return jax.shard_map(
        program,
        mesh=mesh,
        in_specs=placed,
        out_specs=(P(), P("site", "mode", None), P("site", "mode", None)),
        check_vma=False,
    )
```

time: 156 us -> 55.6 us (0.36)
  blocking collectives: 52.5 us -> 0 us
  waiting for transfers between devices: 60.7 us -> 25 us
  between operations: 14.2 us -> 0.84 us
  Pallas kernels: 0 us -> 11.3 us
  matrix products: 9.92 us -> 0 us
  starting transfers between devices: 7.26 us -> 14.8 us
  local copies, waits for them, and re-layouts: 9.89 us -> 2.69 us
    psum x1 -> x0, waiting for transfers between devices: 60.7 us -> none  [local(): old_sum = lax.psum(old_part, ('site', 'mode'))]
    psum x1 -> x0, blocking collectives: 38 us -> none  [local(): new_sum = lax.psum(new_part, ('site', 'mode'))]
    ppermute x3 -> x12, waiting for transfers between devices: 0.01 us -> 25 us  [send(): return lax.ppermute(x, BOTH, pairs)]
    all_gather x1 -> x0, blocking collectives: 14.5 us -> none  [local(): widened = lax.all_gather(stacked, 'mode', axis=2, tiled=True)]
    pallas_call x0 -> x16, Pallas kernels: none -> 11.3 us  [call(): pl.pallas_call(kernel, out_shape=outs, in_specs=[scalars if i in smem els...]
    dot_general x5 -> x0, matrix products: 9.92 us -> none  [the longest x1 5.31 us: local(): jnp.einsum('bdoi,bdki->bok', hops, gathered, preferred_element_type=jnp.f...]
    ppermute x3 -> x12, starting transfers between devices: 7.22 us -> 14.8 us  [send(): return lax.ppermute(x, BOTH, pairs)]
    all_gather x1 -> x0, local copies, waits for them, and re-layouts: 2.12 us -> none  [local(): widened = lax.all_gather(stacked, 'mode', axis=2, tiled=True)]
  transfers between devices with their start and end apart: 4 -> 12, of which waited for: 1 -> 7; matrix products, arithmetic and copies ran while one was open for 11% -> 1% of each run, Pallas kernels for 0% -> 16%
where the time goes in v2:
time: 55.6 us; the launch traced here: 55.4 us
  waiting for transfers between devices  25 us (45%)
  starting transfers between devices  14.8 us (27%)
  Pallas kernels  11.3 us (20%)
  local copies, waits for them, and re-layouts  2.69 us (5%)
  between operations  0.84 us (2%)
  other arithmetic  0.76 us (1%)
    ppermute x12, waiting for transfers between devices, send(): return lax.ppermute(x, BOTH, pairs)  25 us
    ppermute x12, starting transfers between devices, send(): return lax.ppermute(x, BOTH, pairs)  14.8 us
    pallas_call x16, Pallas kernels, call(): pl.pallas_call(kernel, out_shape=outs, in_specs=[scalars if i in smem els...  11.3 us
    unnamed x12, local copies, waits for them, and re-layouts  2.68 us
  transfers between devices with their start and end apart: 12, of which 7 were waited for; matrix products, arithmetic and copies ran while one was open for 1% of the time, Pallas kernels for 16%

profile of v2, /device:TPU:0, one launch (start us, length us, event | category | flops | bytes accessed | tf_op | source)
XLA Modules:
  0.0 55.4 jit_solution(13172703168037346797)
XLA Ops:
  0.7 1.3 %copy-done.1 = bf16[8,100,512]{2,0,1:T(8,128)(2,1)S(1)} copy-done((bf16[8,100,512]{2,0,1:T(8,128)(2,1)S(1)}, bf16[8,100,512]{2,0,1:T(8,128)(2,1)}, u32[]{:S(2)}) %copy-start.1) | copy-done | bytes 819224
  1.9 1.4 %copy-done.3 = bf16[8,100,496]{2,0,1:T(8,128)(2,1)S(1)} copy-done((bf16[8,100,496]{2,0,1:T(8,128)(2,1)S(1)}, bf16[8,100,496]{2,0,1:T(8,128)(2,1)}, u32[]{:S(2)}) %copy-start.3) | copy-done | bytes 793624
  3.3 0.8 %shard_map.77.pay = bf16[544,512]{1,0:T(8,128)(2,1)S(1)} custom-call(bf16[800,512]{1,0:T(8,128)(2,1)S(1)} %bitcast.17, bf16[800,496]{1,0:T(8,128)(2,1)S(1)} %bitcast.21), custom_call_target="tpu_custom_call" | custom-call | flops 100000000 | bytes 2000000 | tf_op jit(solution)/shard_map/pallas_call | solution.py:60
  4.1 0.5 collective-permute-start
  4.6 0.5 shard_map.76.kept
  5.1 1.1 %collective-permute-done.got = bf16[544,512]{1,0:T(8,128)(2,1)S(1)} collective-permute-done((bf16[544,512]{1,0:T(8,128)(2,1)S(1)}, bf16[544,512]{1,0:T(8,128)(2,1)S(1)}, u32[]{:S(2)}, u32[]{:S(2)}) %collective-permute-start) | collective-permute-done | bytes 557088 | tf_op jit(solution)/shard_map/ppermute | solution.py:327
  6.2 0.2 shard_map.78
  6.4 2.9 %collective-permute-start.1 = (bf16[320,512]{1,0:T(8,128)(2,1)S(1)}, bf16[320,512]{1,0:T(8,128)(2,1)S(1)}, u32[]{:S(2)}, u32[]{:S(2)}) collective-permute-start(bf16[320,512]{1,0:T(8,128)(2,1)S(1)} %get-tuple-element.18), channel_id=1, source_target_pairs={{0,2},{1,5},{2,0},{3,7},{4,6},{5,1},{6,4},{7,3},{8,10},{9,13},{10,... | collective-permute-start | bytes 983048 | tf_op jit(solution)/shard_map/ppermute | solution.py:327
  9.3 0.7 %collective-permute-start.2 = (bf16[64,512]{1,0:T(8,128)(2,1)S(1)}, bf16[64,512]{1,0:T(8,128)(2,1)S(1)}, u32[]{:S(2)}, u32[]{:S(2)}) collective-permute-start(bf16[64,512]{1,0:T(8,128)(2,1)S(1)} %get-tuple-element.19.pair), channel_id=1, source_target_pairs={{1,17},{3,19},{5,21},{7,23},{9,25},{11,27},{13,29},{15,31},{17,1},... | collective-permute-start | bytes 196616 | tf_op jit(solution)/shard_map/ppermute | solution.py:327
  10.0 4.4 %collective-permute-done.1.got.got1 = bf16[320,512]{1,0:T(8,128)(2,1)S(1)} collective-permute-done((bf16[320,512]{1,0:T(8,128)(2,1)S(1)}, bf16[320,512]{1,0:T(8,128)(2,1)S(1)}, u32[]{:S(2)}, u32[]{:S(2)}) %collective-permute-start.1) | collective-permute-done | bytes 327712 | tf_op jit(solution)/shard_map/ppermute | solution.py:327
  14.4 0.1 shard_map.79
  14.4 2.2 %collective-permute-start.3 = (bf16[256,512]{1,0:T(8,128)(2,1)S(1)}, bf16[256,512]{1,0:T(8,128)(2,1)S(1)}, u32[]{:S(2)}, u32[]{:S(2)}) collective-permute-start(bf16[256,512]{1,0:T(8,128)(2,1)S(1)} %get-tuple-element.21), channel_id=1, source_target_pairs={{0,8},{1,3},{2,10},{3,1},{4,12},{5,7},{6,14},{7,5},{8,0},{9,11},{1... | collective-permute-start | bytes 786440 | tf_op jit(solution)/shard_map/ppermute | solution.py:327
  16.6 4.4 %collective-permute-done.3.got.got2 = bf16[256,512]{1,0:T(8,128)(2,1)S(1)} collective-permute-done((bf16[256,512]{1,0:T(8,128)(2,1)S(1)}, bf16[256,512]{1,0:T(8,128)(2,1)S(1)}, u32[]{:S(2)}, u32[]{:S(2)}) %collective-permute-start.3) | collective-permute-done | bytes 262176 | tf_op jit(solution)/shard_map/ppermute | solution.py:327
  21.0 0.1 collective-permute-start.6
  21.1 0.5 collective-permute-start.5
  21.6 3.0 %collective-permute-start.4 = (bf16[64,512]{1,0:T(8,128)(2,1)S(1)}, bf16[64,512]{1,0:T(8,128)(2,1)S(1)}, u32[]{:S(2)}, u32[]{:S(2)}) collective-permute-start(bf16[64,512]{1,0:T(8,128)(2,1)S(1)} %get-tuple-element.23), channel_id=1, source_target_pairs={{0,16},{1,9},{2,18},{3,11},{4,20},{5,13},{6,22},{7,15},{8,24},{9,1... | collective-permute-start | bytes 196616 | tf_op jit(solution)/shard_map/ppermute | solution.py:327
  24.6 0.8 %pad_add_fusion.table = s32[8,9]{1,0:T(8,128)S(1)} fusion(s32[8,8]{1,0:T(8,128)} %param.8, s32[8,1]{1,0:T(8,128)S(1)} %iota.4), kind=kLoop, calls=%fused_computation | loop fusion | flops 72 | bytes 576 | tf_op jit(solution)/shard_map/concatenate | solution.py:335
  25.4 0.9 %shard_map.81 = (bf16[9,256,128]{2,1,0:T(8,128)(2,1)S(1)}, bf16[400,512]{1,0:T(8,128)(2,1)S(1)}) custom-call(s32[8,9]{1,0:T(8,128)S(1)} %pad_add_fusion.table), custom_call_target="tpu_custom_call" | custom-call | flops 100000000 | bytes 2000000 | tf_op jit(solution)/shard_map/pallas_call | solution.py:60
  26.3 1.3 %shard_map.82 = (f32[800,128]{1,0:T(8,128)S(1)}, bf16[400,128]{1,0:T(8,128)(2,1)S(1)}) custom-call(bf16[64,512]{1,0:T(8,128)(2,1)S(1)} %get-tuple-element.19.pair, bf16[320,512]{1,0:T(8,128)(2,1)S(1)} %collective-permute-done.1.got.got1, bf16[64,512]{1,0:T(8,128)(2,1)S(1)} %collective-permute-done.5.crossed, bf16[9,800,400]{2,1,0:T(8,128)(2,1)S(1)} %bitcast.15, ...), custom_call_target="tpu_custom_call" | custom-call | flops 100000000 | bytes 2000000 | tf_op jit(solution)/shard_map/pallas_call | solution.py:60
  27.7 3.1 %shard_map.83 = (bf16[800,128]{1,0:T(8,128)(2,1)S(1)}, bf16[32,512]{1,0:T(8,128)(2,1)S(1)}) custom-call(bf16[400,128]{1,0:T(8,128)(2,1)S(1)} %get-tuple-element.26.own, bf16[256,512]{1,0:T(8,128)(2,1)S(1)} %collective-permute-done.3.got.got2, bf16[192,512]{1,0:T(8,128)(2,1)S(1)} %collective-permute-done.6.cross, ...), custom_call_target="tpu_custom_call" | custom-call | flops 100000000 | bytes 2000000 | tf_op jit(solution)/shard_map/pallas_call | solution.py:60
  30.9 1.6 %collective-permute-start.7 = (bf16[96,512]{1,0:T(8,128)(2,1)S(1)}, bf16[96,512]{1,0:T(8,128)(2,1)S(1)}, u32[]{:S(2)}, u32[]{:S(2)}) collective-permute-start(bf16[96,512]{1,0:T(8,128)(2,1)S(1)} %shard_map.84.pay), channel_id=1, source_target_pairs={{0,4},{1,17},{2,6},{3,19},{4,0},{5,21},{6,2},{7,23},{8,12},{9,25},... | collective-permute-start | bytes 294920 | tf_op jit(solution)/shard_map/ppermute | solution.py:327
  32.5 3.1 %collective-permute-done.7.got = bf16[96,512]{1,0:T(8,128)(2,1)S(1)} collective-permute-done((bf16[96,512]{1,0:T(8,128)(2,1)S(1)}, bf16[96,512]{1,0:T(8,128)(2,1)S(1)}, u32[]{:S(2)}, u32[]{:S(2)}) %collective-permute-start.7) | collective-permute-done | bytes 98336 | tf_op jit(solution)/shard_map/ppermute | solution.py:327
  35.6 0.1 collective-permute-start.8
  35.7 5.2 %collective-permute-done.8.got = bf16[64,512]{1,0:T(8,128)(2,1)S(1)} collective-permute-done((bf16[64,512]{1,0:T(8,128)(2,1)S(1)}, bf16[64,512]{1,0:T(8,128)(2,1)S(1)}, u32[]{:S(2)}, u32[]{:S(2)}) %collective-permute-start.8) | collective-permute-done | bytes 65568 | tf_op jit(solution)/shard_map/ppermute | solution.py:327
  40.9 1.6 %collective-permute-start.9 = (bf16[96,512]{1,0:T(8,128)(2,1)S(1)}, bf16[96,512]{1,0:T(8,128)(2,1)S(1)}, u32[]{:S(2)}, u32[]{:S(2)}) collective-permute-start(bf16[96,512]{1,0:T(8,128)(2,1)S(1)} %shard_map.86.pay), channel_id=1, source_target_pairs={{0,8},{1,3},{2,10},{3,1},{4,12},{5,7},{6,14},{7,5},{8,0},{9,11},{1... | collective-permute-start | bytes 294920 | tf_op jit(solution)/shard_map/ppermute | solution.py:327
  42.5 3.0 %collective-permute-done.9.got = bf16[96,512]{1,0:T(8,128)(2,1)S(1)} collective-permute-done((bf16[96,512]{1,0:T(8,128)(2,1)S(1)}, bf16[96,512]{1,0:T(8,128)(2,1)S(1)}, u32[]{:S(2)}, u32[]{:S(2)}) %collective-permute-start.9) | collective-permute-done | bytes 98336 | tf_op jit(solution)/shard_map/ppermute | solution.py:327
  45.6 1.6 %collective-permute-start.10 = (bf16[160,512]{1,0:T(8,128)(2,1)S(1)}, bf16[160,512]{1,0:T(8,128)(2,1)S(1)}, u32[]{:S(2)}, u32[]{:S(2)}) collective-permute-start(bf16[160,512]{1,0:T(8,128)(2,1)S(1)} %shard_map.87.pay), channel_id=1, source_target_pairs={{0,2},{1,5},{2,0},{3,7},{4,6},{5,1},{6,4},{7,3},{8,10},{9,13},{10,... | collective-permute-start | bytes 491528 | tf_op jit(solution)/shard_map/ppermute | solution.py:327
  47.1 3.8 %collective-permute-done.10.got = bf16[160,512]{1,0:T(8,128)(2,1)S(1)} collective-permute-done((bf16[160,512]{1,0:T(8,128)(2,1)S(1)}, bf16[160,512]{1,0:T(8,128)(2,1)S(1)}, u32[]{:S(2)}, u32[]{:S(2)}) %collective-permute-start.10) | collective-permute-done | bytes 163872 | tf_op jit(solution)/shard_map/ppermute | solution.py:327
  51.0 0.1 collective-permute-start.11
  51.1 1.5 %shard_map.90 = bf16[800,512]{1,0:T(8,128)(2,1)} custom-call(bf16[800,512]{1,0:T(8,128)(2,1)S(1)} %bitcast.20, bf16[512,512]{1,0:T(8,128)(2,1)S(1)} %copy-done.5), custom_call_target="tpu_custom_call" | custom-call | flops 100000000 | bytes 2000000 | tf_op jit(solution)/shard_map/pallas_call | solution.py:60
  52.6 1.7 %shard_map.91 = bf16[800,512]{1,0:T(8,128)(2,1)} custom-call(bf16[800,496]{1,0:T(8,128)(2,1)S(1)} %bitcast.23, bf16[800,128]{1,0:T(8,128)(2,1)S(1)} %get-tuple-element.30.masked, bf16[512,512]{1,0:T(8,128)(2,1)S(1)} %copy-done.5), custom_call_target="tpu_custom_call" | custom-call | flops 100000000 | bytes 2000000 | tf_op jit(solution)/shard_map/pallas_call | solution.py:60
  54.3 1.1 %shard_map.89 = f32[512,512]{1,0:T(8,128)} custom-call(bf16[288,512]{1,0:T(8,128)(2,1)S(1)} %shard_map.88.pay, bf16[288,512]{1,0:T(8,128)(2,1)S(1)} %collective-permute-done.11.got), custom_call_target="tpu_custom_call" | custom-call | flops 100000000 | bytes 2000000 | tf_op jit(solution)/shard_map/pallas_call | solution.py:60
  (23 shorter events, 0.3 us)
Async XLA Ops:
  0.6 25.7 %copy-start = (bf16[8,9,100,400]{3,0,2,1:T(8,128)(2,1)S(1)}, bf16[8,9,100,400]{3,0,2,1:T(8,128)(2,1)}, u32[]{:S(2)}) copy-start(bf16[8,9,100,400]{3,0,2,1:T(8,128)(2,1)} %param.7) | copy-start | bytes 17280004
  0.6 1.3 %copy-start.1 = (bf16[8,100,512]{2,0,1:T(8,128)(2,1)S(1)}, bf16[8,100,512]{2,0,1:T(8,128)(2,1)}, u32[]{:S(2)}) copy-start(bf16[8,100,512]{2,0,1:T(8,128)(2,1)} %param.5) | copy-start | bytes 2457604
  1.9 1.4 %copy-start.3 = (bf16[8,100,496]{2,0,1:T(8,128)(2,1)S(1)}, bf16[8,100,496]{2,0,1:T(8,128)(2,1)}, u32[]{:S(2)}) copy-start(bf16[8,100,496]{2,0,1:T(8,128)(2,1)} %param.6) | copy-start | bytes 2380804
  4.1 23.6 %copy-start.2 = (bf16[8,100,512]{2,0,1:T(8,128)(2,1)S(1)}, bf16[8,100,512]{2,0,1:T(8,128)(2,1)}, u32[]{:S(2)}) copy-start(bf16[8,100,512]{2,0,1:T(8,128)(2,1)} %param.5) | copy-start | bytes 2457604
  4.1 2.1 %collective-permute-start = (bf16[544,512]{1,0:T(8,128)(2,1)S(1)}, bf16[544,512]{1,0:T(8,128)(2,1)S(1)}, u32[]{:S(2)}, u32[]{:S(2)}) collective-permute-start(bf16[544,512]{1,0:T(8,128)(2,1)S(1)} %shard_map.77.pay), channel_id=1, source_target_pairs={{0,1},{1,0},{2,3},{3,2},{4,5},{5,4},{6,7},{7,6},{8,9},{9,8},{10,11... | collective-permute-start | bytes 1671176 | tf_op jit(solution)/shard_map/ppermute | solution.py:327
  6.4 8.0 %collective-permute-start.1 = (bf16[320,512]{1,0:T(8,128)(2,1)S(1)}, bf16[320,512]{1,0:T(8,128)(2,1)S(1)}, u32[]{:S(2)}, u32[]{:S(2)}) collective-permute-start(bf16[320,512]{1,0:T(8,128)(2,1)S(1)} %get-tuple-element.18), channel_id=1, source_target_pairs={{0,2},{1,5},{2,0},{3,7},{4,6},{5,1},{6,4},{7,3},{8,10},{9,13},{10,... | collective-permute-start | bytes 983048 | tf_op jit(solution)/shard_map/ppermute | solution.py:327
  9.3 0.7 %collective-permute-start.2 = (bf16[64,512]{1,0:T(8,128)(2,1)S(1)}, bf16[64,512]{1,0:T(8,128)(2,1)S(1)}, u32[]{:S(2)}, u32[]{:S(2)}) collective-permute-start(bf16[64,512]{1,0:T(8,128)(2,1)S(1)} %get-tuple-element.19.pair), channel_id=1, source_target_pairs={{1,17},{3,19},{5,21},{7,23},{9,25},{11,27},{13,29},{15,31},{17,1},... | collective-permute-start | bytes 196616 | tf_op jit(solution)/shard_map/ppermute | solution.py:327
  14.4 6.5 %collective-permute-start.3 = (bf16[256,512]{1,0:T(8,128)(2,1)S(1)}, bf16[256,512]{1,0:T(8,128)(2,1)S(1)}, u32[]{:S(2)}, u32[]{:S(2)}) collective-permute-start(bf16[256,512]{1,0:T(8,128)(2,1)S(1)} %get-tuple-element.21), channel_id=1, source_target_pairs={{0,8},{1,3},{2,10},{3,1},{4,12},{5,7},{6,14},{7,5},{8,0},{9,11},{1... | collective-permute-start | bytes 786440 | tf_op jit(solution)/shard_map/ppermute | solution.py:327
  21.0 6.7 %collective-permute-start.6 = (bf16[192,512]{1,0:T(8,128)(2,1)S(1)}, bf16[192,512]{1,0:T(8,128)(2,1)S(1)}, u32[]{:S(2)}, u32[]{:S(2)}) collective-permute-start(bf16[192,512]{1,0:T(8,128)(2,1)S(1)} %get-tuple-element.27), channel_id=1, source_target_pairs={{0,1},{1,0},{2,3},{3,2},{4,5},{5,4},{6,7},{7,6},{8,9},{9,8},{10,11... | collective-permute-start | bytes 589832 | tf_op jit(solution)/shard_map/ppermute | solution.py:327
  21.1 5.2 %collective-permute-start.5 = (bf16[64,512]{1,0:T(8,128)(2,1)S(1)}, bf16[64,512]{1,0:T(8,128)(2,1)S(1)}, u32[]{:S(2)}, u32[]{:S(2)}) collective-permute-start(bf16[64,512]{1,0:T(8,128)(2,1)S(1)} %slice.4), channel_id=1, source_target_pairs={{0,1},{1,0},{2,3},{3,2},{4,5},{5,4},{6,7},{7,6},{8,9},{9,8},{10,11... | collective-permute-start | bytes 196616 | tf_op jit(solution)/shard_map/ppermute | solution.py:327
  21.6 9.2 %collective-permute-start.4 = (bf16[64,512]{1,0:T(8,128)(2,1)S(1)}, bf16[64,512]{1,0:T(8,128)(2,1)S(1)}, u32[]{:S(2)}, u32[]{:S(2)}) collective-permute-start(bf16[64,512]{1,0:T(8,128)(2,1)S(1)} %get-tuple-element.23), channel_id=1, source_target_pairs={{0,16},{1,9},{2,18},{3,11},{4,20},{5,13},{6,22},{7,15},{8,24},{9,1... | collective-permute-start | bytes 196616 | tf_op jit(solution)/shard_map/ppermute | solution.py:327
  27.7 23.4 %copy-start.5 = (bf16[512,512]{1,0:T(8,128)(2,1)S(1)}, bf16[512,512]{1,0:T(8,128)(2,1)}, u32[]{:S(2)}) copy-start(bf16[512,512]{1,0:T(8,128)(2,1)} %rotation.3) | copy-start | bytes 1572868
  27.7 24.9 %copy-start.4 = (bf16[8,100,496]{2,0,1:T(8,128)(2,1)S(1)}, bf16[8,100,496]{2,0,1:T(8,128)(2,1)}, u32[]{:S(2)}) copy-start(bf16[8,100,496]{2,0,1:T(8,128)(2,1)} %param.6) | copy-start | bytes 2380804
  30.9 4.7 %collective-permute-start.7 = (bf16[96,512]{1,0:T(8,128)(2,1)S(1)}, bf16[96,512]{1,0:T(8,128)(2,1)S(1)}, u32[]{:S(2)}, u32[]{:S(2)}) collective-permute-start(bf16[96,512]{1,0:T(8,128)(2,1)S(1)} %shard_map.84.pay), channel_id=1, source_target_pairs={{0,4},{1,17},{2,6},{3,19},{4,0},{5,21},{6,2},{7,23},{8,12},{9,25},... | collective-permute-start | bytes 294920 | tf_op jit(solution)/shard_map/ppermute | solution.py:327
  35.6 5.2 %collective-permute-start.8 = (bf16[64,512]{1,0:T(8,128)(2,1)S(1)}, bf16[64,512]{1,0:T(8,128)(2,1)S(1)}, u32[]{:S(2)}, u32[]{:S(2)}) collective-permute-start(bf16[64,512]{1,0:T(8,128)(2,1)S(1)} %shard_map.85.pay), channel_id=1, source_target_pairs={{0,16},{1,9},{2,18},{3,11},{4,20},{5,13},{6,22},{7,15},{8,24},{9,1... | collective-permute-start | bytes 196616 | tf_op jit(solution)/shard_map/ppermute | solution.py:327
  40.9 4.7 %collective-permute-start.9 = (bf16[96,512]{1,0:T(8,128)(2,1)S(1)}, bf16[96,512]{1,0:T(8,128)(2,1)S(1)}, u32[]{:S(2)}, u32[]{:S(2)}) collective-permute-start(bf16[96,512]{1,0:T(8,128)(2,1)S(1)} %shard_map.86.pay), channel_id=1, source_target_pairs={{0,8},{1,3},{2,10},{3,1},{4,12},{5,7},{6,14},{7,5},{8,0},{9,11},{1... | collective-permute-start | bytes 294920 | tf_op jit(solution)/shard_map/ppermute | solution.py:327
  45.6 5.4 %collective-permute-start.10 = (bf16[160,512]{1,0:T(8,128)(2,1)S(1)}, bf16[160,512]{1,0:T(8,128)(2,1)S(1)}, u32[]{:S(2)}, u32[]{:S(2)}) collective-permute-start(bf16[160,512]{1,0:T(8,128)(2,1)S(1)} %shard_map.87.pay), channel_id=1, source_target_pairs={{0,2},{1,5},{2,0},{3,7},{4,6},{5,1},{6,4},{7,3},{8,10},{9,13},{10,... | collective-permute-start | bytes 491528 | tf_op jit(solution)/shard_map/ppermute | solution.py:327
  51.0 3.2 %collective-permute-start.11 = (bf16[288,512]{1,0:T(8,128)(2,1)S(1)}, bf16[288,512]{1,0:T(8,128)(2,1)S(1)}, u32[]{:S(2)}, u32[]{:S(2)}) collective-permute-start(bf16[288,512]{1,0:T(8,128)(2,1)S(1)} %shard_map.88.pay), channel_id=1, source_target_pairs={{0,1},{1,0},{2,3},{3,2},{4,5},{5,4},{6,7},{7,6},{8,9},{9,8},{10,11... | collective-permute-start | bytes 884744 | tf_op jit(solution)/shard_map/ppermute | solution.py:327

commit v3 on v2

--- a/solution.py
+++ b/solution.py
@@ -13,6 +13,7 @@
 BF16 = jnp.bfloat16
 BOTH = ("site", "mode")
 LANES = 128
+PIECES = 5
 
 
 def dot_nn(a, b):
@@ -54,50 +55,78 @@
     return pl.ds(pl.multiple_of(index * count, count), count)
 
 
-def call(kernel, outs, *args, scratch=(), flops=10**8, moved=2 * 10**6, smem=()):
+def call(kernel, outs, *args, scratch=(), flops=10**8, moved=2 * 10**6, smem=(), far=(), out_far=False):
     vmem = pl.BlockSpec(memory_space=pltpu.VMEM)
     scalars = pl.BlockSpec(memory_space=pltpu.SMEM)
+    distant = pl.BlockSpec(memory_space=pltpu.HBM)
     return pl.pallas_call(
         kernel,
         out_shape=outs,
-        in_specs=[scalars if i in smem else vmem for i in range(len(args))],
-        out_specs=jax.tree.map(lambda _: vmem, outs),
+        in_specs=[scalars if i in smem else distant if i in far else vmem for i in range(len(args))],
+        out_specs=jax.tree.map(lambda _: pl.BlockSpec(memory_space=pl.ANY) if out_far else vmem, outs),
         scratch_shapes=scratch,
         compiler_params=pltpu.CompilerParams(vmem_limit_bytes=16 * 2**20),
         cost_estimate=pl.CostEstimate(flops=flops, bytes_accessed=moved, transcendentals=0),
     )(*args)
 
 
+def stay(x):
+    return pltpu.with_memory_space_constraint(x, pltpu.HBM)
+
+
 def shaped(rows, cols, dtype):
     return jax.ShapeDtypeStruct((rows, cols), dtype)
 
 
-def first_kernel(nb, basis, images, pay):
+def open_kernel(nb, spots, basis_far, images_far, pay, basis, images, shift, sems):
     rows, nvec = basis.shape
     old = images.shape[1]
     blk = nvec - old
+    step = rows // PIECES
+    copies = []
+    for j, (far, here) in enumerate(((basis_far, basis), (images_far, images))):
+        for i in range(PIECES):
+            span = pl.ds(i * step, step)
+            copies.append(pltpu.make_async_copy(far.at[span], here.at[span], sems.at[j * PIECES + i]))
+    for copy in copies:
+        copy.start()
     core = place()[0]
     top = nvec // 2
-    keep = basis[:, pl.ds(pl.multiple_of((1 - core) * top, top), top)]
-    part = dot_tn(keep, images[...])
-    high, low = split(part)
-    pay[:top, :old] = high
-    pay[:top, old:] = jnp.zeros((top, blk), BF16)
-    pay[top : 2 * top, :old] = low
-    pay[top : 2 * top, old:] = jnp.zeros((top, blk), BF16)
     wide = nb * blk
-    last = basis[:, nvec - LANES :]
+    share = shift.shape[0] // spots
+    shift[...] = onehot(
+        shift.shape,
+        lambda r, c: (lax.rem(c, LANES) < share) & (lax.div(c, LANES) * share + lax.rem(c, LANES) == r),
+    )
+    gather = onehot((LANES, rows), lambda r, c: lax.div(c, nb) == r)
     spread = onehot((LANES, wide), lambda r, c: r - (LANES - blk) == lax.rem(c, blk))
-    tiled = dot_nn(last, spread)
+    for copy in copies[:PIECES]:
+        copy.wait()
+    tiled = dot_nn(basis[:, nvec - LANES :], spread)
     row = lax.broadcasted_iota(jnp.int32, (rows, wide), 0)
     col = lax.broadcasted_iota(jnp.int32, (rows, wide), 1)
     tiled = jnp.where(lax.rem(row, nb) == lax.div(col, blk), tiled, 0.0).astype(BF16)
-    gather = onehot((LANES, rows), lambda r, c: lax.div(c, nb) == r)
     merged = dot_nn(gather, tiled).astype(BF16)
     groups = nvec // LANES
     each = LANES // groups
     for g in range(groups):
         pay[2 * top :, g * LANES : (g + 1) * LANES] = merged[g * each : (g + 1) * each]
+    for copy in copies[PIECES:]:
+        copy.wait()
+    give = basis[:, pl.ds(pl.multiple_of((1 - core) * top, top), top)]
+    high, low = split(dot_tn(give, images[...]))
+    pay[:top, :old] = high
+    pay[:top, old:] = jnp.zeros((top, blk), BF16)
+    pay[top : 2 * top, :old] = low
+    pay[top : 2 * top, old:] = jnp.zeros((top, blk), BF16)
+
+
+def fetch_kernel(order, far, near, sems):
+    copies = [pltpu.make_async_copy(far.at[hop], near.at[i], sems.at[i]) for i, hop in enumerate(order)]
+    for copy in copies:
+        copy.start()
+    for copy in copies:
+        copy.wait()
 
 
 def keep_kernel(basis, images, kept):
@@ -110,8 +139,21 @@
     kept[:, old:] = jnp.zeros((top, nvec - old), F32)
 
 
-def rotate_kernel(basis, rotation, out):
-    out[...] = dot_nn(basis[...], rotation[...]).astype(BF16)
+def put(far, held, sems, pieces, work):
+    step = held.shape[0] // pieces
+    copies = []
+    for i in range(pieces):
+        span = pl.ds(i * step, step)
+        held[span, :] = work(span)
+        copy = pltpu.make_async_copy(held.at[span], far.at[span], sems.at[i])
+        copy.start()
+        copies.append(copy)
+    for copy in copies:
+        copy.wait()
+
+
+def rotate_kernel(basis, rotation, far, held, sems):
+    put(far, held, sems, PIECES, lambda span: dot_nn(basis[span, :], rotation[...]).astype(BF16))
 
 
 def joined(kept, got, start, count):
@@ -150,10 +192,10 @@
 
 
 def fourth_kernel(kept, got, far, out, rest, cross):
-    core, _, _, z0, z1 = place()
+    core, _, y, _, z1 = place()
     whole = kept.shape[0]
     n = whole // 2
-    bit = pick(core, z1, z0)
+    bit = pick(core, y, z1)
     out[:n, :], out[n:, :] = split(joined(kept, got, (1 - bit) * n, n))
     rest[...] = joined(kept, got, bit * n, n)
     area = got.shape[0] - 2 * whole
@@ -161,27 +203,20 @@
     cross[area:, :] = far[...]
 
 
-def setup_kernel(near, nb, blk, spots, table, perms, shift):
+def setup_kernel(near, nb, blk, table, perms):
     hops = perms.shape[0]
     wide = nb * blk
-    coarse = shift.shape[0]
-    share = coarse // spots
     row = lax.broadcasted_iota(jnp.int32, (2 * wide, wide), 0)
-    col = lax.broadcasted_iota(jnp.int32, (2 * wide, wide), 1)
+    col = lax.broadcasted_iota(jnp.int32, (1, wide), 1)
     for hop in range(hops):
-        wanted = lax.rem(col, blk)
-        for b in range(nb):
-            entry = table[b, hop]
-            q = lax.rem(entry, nb)
-            base = q * blk
+        wanted = col if hop == 0 else lax.rem(col, blk)
+        for b in range(nb if hop else 0):
+            entry = table[b, hop - 1]
+            base = lax.rem(entry, nb) * blk
             if hop not in near:
                 base = base + jnp.where(entry >= nb, wide, 0)
             wanted = wanted + jnp.where(lax.div(col, blk) == b, base, 0)
         perms[hop] = jnp.where(row == wanted, 1.0, 0.0).astype(BF16)
-    shift[...] = onehot(
-        (coarse, spots * LANES),
-        lambda r, c: (lax.rem(c, LANES) < share) & (lax.div(c, LANES) * share + lax.rem(c, LANES) == r),
-    )
 
 
 def stack(ref, at, piece):
@@ -209,9 +244,9 @@
     step = rows // 2
     for r in range(2):
         span = pl.ds(r * step, step)
-        part = dot_nn(hops[order[0], span, :], mixed[0])
+        part = dot_nn(hops[0, span, :], mixed[0])
         for i in range(1, len(order)):
-            part = part + dot_nn(hops[order[i], span, :], mixed[i])
+            part = part + dot_nn(hops[i, span, :], mixed[i])
         total[span, :] = part
 
 
@@ -241,16 +276,15 @@
         sites[7 + k] = ref[...]
     order = sorted(sites)
     mixed = [
-        (dot_nn(own[...], perms[hop, :wide, :]) + dot_nn(sites[hop], perms[hop, wide:, :])).astype(BF16)
-        for hop in order
+        dot_nn(jnp.concatenate([own[...], sites[hop]], axis=1), perms[hop]).astype(BF16) for hop in order
     ]
     step = rows // 2
     sums = jnp.zeros((wide, nvec), F32)
     for r in range(2):
         span = pl.ds(r * step, step)
         part = total[span, :]
-        for i, hop in enumerate(order):
-            part = part + dot_nn(hops[hop, span, :], mixed[i])
+        for i in range(len(order)):
+            part = part + dot_nn(hops[i, span, :], mixed[i])
         row = lax.broadcasted_iota(jnp.int32, (step, wide), 0)
         col = lax.broadcasted_iota(jnp.int32, (step, wide), 1)
         chosen = jnp.where(lax.rem(row, nb) == lax.div(col, blk), part, 0.0).astype(BF16)
@@ -269,11 +303,17 @@
     out[2 * n :, :] = new[...]
 
 
-def turn_kernel(nb, images, masked, rotation, out):
+def turn_kernel(nb, images, masked, rotation, far, held, sems):
     old = images.shape[1]
     tail = rotation[old:, :]
     deep = jnp.concatenate([tail] * nb, axis=0)
-    out[...] = (dot_nn(images[...], rotation[:old, :]) + dot_nn(masked[...], deep)).astype(BF16)
+    put(
+        far,
+        held,
+        sems,
+        PIECES,
+        lambda span: (dot_nn(images[span, :], rotation[:old, :]) + dot_nn(masked[span, :], deep)).astype(BF16),
+    )
 
 
 def value(ref, start, count):
@@ -297,16 +337,29 @@
     out[2 * n : 2 * n + blk, :], out[2 * n + blk :, :] = split(value(pay, n, blk) + value(got, n, blk))
 
 
-def final_kernel(n, blk, scale, pay, got, out):
-    nvec = out.shape[1]
+def final_kernel(n, blk, scale, pay, got, far, held, sems):
+    nvec = far.shape[1]
     core = place()[0]
-    out[rows_at(core, n), :] = pay[:n, :].astype(F32)
-    out[rows_at(1 - core, n), :] = got[:n, :].astype(F32)
     new = (value(pay, n, blk) + value(got, n, blk)) * scale
     tall = jnp.concatenate([jnp.zeros((LANES - blk, nvec), F32), new], axis=0)
-    flipped = tall.T
-    lane = lax.broadcasted_iota(jnp.int32, (nvec, LANES), 1)
-    out[:, nvec - LANES :] = jnp.where(lane < LANES - blk, out[:, nvec - LANES :], flipped)
+    held[:, nvec - LANES :] = tall.T
+    step = n // 2
+    lane = lax.broadcasted_iota(jnp.int32, (step, LANES), 1)
+    copies = []
+    for i in range(4):
+        side = core if i < 2 else 1 - core
+        source = pay if i < 2 else got
+        part = source[(i % 2) * step : (i % 2 + 1) * step, :].astype(F32)
+        span = pl.ds(pl.multiple_of(side * n + (i % 2) * step, step), step)
+        held[span, : nvec - LANES] = part[:, : nvec - LANES]
+        held[span, nvec - LANES :] = jnp.where(
+            lane < LANES - blk, part[:, nvec - LANES :], held[span, nvec - LANES :]
+        )
+        copy = pltpu.make_async_copy(held.at[span], far.at[span], sems.at[i])
+        copy.start()
+        copies.append(copy)
+    for copy in copies:
+        copy.wait()
 
 
 def program(basis, images, hops, neighbours, rotation):
@@ -331,15 +384,43 @@
     flat_basis = jnp.transpose(basis, (1, 0, 2)).reshape(rows, nvec)
     flat_images = jnp.transpose(images, (1, 0, 2)).reshape(rows, old)
     flat_hops = jnp.transpose(hops, (1, 2, 0, 3)).reshape(hops.shape[1], rows, coarse)
-    own_rows = jnp.arange(nb, dtype=jnp.int32)
-    table = jnp.concatenate([own_rows[:, None], neighbours], axis=1)
-    near_order = [0] if sites > 8 else [0, 7, 8]
-
     half = nvec // 2
     n = half // 8
-    pay0 = call(functools.partial(first_kernel, nb), shaped(nvec + chunk, nvec, BF16), flat_basis, flat_images)
+    pay0, basis_here, images_here, shift = call(
+        functools.partial(open_kernel, nb, spots),
+        (
+            shaped(nvec + chunk, nvec, BF16),
+            shaped(rows, nvec, BF16),
+            shaped(rows, old, BF16),
+            shaped(coarse, spots * LANES, BF16),
+        ),
+        stay(flat_basis),
+        stay(flat_images),
+        far=(0, 1),
+        scratch=[pltpu.SemaphoreType.DMA((2 * PIECES,))],
+    )
     got0 = send(pay0, core_hop, core_hop)
-    kept0 = call(keep_kernel, shaped(half, nvec, F32), flat_basis, flat_images)
+    kept0 = call(keep_kernel, shaped(half, nvec, F32), basis_here, images_here)
+    near_order = [0] if sites > 8 else [0, 7, 8]
+    far_order = [hop for hop in range(hops.shape[1]) if hop not in near_order]
+
+    def fetched(order):
+        return call(
+            functools.partial(fetch_kernel, order),
+            jax.ShapeDtypeStruct((len(order), rows, coarse), BF16),
+            stay(flat_hops),
+            far=(0,),
+            scratch=[pltpu.SemaphoreType.DMA((len(order),))],
+        )
+
+    far_hops = fetched(far_order)
+    near_hops = fetched(near_order)
+    perms = call(
+        functools.partial(setup_kernel, near_order, nb, blk),
+        jax.ShapeDtypeStruct((hops.shape[1], 2 * wide, wide), BF16),
+        neighbours,
+        smem=(0,),
+    )
     pay1, kept1, pair = call(
         second_kernel,
         (shaped(half + 2 * chunk, nvec, BF16), shaped(half // 2, nvec, F32), shaped(2 * chunk, nvec, BF16)),
@@ -349,16 +430,6 @@
     )
     got1 = send(pay1, x_hop, y_hop)
     far = send(pair, 0, z1_hop)
-    perms, shift = call(
-        functools.partial(setup_kernel, near_order, nb, blk, spots),
-        (
-            jax.ShapeDtypeStruct((hops.shape[1], 2 * wide, wide), BF16),
-            shaped(coarse, spots * LANES, BF16),
-        ),
-        table,
-        smem=(0,),
-    )
-    turned_basis = call(rotate_kernel, shaped(rows, nvec, BF16), flat_basis, rotation)
     pay2, kept2 = call(
         third_kernel,
         (shaped(half // 2 + 4 * chunk, nvec, BF16), shaped(half // 4, nvec, F32)),
@@ -375,7 +446,7 @@
         pair,
         got1,
         crossed,
-        flat_hops,
+        near_hops,
         perms,
         shift,
         scratch=[pltpu.VMEM((spots * LANES, wide), BF16)],
@@ -392,7 +463,7 @@
         far,
     )
     cross = send(cross_pay, core_hop, core_hop)
-    got3 = send(pay3, z1_hop, z0_hop)
+    got3 = send(pay3, y_hop, z1_hop)
     masked, new = call(
         functools.partial(far_kernel, nb, blk),
         (shaped(rows, wide, BF16), shaped(2 * blk, nvec, BF16)),
@@ -403,16 +474,25 @@
         got1,
         crossed,
         total,
-        flat_basis,
-        flat_hops,
+        basis_here,
+        far_hops,
         perms,
         shift,
         *times,
         scratch=[pltpu.VMEM((3, spots * LANES, wide), BF16)],
     )
     payc = call(join_kernel, shaped(2 * n + 2 * blk, nvec, BF16), kept3, got3, new)
-    gotc = send(payc, y_hop, z1_hop)
-    turned_images = call(functools.partial(turn_kernel, nb), shaped(rows, nvec, BF16), flat_images, masked, rotation)
+    turned = [pltpu.VMEM((rows, nvec), BF16), pltpu.SemaphoreType.DMA((PIECES,))]
+    gotc = send(payc, z1_hop, z0_hop)
+    turned_images = call(
+        functools.partial(turn_kernel, nb),
+        shaped(rows, nvec, BF16),
+        images_here,
+        masked,
+        rotation,
+        out_far=True,
+        scratch=turned,
+    )
     hop = 8 * spots
     while hop < count:
         payc = call(functools.partial(extra_kernel, n, blk), shaped(2 * n + 2 * blk, nvec, BF16), payc, gotc)
@@ -420,9 +500,12 @@
         hop *= 2
     payc = call(functools.partial(settle_kernel, n, blk, scale), shaped(n + 2 * blk, nvec, BF16), payc, gotc)
     steps = (
-        (z1_hop, z0_hop, lambda core, half, y, z0, z1: pick(core, z1, z0)),
+        (y_hop, z1_hop, lambda core, half, y, z0, z1: pick(core, y, z1)),
         (z0_hop, x_hop, lambda core, half, y, z0, z1: pick(core, z0, half)),
         (x_hop, y_hop, lambda core, half, y, z0, z1: pick(core, half, y)),
+    )
+    turned_basis = call(
+        rotate_kernel, shaped(rows, nvec, BF16), basis_here, rotation, out_far=True, scratch=turned
     )
     for first, second, chooser in steps:
         gotc = send(payc, first, second)
@@ -431,7 +514,14 @@
         )
         n *= 2
     gotc = send(payc, core_hop, core_hop)
-    projected = call(functools.partial(final_kernel, n, blk, scale), shaped(nvec, nvec, F32), payc, gotc)
+    projected = call(
+        functools.partial(final_kernel, n, blk, scale),
+        shaped(nvec, nvec, F32),
+        payc,
+        gotc,
+        out_far=True,
+        scratch=[pltpu.VMEM((nvec, nvec), F32), pltpu.SemaphoreType.DMA((4,))],
+    )
 
     def back(x):
         return jnp.transpose(x.reshape(modes_here, nb, nvec), (1, 0, 2))

time: 55.6 us -> 57.3 us (1.031)
  Pallas kernels: 11.3 us -> 16 us
  local copies, waits for them, and re-layouts: 2.69 us -> 0.02 us
  waiting for transfers between devices: 25 us -> 22.9 us
  starting transfers between devices: 14.8 us -> 16.8 us
  other arithmetic: 0.76 us -> 0 us
    pallas_call x16 -> x18, Pallas kernels: 11.3 us -> 16 us  [call(): pl.pallas_call(kernel, out_shape=outs, in_specs=[scalars if i in smem els...]
    unnamed x12 -> x4, local copies, waits for them, and re-layouts: 2.68 us -> 0.01 us
    ppermute x12, waiting for transfers between devices: 25 us -> 22.9 us  [send(): return lax.ppermute(x, BOTH, pairs)]
    ppermute x12, starting transfers between devices: 14.8 us -> 16.8 us  [send(): return lax.ppermute(x, BOTH, pairs)]
    concatenate x1 -> x0, other arithmetic: 0.76 us -> none  [program(): table = jnp.concatenate([own_rows[:, None], neighbours], axis=1)]
  transfers between devices with their start and end apart: 12 -> 12, of which waited for: 7 -> 7; matrix products, arithmetic and copies ran while one was open for 1% -> 0% of each run, Pallas kernels for 16% -> 21%
where the time goes in v3:
time: 57.3 us; the launch traced here: 56.7 us
  waiting for transfers between devices  22.9 us (40%)
  starting transfers between devices  16.8 us (29%)
  Pallas kernels  16 us (28%)
  between operations  0.84 us (1%)
    ppermute x12, waiting for transfers between devices, send(): return lax.ppermute(x, BOTH, pairs)  22.9 us
    ppermute x12, starting transfers between devices, send(): return lax.ppermute(x, BOTH, pairs)  16.8 us
    pallas_call x18, Pallas kernels, call(): pl.pallas_call(kernel, out_shape=outs, in_specs=[scalars if i in smem els...  16 us
  transfers between devices with their start and end apart: 12, of which 7 were waited for; matrix products, arithmetic and copies ran while one was open for 0% of the time, Pallas kernels for 21%

profile of v3, /device:TPU:0, one launch (start us, length us, event | category | flops | bytes accessed | tf_op | source)
XLA Modules:
  0.0 56.7 jit_solution(5562346685122074822)
XLA Ops:
  0.6 2.2 %shard_map.76 = (bf16[544,512]{1,0:T(8,128)(2,1)S(1)}, bf16[800,512]{1,0:T(8,128)(2,1)S(1)}, bf16[800,496]{1,0:T(8,128)(2,1)S(1)}, bf16[400,512]{1,0:T(8,128)(2,1)S(1)}) custom-call(bf16[800,512]{1,0:T(8,128)(2,1)} %bitcast.17, bf16[800,496]{1,0:T(8,128)(2,1)} %bitcast.18), custom_call_target="tpu_custom_call" | custom-call | flops 100000000 | bytes 2000000 | tf_op jit(solution)/shard_map/pallas_call | solution.py:62
  2.9 0.5 collective-permute-start
  3.4 0.5 shard_map.77.kept
  3.9 1.1 %collective-permute-done.got = bf16[544,512]{1,0:T(8,128)(2,1)S(1)} collective-permute-done((bf16[544,512]{1,0:T(8,128)(2,1)S(1)}, bf16[544,512]{1,0:T(8,128)(2,1)S(1)}, u32[]{:S(2)}, u32[]{:S(2)}) %collective-permute-start) | collective-permute-done | bytes 557088 | tf_op jit(solution)/shard_map/ppermute | solution.py:380
  5.0 0.2 shard_map.78
  5.2 2.9 %collective-permute-start.1 = (bf16[320,512]{1,0:T(8,128)(2,1)S(1)}, bf16[320,512]{1,0:T(8,128)(2,1)S(1)}, u32[]{:S(2)}, u32[]{:S(2)}) collective-permute-start(bf16[320,512]{1,0:T(8,128)(2,1)S(1)} %get-tuple-element.23), channel_id=1, source_target_pairs={{0,2},{1,5},{2,0},{3,7},{4,6},{5,1},{6,4},{7,3},{8,10},{9,13},{10,... | collective-permute-start | bytes 983048 | tf_op jit(solution)/shard_map/ppermute | solution.py:380
  8.1 0.7 %collective-permute-start.2 = (bf16[64,512]{1,0:T(8,128)(2,1)S(1)}, bf16[64,512]{1,0:T(8,128)(2,1)S(1)}, u32[]{:S(2)}, u32[]{:S(2)}) collective-permute-start(bf16[64,512]{1,0:T(8,128)(2,1)S(1)} %get-tuple-element.24.pair), channel_id=1, source_target_pairs={{1,17},{3,19},{5,21},{7,23},{9,25},{11,27},{13,29},{15,31},{17,1},... | collective-permute-start | bytes 196616 | tf_op jit(solution)/shard_map/ppermute | solution.py:380
  8.8 4.4 %collective-permute-done.1.got.got1 = bf16[320,512]{1,0:T(8,128)(2,1)S(1)} collective-permute-done((bf16[320,512]{1,0:T(8,128)(2,1)S(1)}, bf16[320,512]{1,0:T(8,128)(2,1)S(1)}, u32[]{:S(2)}, u32[]{:S(2)}) %collective-permute-start.1) | collective-permute-done | bytes 327712 | tf_op jit(solution)/shard_map/ppermute | solution.py:380
  13.1 0.1 shard_map.79
  13.2 2.2 %collective-permute-start.3 = (bf16[256,512]{1,0:T(8,128)(2,1)S(1)}, bf16[256,512]{1,0:T(8,128)(2,1)S(1)}, u32[]{:S(2)}, u32[]{:S(2)}) collective-permute-start(bf16[256,512]{1,0:T(8,128)(2,1)S(1)} %get-tuple-element.26), channel_id=1, source_target_pairs={{0,8},{1,3},{2,10},{3,1},{4,12},{5,7},{6,14},{7,5},{8,0},{9,11},{1... | collective-permute-start | bytes 786440 | tf_op jit(solution)/shard_map/ppermute | solution.py:380
  15.4 4.4 %collective-permute-done.3.got.got2 = bf16[256,512]{1,0:T(8,128)(2,1)S(1)} collective-permute-done((bf16[256,512]{1,0:T(8,128)(2,1)S(1)}, bf16[256,512]{1,0:T(8,128)(2,1)S(1)}, u32[]{:S(2)}, u32[]{:S(2)}) %collective-permute-start.3) | collective-permute-done | bytes 262176 | tf_op jit(solution)/shard_map/ppermute | solution.py:380
  19.8 0.1 collective-permute-start.6
  19.9 0.5 collective-permute-start.5
  20.4 2.0 %collective-permute-start.4 = (bf16[64,512]{1,0:T(8,128)(2,1)S(1)}, bf16[64,512]{1,0:T(8,128)(2,1)S(1)}, u32[]{:S(2)}, u32[]{:S(2)}) collective-permute-start(bf16[64,512]{1,0:T(8,128)(2,1)S(1)} %get-tuple-element.28), channel_id=1, source_target_pairs={{0,4},{1,17},{2,6},{3,19},{4,0},{5,21},{6,2},{7,23},{8,12},{9,25},... | collective-permute-start | bytes 196616 | tf_op jit(solution)/shard_map/ppermute | solution.py:380
  22.4 1.7 %shard_map.81.hops = bf16[3,800,400]{2,1,0:T(8,128)(2,1)S(1)} custom-call(bf16[9,800,400]{2,1,0:T(8,128)(2,1)} %bitcast.15), custom_call_target="tpu_custom_call" | custom-call | flops 100000000 | bytes 2000000 | tf_op jit(solution)/shard_map/pallas_call | solution.py:62
  24.0 2.4 %shard_map.84.hops = bf16[6,800,400]{2,1,0:T(8,128)(2,1)S(1)} custom-call(bf16[9,800,400]{2,1,0:T(8,128)(2,1)} %bitcast.16), custom_call_target="tpu_custom_call" | custom-call | flops 100000000 | bytes 2000000 | tf_op jit(solution)/shard_map/pallas_call | solution.py:62
  26.5 0.8 %shard_map.82.perms = bf16[9,256,128]{2,1,0:T(8,128)(2,1)S(1)} custom-call(s32[8,8]{1,0:T(8,128)S(1)} %copy-done.1), custom_call_target="tpu_custom_call" | custom-call | flops 100000000 | bytes 2000000 | tf_op jit(solution)/shard_map/pallas_call | solution.py:62
  27.3 1.3 %shard_map.83 = (f32[800,128]{1,0:T(8,128)S(1)}, bf16[400,128]{1,0:T(8,128)(2,1)S(1)}) custom-call(bf16[64,512]{1,0:T(8,128)(2,1)S(1)} %get-tuple-element.24.pair, bf16[320,512]{1,0:T(8,128)(2,1)S(1)} %collective-permute-done.1.got.got1, bf16[64,512]{1,0:T(8,128)(2,1)S(1)} %collective-permute-done.5.crossed, bf16[3,800,400]{2,1,0:T(8,128)(2,1)S(1)} %shard_map.81.hops, ...), custom_call_target="tpu_custom_call" | custom-call | flops 100000000 | bytes 2000000 | tf_op jit(solution)/shard_map/pallas_call | solution.py:62
  28.7 2.6 %shard_map.85 = (bf16[800,128]{1,0:T(8,128)(2,1)S(1)}, bf16[32,512]{1,0:T(8,128)(2,1)S(1)}) custom-call(bf16[400,128]{1,0:T(8,128)(2,1)S(1)} %get-tuple-element.30.own, bf16[256,512]{1,0:T(8,128)(2,1)S(1)} %collective-permute-done.3.got.got2, bf16[192,512]{1,0:T(8,128)(2,1)S(1)} %collective-permute-done.6.cross, ...), custom_call_target="tpu_custom_call" | custom-call | flops 100000000 | bytes 2000000 | tf_op jit(solution)/shard_map/pallas_call | solution.py:62
  31.3 0.0 collective-permute-done.4.got
  31.4 2.7 %collective-permute-start.7 = (bf16[96,512]{1,0:T(8,128)(2,1)S(1)}, bf16[96,512]{1,0:T(8,128)(2,1)S(1)}, u32[]{:S(2)}, u32[]{:S(2)}) collective-permute-start(bf16[96,512]{1,0:T(8,128)(2,1)S(1)} %shard_map.86.pay), channel_id=1, source_target_pairs={{0,16},{1,9},{2,18},{3,11},{4,20},{5,13},{6,22},{7,15},{8,24},{9,1... | collective-permute-start | bytes 294920 | tf_op jit(solution)/shard_map/ppermute | solution.py:380
  34.0 3.0 %collective-permute-done.7.got = bf16[96,512]{1,0:T(8,128)(2,1)S(1)} collective-permute-done((bf16[96,512]{1,0:T(8,128)(2,1)S(1)}, bf16[96,512]{1,0:T(8,128)(2,1)S(1)}, u32[]{:S(2)}, u32[]{:S(2)}) %collective-permute-start.7) | collective-permute-done | bytes 98336 | tf_op jit(solution)/shard_map/ppermute | solution.py:380
  37.1 0.7 %collective-permute-start.8 = (bf16[64,512]{1,0:T(8,128)(2,1)S(1)}, bf16[64,512]{1,0:T(8,128)(2,1)S(1)}, u32[]{:S(2)}, u32[]{:S(2)}) collective-permute-start(bf16[64,512]{1,0:T(8,128)(2,1)S(1)} %shard_map.87.pay), channel_id=1, source_target_pairs={{0,4},{1,17},{2,6},{3,19},{4,0},{5,21},{6,2},{7,23},{8,12},{9,25},... | collective-permute-start | bytes 196616 | tf_op jit(solution)/shard_map/ppermute | solution.py:380
  37.7 3.7 %collective-permute-done.8.got = bf16[64,512]{1,0:T(8,128)(2,1)S(1)} collective-permute-done((bf16[64,512]{1,0:T(8,128)(2,1)S(1)}, bf16[64,512]{1,0:T(8,128)(2,1)S(1)}, u32[]{:S(2)}, u32[]{:S(2)}) %collective-permute-start.8) | collective-permute-done | bytes 65568 | tf_op jit(solution)/shard_map/ppermute | solution.py:380
  41.4 3.1 %collective-permute-start.9 = (bf16[96,512]{1,0:T(8,128)(2,1)S(1)}, bf16[96,512]{1,0:T(8,128)(2,1)S(1)}, u32[]{:S(2)}, u32[]{:S(2)}) collective-permute-start(bf16[96,512]{1,0:T(8,128)(2,1)S(1)} %shard_map.88.pay), channel_id=1, source_target_pairs={{0,8},{1,3},{2,10},{3,1},{4,12},{5,7},{6,14},{7,5},{8,0},{9,11},{1... | collective-permute-start | bytes 294920 | tf_op jit(solution)/shard_map/ppermute | solution.py:380
  44.5 2.6 %collective-permute-done.9.got = bf16[96,512]{1,0:T(8,128)(2,1)S(1)} collective-permute-done((bf16[96,512]{1,0:T(8,128)(2,1)S(1)}, bf16[96,512]{1,0:T(8,128)(2,1)S(1)}, u32[]{:S(2)}, u32[]{:S(2)}) %collective-permute-start.9) | collective-permute-done | bytes 98336 | tf_op jit(solution)/shard_map/ppermute | solution.py:380
  47.1 1.6 %collective-permute-start.10 = (bf16[160,512]{1,0:T(8,128)(2,1)S(1)}, bf16[160,512]{1,0:T(8,128)(2,1)S(1)}, u32[]{:S(2)}, u32[]{:S(2)}) collective-permute-start(bf16[160,512]{1,0:T(8,128)(2,1)S(1)} %shard_map.89.pay), channel_id=1, source_target_pairs={{0,2},{1,5},{2,0},{3,7},{4,6},{5,1},{6,4},{7,3},{8,10},{9,13},{10,... | collective-permute-start | bytes 491528 | tf_op jit(solution)/shard_map/ppermute | solution.py:380
  48.7 3.8 %collective-permute-done.10.got = bf16[160,512]{1,0:T(8,128)(2,1)S(1)} collective-permute-done((bf16[160,512]{1,0:T(8,128)(2,1)S(1)}, bf16[160,512]{1,0:T(8,128)(2,1)S(1)}, u32[]{:S(2)}, u32[]{:S(2)}) %collective-permute-start.10) | collective-permute-done | bytes 163872 | tf_op jit(solution)/shard_map/ppermute | solution.py:380
  52.5 0.1 collective-permute-start.11
  52.6 1.3 %shard_map.92 = bf16[800,512]{1,0:T(8,128)(2,1)} custom-call(bf16[800,512]{1,0:T(8,128)(2,1)S(1)} %get-tuple-element.19.basis, bf16[512,512]{1,0:T(8,128)(2,1)S(1)} %copy-done), custom_call_target="tpu_custom_call" | custom-call | flops 100000000 | bytes 2000000 | tf_op jit(solution)/shard_map/pallas_call | solution.py:62
  54.0 1.5 %shard_map.93 = bf16[800,512]{1,0:T(8,128)(2,1)} custom-call(bf16[800,496]{1,0:T(8,128)(2,1)S(1)} %get-tuple-element.20.images, bf16[800,128]{1,0:T(8,128)(2,1)S(1)} %get-tuple-element.34.masked, bf16[512,512]{1,0:T(8,128)(2,1)S(1)} %copy-done), custom_call_target="tpu_custom_call" | custom-call | flops 100000000 | bytes 2000000 | tf_op jit(solution)/shard_map/pallas_call | solution.py:62
  55.5 1.2 %shard_map.91 = f32[512,512]{1,0:T(8,128)} custom-call(bf16[288,512]{1,0:T(8,128)(2,1)S(1)} %shard_map.90.pay, bf16[288,512]{1,0:T(8,128)(2,1)S(1)} %collective-permute-done.11.got), custom_call_target="tpu_custom_call" | custom-call | flops 100000000 | bytes 2000000 | tf_op jit(solution)/shard_map/pallas_call | solution.py:62
  (15 shorter events, 0.2 us)
Async XLA Ops:
  2.9 2.1 %collective-permute-start = (bf16[544,512]{1,0:T(8,128)(2,1)S(1)}, bf16[544,512]{1,0:T(8,128)(2,1)S(1)}, u32[]{:S(2)}, u32[]{:S(2)}) collective-permute-start(bf16[544,512]{1,0:T(8,128)(2,1)S(1)} %get-tuple-element.21.pay), channel_id=1, source_target_pairs={{0,1},{1,0},{2,3},{3,2},{4,5},{5,4},{6,7},{7,6},{8,9},{9,8},{10,11... | collective-permute-start | bytes 1671176 | tf_op jit(solution)/shard_map/ppermute | solution.py:380
  5.2 8.0 %collective-permute-start.1 = (bf16[320,512]{1,0:T(8,128)(2,1)S(1)}, bf16[320,512]{1,0:T(8,128)(2,1)S(1)}, u32[]{:S(2)}, u32[]{:S(2)}) collective-permute-start(bf16[320,512]{1,0:T(8,128)(2,1)S(1)} %get-tuple-element.23), channel_id=1, source_target_pairs={{0,2},{1,5},{2,0},{3,7},{4,6},{5,1},{6,4},{7,3},{8,10},{9,13},{10,... | collective-permute-start | bytes 983048 | tf_op jit(solution)/shard_map/ppermute | solution.py:380
  8.1 0.7 %collective-permute-start.2 = (bf16[64,512]{1,0:T(8,128)(2,1)S(1)}, bf16[64,512]{1,0:T(8,128)(2,1)S(1)}, u32[]{:S(2)}, u32[]{:S(2)}) collective-permute-start(bf16[64,512]{1,0:T(8,128)(2,1)S(1)} %get-tuple-element.24.pair), channel_id=1, source_target_pairs={{1,17},{3,19},{5,21},{7,23},{9,25},{11,27},{13,29},{15,31},{17,1},... | collective-permute-start | bytes 196616 | tf_op jit(solution)/shard_map/ppermute | solution.py:380
  13.2 6.5 %collective-permute-start.3 = (bf16[256,512]{1,0:T(8,128)(2,1)S(1)}, bf16[256,512]{1,0:T(8,128)(2,1)S(1)}, u32[]{:S(2)}, u32[]{:S(2)}) collective-permute-start(bf16[256,512]{1,0:T(8,128)(2,1)S(1)} %get-tuple-element.26), channel_id=1, source_target_pairs={{0,8},{1,3},{2,10},{3,1},{4,12},{5,7},{6,14},{7,5},{8,0},{9,11},{1... | collective-permute-start | bytes 786440 | tf_op jit(solution)/shard_map/ppermute | solution.py:380
  19.8 8.9 %collective-permute-start.6 = (bf16[192,512]{1,0:T(8,128)(2,1)S(1)}, bf16[192,512]{1,0:T(8,128)(2,1)S(1)}, u32[]{:S(2)}, u32[]{:S(2)}) collective-permute-start(bf16[192,512]{1,0:T(8,128)(2,1)S(1)} %get-tuple-element.31), channel_id=1, source_target_pairs={{0,1},{1,0},{2,3},{3,2},{4,5},{5,4},{6,7},{7,6},{8,9},{9,8},{10,11... | collective-permute-start | bytes 589832 | tf_op jit(solution)/shard_map/ppermute | solution.py:380
  19.9 7.4 %collective-permute-start.5 = (bf16[64,512]{1,0:T(8,128)(2,1)S(1)}, bf16[64,512]{1,0:T(8,128)(2,1)S(1)}, u32[]{:S(2)}, u32[]{:S(2)}) collective-permute-start(bf16[64,512]{1,0:T(8,128)(2,1)S(1)} %slice.4), channel_id=1, source_target_pairs={{0,1},{1,0},{2,3},{3,2},{4,5},{5,4},{6,7},{7,6},{8,9},{9,8},{10,11... | collective-permute-start | bytes 196616 | tf_op jit(solution)/shard_map/ppermute | solution.py:380
  20.4 11.0 %collective-permute-start.4 = (bf16[64,512]{1,0:T(8,128)(2,1)S(1)}, bf16[64,512]{1,0:T(8,128)(2,1)S(1)}, u32[]{:S(2)}, u32[]{:S(2)}) collective-permute-start(bf16[64,512]{1,0:T(8,128)(2,1)S(1)} %get-tuple-element.28), channel_id=1, source_target_pairs={{0,4},{1,17},{2,6},{3,19},{4,0},{5,21},{6,2},{7,23},{8,12},{9,25},... | collective-permute-start | bytes 196616 | tf_op jit(solution)/shard_map/ppermute | solution.py:380
  24.0 2.5 %copy-start.1 = (s32[8,8]{1,0:T(8,128)S(1)}, s32[8,8]{1,0:T(8,128)}, u32[]{:S(2)}) copy-start(s32[8,8]{1,0:T(8,128)} %table.1) | copy-start | bytes 772
  28.7 23.9 %copy-start = (bf16[512,512]{1,0:T(8,128)(2,1)S(1)}, bf16[512,512]{1,0:T(8,128)(2,1)}, u32[]{:S(2)}) copy-start(bf16[512,512]{1,0:T(8,128)(2,1)} %rotation.3) | copy-start | bytes 1572868
  31.4 5.6 %collective-permute-start.7 = (bf16[96,512]{1,0:T(8,128)(2,1)S(1)}, bf16[96,512]{1,0:T(8,128)(2,1)S(1)}, u32[]{:S(2)}, u32[]{:S(2)}) collective-permute-start(bf16[96,512]{1,0:T(8,128)(2,1)S(1)} %shard_map.86.pay), channel_id=1, source_target_pairs={{0,16},{1,9},{2,18},{3,11},{4,20},{5,13},{6,22},{7,15},{8,24},{9,1... | collective-permute-start | bytes 294920 | tf_op jit(solution)/shard_map/ppermute | solution.py:380
  37.1 4.3 %collective-permute-start.8 = (bf16[64,512]{1,0:T(8,128)(2,1)S(1)}, bf16[64,512]{1,0:T(8,128)(2,1)S(1)}, u32[]{:S(2)}, u32[]{:S(2)}) collective-permute-start(bf16[64,512]{1,0:T(8,128)(2,1)S(1)} %shard_map.87.pay), channel_id=1, source_target_pairs={{0,4},{1,17},{2,6},{3,19},{4,0},{5,21},{6,2},{7,23},{8,12},{9,25},... | collective-permute-start | bytes 196616 | tf_op jit(solution)/shard_map/ppermute | solution.py:380
  41.4 5.7 %collective-permute-start.9 = (bf16[96,512]{1,0:T(8,128)(2,1)S(1)}, bf16[96,512]{1,0:T(8,128)(2,1)S(1)}, u32[]{:S(2)}, u32[]{:S(2)}) collective-permute-start(bf16[96,512]{1,0:T(8,128)(2,1)S(1)} %shard_map.88.pay), channel_id=1, source_target_pairs={{0,8},{1,3},{2,10},{3,1},{4,12},{5,7},{6,14},{7,5},{8,0},{9,11},{1... | collective-permute-start | bytes 294920 | tf_op jit(solution)/shard_map/ppermute | solution.py:380
  47.1 5.4 %collective-permute-start.10 = (bf16[160,512]{1,0:T(8,128)(2,1)S(1)}, bf16[160,512]{1,0:T(8,128)(2,1)S(1)}, u32[]{:S(2)}, u32[]{:S(2)}) collective-permute-start(bf16[160,512]{1,0:T(8,128)(2,1)S(1)} %shard_map.89.pay), channel_id=1, source_target_pairs={{0,2},{1,5},{2,0},{3,7},{4,6},{5,1},{6,4},{7,3},{8,10},{9,13},{10,... | collective-permute-start | bytes 491528 | tf_op jit(solution)/shard_map/ppermute | solution.py:380
  52.5 2.9 %collective-permute-start.11 = (bf16[288,512]{1,0:T(8,128)(2,1)S(1)}, bf16[288,512]{1,0:T(8,128)(2,1)S(1)}, u32[]{:S(2)}, u32[]{:S(2)}) collective-permute-start(bf16[288,512]{1,0:T(8,128)(2,1)S(1)} %shard_map.90.pay), channel_id=1, source_target_pairs={{0,1},{1,0},{2,3},{3,2},{4,5},{5,4},{6,7},{7,6},{8,9},{9,8},{10,11... | collective-permute-start | bytes 884744 | tf_op jit(solution)/shard_map/ppermute | solution.py:380

commit v4 on v3

--- a/solution.py
+++ b/solution.py
@@ -78,7 +78,7 @@
     return jax.ShapeDtypeStruct((rows, cols), dtype)
 
 
-def open_kernel(nb, spots, basis_far, images_far, pay, basis, images, shift, sems):
+def open_kernel(nb, spots, near, basis_far, images_far, table_far, hops_far, pay, basis, images, shift, perms, hops, table, sems):
     rows, nvec = basis.shape
     old = images.shape[1]
     blk = nvec - old
@@ -88,6 +88,10 @@
         for i in range(PIECES):
             span = pl.ds(i * step, step)
             copies.append(pltpu.make_async_copy(far.at[span], here.at[span], sems.at[j * PIECES + i]))
+    small = pltpu.make_async_copy(table_far, table, sems.at[2 * PIECES])
+    small.start()
+    for i, hop in enumerate(near):
+        copies.append(pltpu.make_async_copy(hops_far.at[hop], hops.at[i], sems.at[2 * PIECES + 1 + i]))
     for copy in copies:
         copy.start()
     core = place()[0]
@@ -100,6 +104,8 @@
     )
     gather = onehot((LANES, rows), lambda r, c: lax.div(c, nb) == r)
     spread = onehot((LANES, wide), lambda r, c: r - (LANES - blk) == lax.rem(c, blk))
+    small.wait()
+    choose(near, nb, blk, table[...], perms)
     for copy in copies[:PIECES]:
         copy.wait()
     tiled = dot_nn(basis[:, nvec - LANES :], spread)
@@ -111,7 +117,7 @@
     each = LANES // groups
     for g in range(groups):
         pay[2 * top :, g * LANES : (g + 1) * LANES] = merged[g * each : (g + 1) * each]
-    for copy in copies[PIECES:]:
+    for copy in copies[PIECES : 2 * PIECES]:
         copy.wait()
     give = basis[:, pl.ds(pl.multiple_of((1 - core) * top, top), top)]
     high, low = split(dot_tn(give, images[...]))
@@ -119,6 +125,8 @@
     pay[:top, old:] = jnp.zeros((top, blk), BF16)
     pay[top : 2 * top, :old] = low
     pay[top : 2 * top, old:] = jnp.zeros((top, blk), BF16)
+    for copy in copies[2 * PIECES :]:
+        copy.wait()
 
 
 def fetch_kernel(order, far, near, sems):
@@ -203,20 +211,20 @@
     cross[area:, :] = far[...]
 
 
-def setup_kernel(near, nb, blk, table, perms):
+def choose(near, nb, blk, table, perms):
     hops = perms.shape[0]
     wide = nb * blk
     row = lax.broadcasted_iota(jnp.int32, (2 * wide, wide), 0)
-    col = lax.broadcasted_iota(jnp.int32, (1, wide), 1)
-    for hop in range(hops):
-        wanted = col if hop == 0 else lax.rem(col, blk)
-        for b in range(nb if hop else 0):
-            entry = table[b, hop - 1]
-            base = lax.rem(entry, nb) * blk
-            if hop not in near:
-                base = base + jnp.where(entry >= nb, wide, 0)
-            wanted = wanted + jnp.where(lax.div(col, blk) == b, base, 0)
-        perms[hop] = jnp.where(row == wanted, 1.0, 0.0).astype(BF16)
+    col = lax.broadcasted_iota(jnp.int32, (hops - 1, wide), 1)
+    repeat = onehot((nb, wide), lambda r, c: lax.div(c, blk) == r)
+    entry = dot_tn(table.astype(F32).astype(BF16), repeat).astype(jnp.int32)
+    piece = lax.div(entry, nb)
+    wanted = (entry - piece * nb) * blk + lax.rem(col, blk)
+    aside = wanted + jnp.where(piece > 0, wide, 0)
+    perms[0] = onehot((2 * wide, wide), lambda r, c: r == c)
+    for hop in range(1, hops):
+        target = (wanted if hop in near else aside)[hop - 1 : hop, :]
+        perms[hop] = jnp.where(row == target, 1.0, 0.0).astype(BF16)
 
 
 def stack(ref, at, piece):
@@ -250,7 +258,7 @@
         total[span, :] = part
 
 
-def far_kernel(nb, blk, own, got2, cross, far, got1, crossed, total, basis, hops, perms, shift, *refs):
+def far_kernel(nb, blk, own, got2, cross, far, got1, crossed, total, basis, hops, more, perms, shift, *refs):
     times, (masked, new_out, column) = refs[:-3], refs[-3:]
     core, half, _, _, _ = place()
     each = far.shape[0]
@@ -284,7 +292,8 @@
         span = pl.ds(r * step, step)
         part = total[span, :]
         for i in range(len(order)):
-            part = part + dot_nn(hops[i, span, :], mixed[i])
+            source = hops if i < hops.shape[0] else more
+            part = part + dot_nn(source[i % hops.shape[0], span, :], mixed[i])
         row = lax.broadcasted_iota(jnp.int32, (step, wide), 0)
         col = lax.broadcasted_iota(jnp.int32, (step, wide), 1)
         chosen = jnp.where(lax.rem(row, nb) == lax.div(col, blk), part, 0.0).astype(BF16)
@@ -335,6 +344,17 @@
     out[rows_at(bit, n), :] = pay[:n, :]
     out[rows_at(1 - bit, n), :] = got[:n, :]
     out[2 * n : 2 * n + blk, :], out[2 * n + blk :, :] = split(value(pay, n, blk) + value(got, n, blk))
+
+
+def join_four_kernel(n, blk, first, second, pay, got_a, got_b, got_ab, out):
+    spot = place()
+    a, b = first(*spot), second(*spot)
+    out[rows_at(2 * b + a, n), :] = pay[:n, :]
+    out[rows_at(2 * b + 1 - a, n), :] = got_a[:n, :]
+    out[rows_at(2 * (1 - b) + a, n), :] = got_b[:n, :]
+    out[rows_at(2 * (1 - b) + 1 - a, n), :] = got_ab[:n, :]
+    new = (value(pay, n, blk) + value(got_a, n, blk)) + (value(got_b, n, blk) + value(got_ab, n, blk))
+    out[4 * n : 4 * n + blk, :], out[4 * n + blk :, :] = split(new)
 
 
 def final_kernel(n, blk, scale, pay, got, far, held, sems):
@@ -386,23 +406,30 @@
     flat_hops = jnp.transpose(hops, (1, 2, 0, 3)).reshape(hops.shape[1], rows, coarse)
     half = nvec // 2
     n = half // 8
-    pay0, basis_here, images_here, shift = call(
-        functools.partial(open_kernel, nb, spots),
+    near_order = [0] if sites > 8 else [0, 7, 8]
+    far_order = [hop for hop in range(hops.shape[1]) if hop not in near_order]
+    pay0, basis_here, images_here, shift, perms, near_hops = call(
+        functools.partial(open_kernel, nb, spots, near_order),
         (
             shaped(nvec + chunk, nvec, BF16),
             shaped(rows, nvec, BF16),
             shaped(rows, old, BF16),
             shaped(coarse, spots * LANES, BF16),
+            jax.ShapeDtypeStruct((hops.shape[1], 2 * wide, wide), BF16),
+            jax.ShapeDtypeStruct((len(near_order), rows, coarse), BF16),
         ),
         stay(flat_basis),
         stay(flat_images),
-        far=(0, 1),
-        scratch=[pltpu.SemaphoreType.DMA((2 * PIECES,))],
+        stay(neighbours),
+        stay(flat_hops),
+        far=(0, 1, 2, 3),
+        scratch=[
+            pltpu.VMEM(neighbours.shape, jnp.int32),
+            pltpu.SemaphoreType.DMA((2 * PIECES + 1 + len(near_order),)),
+        ],
     )
     got0 = send(pay0, core_hop, core_hop)
     kept0 = call(keep_kernel, shaped(half, nvec, F32), basis_here, images_here)
-    near_order = [0] if sites > 8 else [0, 7, 8]
-    far_order = [hop for hop in range(hops.shape[1]) if hop not in near_order]
 
     def fetched(order):
         return call(
@@ -413,14 +440,9 @@
             scratch=[pltpu.SemaphoreType.DMA((len(order),))],
         )
 
-    far_hops = fetched(far_order)
-    near_hops = fetched(near_order)
-    perms = call(
-        functools.partial(setup_kernel, near_order, nb, blk),
-        jax.ShapeDtypeStruct((hops.shape[1], 2 * wide, wide), BF16),
-        neighbours,
-        smem=(0,),
-    )
+    middle = len(far_order) // 2
+    far_hops = fetched(far_order[:middle])
+    more_hops = fetched(far_order[middle:])
     pay1, kept1, pair = call(
         second_kernel,
         (shaped(half + 2 * chunk, nvec, BF16), shaped(half // 2, nvec, F32), shaped(2 * chunk, nvec, BF16)),
@@ -476,6 +498,7 @@
         total,
         basis_here,
         far_hops,
+        more_hops,
         perms,
         shift,
         *times,
@@ -499,20 +522,35 @@
         gotc = send(payc, hop, hop)
         hop *= 2
     payc = call(functools.partial(settle_kernel, n, blk, scale), shaped(n + 2 * blk, nvec, BF16), payc, gotc)
-    steps = (
-        (y_hop, z1_hop, lambda core, half, y, z0, z1: pick(core, y, z1)),
-        (z0_hop, x_hop, lambda core, half, y, z0, z1: pick(core, z0, half)),
-        (x_hop, y_hop, lambda core, half, y, z0, z1: pick(core, half, y)),
-    )
     turned_basis = call(
         rotate_kernel, shaped(rows, nvec, BF16), basis_here, rotation, out_far=True, scratch=turned
     )
-    for first, second, chooser in steps:
-        gotc = send(payc, first, second)
-        payc = call(
-            functools.partial(grow_kernel, n, blk, chooser), shaped(2 * n + 2 * blk, nvec, BF16), payc, gotc
-        )
-        n *= 2
+    gotc = send(payc, y_hop, z1_hop)
+    payc = call(
+        functools.partial(grow_kernel, n, blk, lambda core, half, y, z0, z1: pick(core, y, z1)),
+        shaped(2 * n + 2 * blk, nvec, BF16),
+        payc,
+        gotc,
+    )
+    n *= 2
+    got_ab = send(payc, z0_hop + x_hop, x_hop + y_hop)
+    got_b = send(payc, x_hop, y_hop)
+    got_a = send(payc, z0_hop, x_hop)
+    payc = call(
+        functools.partial(
+            join_four_kernel,
+            n,
+            blk,
+            lambda core, half, y, z0, z1: pick(core, z0, half),
+            lambda core, half, y, z0, z1: pick(core, half, y),
+        ),
+        shaped(4 * n + 2 * blk, nvec, BF16),
+        payc,
+        got_a,
+        got_b,
+        got_ab,
+    )
+    n *= 4
     gotc = send(payc, core_hop, core_hop)
     projected = call(
         functools.partial(final_kernel, n, blk, scale),

time: 57.3 us -> 54.8 us (0.956)
  Pallas kernels: 16 us -> 14.6 us
  waiting for transfers between devices: 22.9 us -> 22 us
    pallas_call x18 -> x16, Pallas kernels: 16 us -> 14.6 us  [call(): pl.pallas_call(kernel, out_shape=outs, in_specs=[scalars if i in smem els...]
    ppermute x12 -> x13, waiting for transfers between devices: 22.9 us -> 22 us  [send(): return lax.ppermute(x, BOTH, pairs)]
    ppermute x12 -> x13, starting transfers between devices: 16.8 us -> 16.8 us  [send(): return lax.ppermute(x, BOTH, pairs)]
  transfers between devices with their start and end apart: 12 -> 13, of which waited for: 7 -> 8; matrix products, arithmetic and copies ran while one was open for 0% -> 0% of each run, Pallas kernels for 21% -> 20%
where the time goes in v4:
time: 54.8 us; the launch traced here: 54.2 us
  waiting for transfers between devices  22 us (40%)
  starting transfers between devices  16.8 us (31%)
  Pallas kernels  14.6 us (27%)
  between operations  0.81 us (1%)
    ppermute x13, waiting for transfers between devices, send(): return lax.ppermute(x, BOTH, pairs)  22 us
    ppermute x13, starting transfers between devices, send(): return lax.ppermute(x, BOTH, pairs)  16.8 us
    pallas_call x16, Pallas kernels, call(): pl.pallas_call(kernel, out_shape=outs, in_specs=[scalars if i in smem els...  14.6 us
  transfers between devices with their start and end apart: 13, of which 8 were waited for; matrix products, arithmetic and copies ran while one was open for 0% of the time, Pallas kernels for 20%

profile of v4, /device:TPU:0, one launch (start us, length us, event | category | flops | bytes accessed | tf_op | source)
XLA Modules:
  0.0 54.2 jit_solution(11608910056465569404)
XLA Ops:
  0.6 2.4 %shard_map.76 = (bf16[544,512]{1,0:T(8,128)(2,1)S(1)}, bf16[800,512]{1,0:T(8,128)(2,1)S(1)}, bf16[800,496]{1,0:T(8,128)(2,1)S(1)}, bf16[400,512]{1,0:T(8,128)(2,...) custom-call(bf16[800,512]{1,0:T(8,128)(2,1)} %bitcast.20, bf16[800,496]{1,0:T(8,128)(2,1)} %bitcast.21, ...), custom_call_target="tpu_custom_call" | custom-call | flops 100000000 | bytes 2000000 | tf_op jit(solution)/shard_map/pallas_call | solution.py:62
  3.0 0.6 %collective-permute-start = (bf16[544,512]{1,0:T(8,128)(2,1)S(1)}, bf16[544,512]{1,0:T(8,128)(2,1)S(1)}, u32[]{:S(2)}, u32[]{:S(2)}) collective-permute-start(bf16[544,512]{1,0:T(8,128)(2,1)S(1)} %get-tuple-element.23.pay), channel_id=1, source_target_pairs={{0,1},{1,0},{2,3},{3,2},{4,5},{5,4},{6,7},{7,6},{8,9},{9,8},{10,11... | collective-permute-start | bytes 1671176 | tf_op jit(solution)/shard_map/ppermute | solution.py:400
  3.6 0.5 shard_map.77.kept
  4.1 1.1 %collective-permute-done.got = bf16[544,512]{1,0:T(8,128)(2,1)S(1)} collective-permute-done((bf16[544,512]{1,0:T(8,128)(2,1)S(1)}, bf16[544,512]{1,0:T(8,128)(2,1)S(1)}, u32[]{:S(2)}, u32[]{:S(2)}) %collective-permute-start) | collective-permute-done | bytes 557088 | tf_op jit(solution)/shard_map/ppermute | solution.py:400
  5.2 0.2 shard_map.78
  5.3 2.9 %collective-permute-start.1 = (bf16[320,512]{1,0:T(8,128)(2,1)S(1)}, bf16[320,512]{1,0:T(8,128)(2,1)S(1)}, u32[]{:S(2)}, u32[]{:S(2)}) collective-permute-start(bf16[320,512]{1,0:T(8,128)(2,1)S(1)} %get-tuple-element.25), channel_id=1, source_target_pairs={{0,2},{1,5},{2,0},{3,7},{4,6},{5,1},{6,4},{7,3},{8,10},{9,13},{10,... | collective-permute-start | bytes 983048 | tf_op jit(solution)/shard_map/ppermute | solution.py:400
  8.3 0.7 %collective-permute-start.2 = (bf16[64,512]{1,0:T(8,128)(2,1)S(1)}, bf16[64,512]{1,0:T(8,128)(2,1)S(1)}, u32[]{:S(2)}, u32[]{:S(2)}) collective-permute-start(bf16[64,512]{1,0:T(8,128)(2,1)S(1)} %get-tuple-element.26.pair), channel_id=1, source_target_pairs={{1,17},{3,19},{5,21},{7,23},{9,25},{11,27},{13,29},{15,31},{17,1},... | collective-permute-start | bytes 196616 | tf_op jit(solution)/shard_map/ppermute | solution.py:400
  8.9 4.4 %collective-permute-done.1.got.got1 = bf16[320,512]{1,0:T(8,128)(2,1)S(1)} collective-permute-done((bf16[320,512]{1,0:T(8,128)(2,1)S(1)}, bf16[320,512]{1,0:T(8,128)(2,1)S(1)}, u32[]{:S(2)}, u32[]{:S(2)}) %collective-permute-start.1) | collective-permute-done | bytes 327712 | tf_op jit(solution)/shard_map/ppermute | solution.py:400
  13.3 0.1 shard_map.79
  13.4 2.2 %collective-permute-start.3 = (bf16[256,512]{1,0:T(8,128)(2,1)S(1)}, bf16[256,512]{1,0:T(8,128)(2,1)S(1)}, u32[]{:S(2)}, u32[]{:S(2)}) collective-permute-start(bf16[256,512]{1,0:T(8,128)(2,1)S(1)} %get-tuple-element.28), channel_id=1, source_target_pairs={{0,8},{1,3},{2,10},{3,1},{4,12},{5,7},{6,14},{7,5},{8,0},{9,11},{1... | collective-permute-start | bytes 786440 | tf_op jit(solution)/shard_map/ppermute | solution.py:400
  15.6 4.4 %collective-permute-done.3.got.got2 = bf16[256,512]{1,0:T(8,128)(2,1)S(1)} collective-permute-done((bf16[256,512]{1,0:T(8,128)(2,1)S(1)}, bf16[256,512]{1,0:T(8,128)(2,1)S(1)}, u32[]{:S(2)}, u32[]{:S(2)}) %collective-permute-start.3) | collective-permute-done | bytes 262176 | tf_op jit(solution)/shard_map/ppermute | solution.py:400
  20.0 0.1 collective-permute-start.6
  20.1 0.5 collective-permute-start.5
  20.6 2.0 %collective-permute-start.4 = (bf16[64,512]{1,0:T(8,128)(2,1)S(1)}, bf16[64,512]{1,0:T(8,128)(2,1)S(1)}, u32[]{:S(2)}, u32[]{:S(2)}) collective-permute-start(bf16[64,512]{1,0:T(8,128)(2,1)S(1)} %get-tuple-element.30), channel_id=1, source_target_pairs={{0,4},{1,17},{2,6},{3,19},{4,0},{5,21},{6,2},{7,23},{8,12},{9,25},... | collective-permute-start | bytes 196616 | tf_op jit(solution)/shard_map/ppermute | solution.py:400
  22.5 1.7 %shard_map.82.hops = bf16[3,800,400]{2,1,0:T(8,128)(2,1)S(1)} custom-call(bf16[9,800,400]{2,1,0:T(8,128)(2,1)} %bitcast.16), custom_call_target="tpu_custom_call" | custom-call | flops 100000000 | bytes 2000000 | tf_op jit(solution)/shard_map/pallas_call | solution.py:62
  24.2 1.7 %shard_map.83.more = bf16[3,800,400]{2,1,0:T(8,128)(2,1)S(1)} custom-call(bf16[9,800,400]{2,1,0:T(8,128)(2,1)} %bitcast.17), custom_call_target="tpu_custom_call" | custom-call | flops 100000000 | bytes 2000000 | tf_op jit(solution)/shard_map/pallas_call | solution.py:62
  25.9 1.3 %shard_map.81 = (f32[800,128]{1,0:T(8,128)S(1)}, bf16[400,128]{1,0:T(8,128)(2,1)S(1)}) custom-call(bf16[64,512]{1,0:T(8,128)(2,1)S(1)} %get-tuple-element.26.pair, bf16[320,512]{1,0:T(8,128)(2,1)S(1)} %collective-permute-done.1.got.got1, bf16[64,512]{1,0:T(8,128)(2,1)S(1)} %collective-permute-done.5.crossed, ...), custom_call_target="tpu_custom_call" | custom-call | flops 100000000 | bytes 2000000 | tf_op jit(solution)/shard_map/pallas_call | solution.py:62
  27.2 2.6 %shard_map.84 = (bf16[800,128]{1,0:T(8,128)(2,1)S(1)}, bf16[32,512]{1,0:T(8,128)(2,1)S(1)}) custom-call(bf16[400,128]{1,0:T(8,128)(2,1)S(1)} %get-tuple-element.34.own, bf16[256,512]{1,0:T(8,128)(2,1)S(1)} %collective-permute-done.3.got.got2, bf16[192,512]{1,0:T(8,128)(2,1)S(1)} %collective-permute-done.6.cross, ...), custom_call_target="tpu_custom_call" | custom-call | flops 100000000 | bytes 2000000 | tf_op jit(solution)/shard_map/pallas_call | solution.py:62
  29.9 2.7 %collective-permute-start.7 = (bf16[96,512]{1,0:T(8,128)(2,1)S(1)}, bf16[96,512]{1,0:T(8,128)(2,1)S(1)}, u32[]{:S(2)}, u32[]{:S(2)}) collective-permute-start(bf16[96,512]{1,0:T(8,128)(2,1)S(1)} %shard_map.85.pay), channel_id=1, source_target_pairs={{0,16},{1,9},{2,18},{3,11},{4,20},{5,13},{6,22},{7,15},{8,24},{9,1... | collective-permute-start | bytes 294920 | tf_op jit(solution)/shard_map/ppermute | solution.py:400
  32.6 3.0 %collective-permute-done.7.got = bf16[96,512]{1,0:T(8,128)(2,1)S(1)} collective-permute-done((bf16[96,512]{1,0:T(8,128)(2,1)S(1)}, bf16[96,512]{1,0:T(8,128)(2,1)S(1)}, u32[]{:S(2)}, u32[]{:S(2)}) %collective-permute-start.7) | collective-permute-done | bytes 98336 | tf_op jit(solution)/shard_map/ppermute | solution.py:400
  35.6 0.7 %collective-permute-start.8 = (bf16[64,512]{1,0:T(8,128)(2,1)S(1)}, bf16[64,512]{1,0:T(8,128)(2,1)S(1)}, u32[]{:S(2)}, u32[]{:S(2)}) collective-permute-start(bf16[64,512]{1,0:T(8,128)(2,1)S(1)} %shard_map.86.pay), channel_id=1, source_target_pairs={{0,4},{1,17},{2,6},{3,19},{4,0},{5,21},{6,2},{7,23},{8,12},{9,25},... | collective-permute-start | bytes 196616 | tf_op jit(solution)/shard_map/ppermute | solution.py:400
  36.3 3.7 %collective-permute-done.8.got = bf16[64,512]{1,0:T(8,128)(2,1)S(1)} collective-permute-done((bf16[64,512]{1,0:T(8,128)(2,1)S(1)}, bf16[64,512]{1,0:T(8,128)(2,1)S(1)}, u32[]{:S(2)}, u32[]{:S(2)}) %collective-permute-start.8) | collective-permute-done | bytes 65568 | tf_op jit(solution)/shard_map/ppermute | solution.py:400
  39.9 3.1 %collective-permute-start.9 = (bf16[96,512]{1,0:T(8,128)(2,1)S(1)}, bf16[96,512]{1,0:T(8,128)(2,1)S(1)}, u32[]{:S(2)}, u32[]{:S(2)}) collective-permute-start(bf16[96,512]{1,0:T(8,128)(2,1)S(1)} %shard_map.87.pay), channel_id=1, source_target_pairs={{0,8},{1,3},{2,10},{3,1},{4,12},{5,7},{6,14},{7,5},{8,0},{9,11},{1... | collective-permute-start | bytes 294920 | tf_op jit(solution)/shard_map/ppermute | solution.py:400
  43.0 1.5 %collective-permute-start.10 = (bf16[96,512]{1,0:T(8,128)(2,1)S(1)}, bf16[96,512]{1,0:T(8,128)(2,1)S(1)}, u32[]{:S(2)}, u32[]{:S(2)}) collective-permute-start(bf16[96,512]{1,0:T(8,128)(2,1)S(1)} %shard_map.87.pay), channel_id=1, source_target_pairs={{0,2},{1,5},{2,0},{3,7},{4,6},{5,1},{6,4},{7,3},{8,10},{9,13},{10,... | collective-permute-start | bytes 294920 | tf_op jit(solution)/shard_map/ppermute | solution.py:400
  44.5 0.1 collective-permute-start.11
  44.5 1.1 %collective-permute-done.9.got_a = bf16[96,512]{1,0:T(8,128)(2,1)S(1)} collective-permute-done((bf16[96,512]{1,0:T(8,128)(2,1)S(1)}, bf16[96,512]{1,0:T(8,128)(2,1)S(1)}, u32[]{:S(2)}, u32[]{:S(2)}) %collective-permute-start.9) | collective-permute-done | bytes 98336 | tf_op jit(solution)/shard_map/ppermute | solution.py:400
  45.6 2.0 %collective-permute-done.10.got_b = bf16[96,512]{1,0:T(8,128)(2,1)S(1)} collective-permute-done((bf16[96,512]{1,0:T(8,128)(2,1)S(1)}, bf16[96,512]{1,0:T(8,128)(2,1)S(1)}, u32[]{:S(2)}, u32[]{:S(2)}) %collective-permute-start.10) | collective-permute-done | bytes 98336 | tf_op jit(solution)/shard_map/ppermute | solution.py:400
  47.6 2.4 %collective-permute-done.11.got_ab = bf16[96,512]{1,0:T(8,128)(2,1)S(1)} collective-permute-done((bf16[96,512]{1,0:T(8,128)(2,1)S(1)}, bf16[96,512]{1,0:T(8,128)(2,1)S(1)}, u32[]{:S(2)}, u32[]{:S(2)}) %collective-permute-start.11) | collective-permute-done | bytes 98336 | tf_op jit(solution)/shard_map/ppermute | solution.py:400
  50.1 0.1 collective-permute-start.12
  50.1 1.3 %shard_map.90 = bf16[800,512]{1,0:T(8,128)(2,1)} custom-call(bf16[800,512]{1,0:T(8,128)(2,1)S(1)} %get-tuple-element.21.basis, bf16[512,512]{1,0:T(8,128)(2,1)S(1)} %copy-done), custom_call_target="tpu_custom_call" | custom-call | flops 100000000 | bytes 2000000 | tf_op jit(solution)/shard_map/pallas_call | solution.py:62
  51.5 1.5 %shard_map.91 = bf16[800,512]{1,0:T(8,128)(2,1)} custom-call(bf16[800,496]{1,0:T(8,128)(2,1)S(1)} %get-tuple-element.22.images, bf16[800,128]{1,0:T(8,128)(2,1)S(1)} %get-tuple-element.38.masked, bf16[512,512]{1,0:T(8,128)(2,1)S(1)} %copy-done), custom_call_target="tpu_custom_call" | custom-call | flops 100000000 | bytes 2000000 | tf_op jit(solution)/shard_map/pallas_call | solution.py:62
  53.0 1.2 %shard_map.89 = f32[512,512]{1,0:T(8,128)} custom-call(bf16[288,512]{1,0:T(8,128)(2,1)S(1)} %shard_map.88.pay, bf16[288,512]{1,0:T(8,128)(2,1)S(1)} %collective-permute-done.12.got), custom_call_target="tpu_custom_call" | custom-call | flops 100000000 | bytes 2000000 | tf_op jit(solution)/shard_map/pallas_call | solution.py:62
  (13 shorter events, 0.2 us)
Async XLA Ops:
  3.0 2.1 %collective-permute-start = (bf16[544,512]{1,0:T(8,128)(2,1)S(1)}, bf16[544,512]{1,0:T(8,128)(2,1)S(1)}, u32[]{:S(2)}, u32[]{:S(2)}) collective-permute-start(bf16[544,512]{1,0:T(8,128)(2,1)S(1)} %get-tuple-element.23.pay), channel_id=1, source_target_pairs={{0,1},{1,0},{2,3},{3,2},{4,5},{5,4},{6,7},{7,6},{8,9},{9,8},{10,11... | collective-permute-start | bytes 1671176 | tf_op jit(solution)/shard_map/ppermute | solution.py:400
  5.3 8.0 %collective-permute-start.1 = (bf16[320,512]{1,0:T(8,128)(2,1)S(1)}, bf16[320,512]{1,0:T(8,128)(2,1)S(1)}, u32[]{:S(2)}, u32[]{:S(2)}) collective-permute-start(bf16[320,512]{1,0:T(8,128)(2,1)S(1)} %get-tuple-element.25), channel_id=1, source_target_pairs={{0,2},{1,5},{2,0},{3,7},{4,6},{5,1},{6,4},{7,3},{8,10},{9,13},{10,... | collective-permute-start | bytes 983048 | tf_op jit(solution)/shard_map/ppermute | solution.py:400
  8.3 0.7 %collective-permute-start.2 = (bf16[64,512]{1,0:T(8,128)(2,1)S(1)}, bf16[64,512]{1,0:T(8,128)(2,1)S(1)}, u32[]{:S(2)}, u32[]{:S(2)}) collective-permute-start(bf16[64,512]{1,0:T(8,128)(2,1)S(1)} %get-tuple-element.26.pair), channel_id=1, source_target_pairs={{1,17},{3,19},{5,21},{7,23},{9,25},{11,27},{13,29},{15,31},{17,1},... | collective-permute-start | bytes 196616 | tf_op jit(solution)/shard_map/ppermute | solution.py:400
  13.4 6.5 %collective-permute-start.3 = (bf16[256,512]{1,0:T(8,128)(2,1)S(1)}, bf16[256,512]{1,0:T(8,128)(2,1)S(1)}, u32[]{:S(2)}, u32[]{:S(2)}) collective-permute-start(bf16[256,512]{1,0:T(8,128)(2,1)S(1)} %get-tuple-element.28), channel_id=1, source_target_pairs={{0,8},{1,3},{2,10},{3,1},{4,12},{5,7},{6,14},{7,5},{8,0},{9,11},{1... | collective-permute-start | bytes 786440 | tf_op jit(solution)/shard_map/ppermute | solution.py:400
  20.0 7.3 %collective-permute-start.6 = (bf16[192,512]{1,0:T(8,128)(2,1)S(1)}, bf16[192,512]{1,0:T(8,128)(2,1)S(1)}, u32[]{:S(2)}, u32[]{:S(2)}) collective-permute-start(bf16[192,512]{1,0:T(8,128)(2,1)S(1)} %get-tuple-element.35), channel_id=1, source_target_pairs={{0,1},{1,0},{2,3},{3,2},{4,5},{5,4},{6,7},{7,6},{8,9},{9,8},{10,11... | collective-permute-start | bytes 589832 | tf_op jit(solution)/shard_map/ppermute | solution.py:400
  20.1 5.8 %collective-permute-start.5 = (bf16[64,512]{1,0:T(8,128)(2,1)S(1)}, bf16[64,512]{1,0:T(8,128)(2,1)S(1)}, u32[]{:S(2)}, u32[]{:S(2)}) collective-permute-start(bf16[64,512]{1,0:T(8,128)(2,1)S(1)} %slice.4), channel_id=1, source_target_pairs={{0,1},{1,0},{2,3},{3,2},{4,5},{5,4},{6,7},{7,6},{8,9},{9,8},{10,11... | collective-permute-start | bytes 196616 | tf_op jit(solution)/shard_map/ppermute | solution.py:400
  20.6 9.3 %collective-permute-start.4 = (bf16[64,512]{1,0:T(8,128)(2,1)S(1)}, bf16[64,512]{1,0:T(8,128)(2,1)S(1)}, u32[]{:S(2)}, u32[]{:S(2)}) collective-permute-start(bf16[64,512]{1,0:T(8,128)(2,1)S(1)} %get-tuple-element.30), channel_id=1, source_target_pairs={{0,4},{1,17},{2,6},{3,19},{4,0},{5,21},{6,2},{7,23},{8,12},{9,25},... | collective-permute-start | bytes 196616 | tf_op jit(solution)/shard_map/ppermute | solution.py:400
  27.2 22.9 %copy-start = (bf16[512,512]{1,0:T(8,128)(2,1)S(1)}, bf16[512,512]{1,0:T(8,128)(2,1)}, u32[]{:S(2)}) copy-start(bf16[512,512]{1,0:T(8,128)(2,1)} %rotation.3) | copy-start | bytes 1572868
  29.9 5.6 %collective-permute-start.7 = (bf16[96,512]{1,0:T(8,128)(2,1)S(1)}, bf16[96,512]{1,0:T(8,128)(2,1)S(1)}, u32[]{:S(2)}, u32[]{:S(2)}) collective-permute-start(bf16[96,512]{1,0:T(8,128)(2,1)S(1)} %shard_map.85.pay), channel_id=1, source_target_pairs={{0,16},{1,9},{2,18},{3,11},{4,20},{5,13},{6,22},{7,15},{8,24},{9,1... | collective-permute-start | bytes 294920 | tf_op jit(solution)/shard_map/ppermute | solution.py:400
  35.6 4.3 %collective-permute-start.8 = (bf16[64,512]{1,0:T(8,128)(2,1)S(1)}, bf16[64,512]{1,0:T(8,128)(2,1)S(1)}, u32[]{:S(2)}, u32[]{:S(2)}) collective-permute-start(bf16[64,512]{1,0:T(8,128)(2,1)S(1)} %shard_map.86.pay), channel_id=1, source_target_pairs={{0,4},{1,17},{2,6},{3,19},{4,0},{5,21},{6,2},{7,23},{8,12},{9,25},... | collective-permute-start | bytes 196616 | tf_op jit(solution)/shard_map/ppermute | solution.py:400
  39.9 5.7 %collective-permute-start.9 = (bf16[96,512]{1,0:T(8,128)(2,1)S(1)}, bf16[96,512]{1,0:T(8,128)(2,1)S(1)}, u32[]{:S(2)}, u32[]{:S(2)}) collective-permute-start(bf16[96,512]{1,0:T(8,128)(2,1)S(1)} %shard_map.87.pay), channel_id=1, source_target_pairs={{0,8},{1,3},{2,10},{3,1},{4,12},{5,7},{6,14},{7,5},{8,0},{9,11},{1... | collective-permute-start | bytes 294920 | tf_op jit(solution)/shard_map/ppermute | solution.py:400
  43.0 4.6 %collective-permute-start.10 = (bf16[96,512]{1,0:T(8,128)(2,1)S(1)}, bf16[96,512]{1,0:T(8,128)(2,1)S(1)}, u32[]{:S(2)}, u32[]{:S(2)}) collective-permute-start(bf16[96,512]{1,0:T(8,128)(2,1)S(1)} %shard_map.87.pay), channel_id=1, source_target_pairs={{0,2},{1,5},{2,0},{3,7},{4,6},{5,1},{6,4},{7,3},{8,10},{9,13},{10,... | collective-permute-start | bytes 294920 | tf_op jit(solution)/shard_map/ppermute | solution.py:400
  44.5 5.5 %collective-permute-start.11 = (bf16[96,512]{1,0:T(8,128)(2,1)S(1)}, bf16[96,512]{1,0:T(8,128)(2,1)S(1)}, u32[]{:S(2)}, u32[]{:S(2)}) collective-permute-start(bf16[96,512]{1,0:T(8,128)(2,1)S(1)} %shard_map.87.pay), channel_id=1, source_target_pairs={{0,10},{1,7},{2,8},{3,5},{4,14},{5,3},{6,12},{7,1},{8,2},{9,15},{1... | collective-permute-start | bytes 294920 | tf_op jit(solution)/shard_map/ppermute | solution.py:400
  50.1 2.9 %collective-permute-start.12 = (bf16[288,512]{1,0:T(8,128)(2,1)S(1)}, bf16[288,512]{1,0:T(8,128)(2,1)S(1)}, u32[]{:S(2)}, u32[]{:S(2)}) collective-permute-start(bf16[288,512]{1,0:T(8,128)(2,1)S(1)} %shard_map.88.pay), channel_id=1, source_target_pairs={{0,1},{1,0},{2,3},{3,2},{4,5},{5,4},{6,7},{7,6},{8,9},{9,8},{10,11... | collective-permute-start | bytes 884744 | tf_op jit(solution)/shard_map/ppermute | solution.py:400

commit v5 on v4

--- a/solution.py
+++ b/solution.py
@@ -13,7 +13,7 @@
 BF16 = jnp.bfloat16
 BOTH = ("site", "mode")
 LANES = 128
-PIECES = 5
+PIECES = 2
 
 
 def dot_nn(a, b):
@@ -55,7 +55,7 @@
     return pl.ds(pl.multiple_of(index * count, count), count)
 
 
-def call(kernel, outs, *args, scratch=(), flops=10**8, moved=2 * 10**6, smem=(), far=(), out_far=False):
+def call(kernel, outs, *args, scratch=(), flops=10**8, moved=2 * 10**6, smem=(), far=(), out_far=False, alias={}):
     vmem = pl.BlockSpec(memory_space=pltpu.VMEM)
     scalars = pl.BlockSpec(memory_space=pltpu.SMEM)
     distant = pl.BlockSpec(memory_space=pltpu.HBM)
@@ -65,6 +65,7 @@
         in_specs=[scalars if i in smem else distant if i in far else vmem for i in range(len(args))],
         out_specs=jax.tree.map(lambda _: pl.BlockSpec(memory_space=pl.ANY) if out_far else vmem, outs),
         scratch_shapes=scratch,
+        input_output_aliases=alias,
         compiler_params=pltpu.CompilerParams(vmem_limit_bytes=16 * 2**20),
         cost_estimate=pl.CostEstimate(flops=flops, bytes_accessed=moved, transcendentals=0),
     )(*args)
@@ -78,7 +79,7 @@
     return jax.ShapeDtypeStruct((rows, cols), dtype)
 
 
-def open_kernel(nb, spots, near, basis_far, images_far, table_far, hops_far, pay, basis, images, shift, perms, hops, table, sems):
+def open_kernel(nb, spots, near, basis_far, images_far, table_far, pay, basis, images, shift, perms, table, sems):
     rows, nvec = basis.shape
     old = images.shape[1]
     blk = nvec - old
@@ -90,14 +91,12 @@
             copies.append(pltpu.make_async_copy(far.at[span], here.at[span], sems.at[j * PIECES + i]))
     small = pltpu.make_async_copy(table_far, table, sems.at[2 * PIECES])
     small.start()
-    for i, hop in enumerate(near):
-        copies.append(pltpu.make_async_copy(hops_far.at[hop], hops.at[i], sems.at[2 * PIECES + 1 + i]))
     for copy in copies:
         copy.start()
     core = place()[0]
     top = nvec // 2
     wide = nb * blk
-    share = shift.shape[0] // spots
+    share = 2 * shift.shape[0] // spots
     shift[...] = onehot(
         shift.shape,
         lambda r, c: (lax.rem(c, LANES) < share) & (lax.div(c, LANES) * share + lax.rem(c, LANES) == r),
@@ -117,16 +116,18 @@
     each = LANES // groups
     for g in range(groups):
         pay[2 * top :, g * LANES : (g + 1) * LANES] = merged[g * each : (g + 1) * each]
-    for copy in copies[PIECES : 2 * PIECES]:
-        copy.wait()
-    give = basis[:, pl.ds(pl.multiple_of((1 - core) * top, top), top)]
-    high, low = split(dot_tn(give, images[...]))
+    give = pl.ds(pl.multiple_of((1 - core) * top, top), top)
+    part = None
+    for i in range(PIECES):
+        span = pl.ds(i * step, step)
+        copies[PIECES + i].wait()
+        piece = dot_tn(basis[span, give], images[span, :])
+        part = piece if part is None else part + piece
+    high, low = split(part)
     pay[:top, :old] = high
     pay[:top, old:] = jnp.zeros((top, blk), BF16)
     pay[top : 2 * top, :old] = low
     pay[top : 2 * top, old:] = jnp.zeros((top, blk), BF16)
-    for copy in copies[2 * PIECES :]:
-        copy.wait()
 
 
 def fetch_kernel(order, far, near, sems):
@@ -227,7 +228,7 @@
         perms[hop] = jnp.where(row == target, 1.0, 0.0).astype(BF16)
 
 
-def stack(ref, at, piece):
+def half_site(shift, piece):
     rows, nvec = piece.shape
     groups = nvec // LANES
     each = LANES // groups
@@ -235,31 +236,38 @@
     parts = [
         piece[m * each : (m + 1) * each, g * LANES : (g + 1) * LANES] for m in range(chunks) for g in range(groups)
     ]
-    ref[rows_at(at, chunks * LANES), :] = jnp.concatenate(parts, axis=0)
-
-
-def near_kernel(order, pair, got, crossed, hops, perms, shift, total, own_out, column):
+    return dot_nn(shift, jnp.concatenate(parts, axis=0))
+
+
+def ordered(half, first, second):
+    low = jnp.where(half == 0, first, second)
+    high = jnp.where(half == 0, second, first)
+    return jnp.concatenate([low, high], axis=0).astype(BF16)
+
+
+def near_kernel(order, spots_of, pair, got, crossed, hops, more, perms, shift, total, own_out):
     core, half, _, _, _ = place()
     each = pair.shape[0]
     wide = own_out.shape[1]
     area = got.shape[0]
-    stack(column, half, pair[...])
-    stack(column, 1 - half, jnp.where(core == 0, got[area - each :, :], crossed[...]))
-    own = dot_nn(shift[...], column[...]).astype(BF16)
+    apart = jnp.where(core == 0, got[area - each :, :], crossed[...])
+    own = ordered(half, half_site(shift[...], pair[...]), half_site(shift[...], apart))
     own_out[...] = own
     rows = total.shape[0]
     mixed = [dot_nn(own, perms[hop, :wide, :]).astype(BF16) for hop in order]
     step = rows // 2
     for r in range(2):
         span = pl.ds(r * step, step)
-        part = dot_nn(hops[0, span, :], mixed[0])
-        for i in range(1, len(order)):
-            part = part + dot_nn(hops[i, span, :], mixed[i])
+        part = None
+        for i, hop in enumerate(order):
+            group, at = spots_of[hop]
+            piece = dot_nn((hops, more)[group][at, span, :], mixed[i])
+            part = piece if part is None else part + piece
         total[span, :] = part
 
 
-def far_kernel(nb, blk, own, got2, cross, far, got1, crossed, total, basis, hops, more, perms, shift, *refs):
-    times, (masked, new_out, column) = refs[:-3], refs[-3:]
+def far_kernel(nb, blk, spots_of, own, got2, cross, far, got1, crossed, total, basis, hops, more, perms, shift, *refs):
+    times, (masked, new_out) = refs[:-2], refs[-2:]
     core, half, _, _, _ = place()
     each = far.shape[0]
     wide = own.shape[1]
@@ -271,14 +279,18 @@
     sites = []
     one = jnp.where(first, theirs, mine)
     two = jnp.where(first, mine, theirs)
-    stack(column.at[0], half, jnp.where(first, crossed[...], got1[got1.shape[0] - each :, :]))
-    stack(column.at[0], 1 - half, one[:each])
-    stack(column.at[1], half, jnp.where(first, cross[2 * each :, :], far[...]))
-    stack(column.at[1], 1 - half, one[each:])
-    stack(column.at[2], 0, two)
-    near_site = dot_nn(shift[...], column[0]).astype(BF16)
-    long_site = dot_nn(shift[...], column[1]).astype(BF16)
-    mid_site = dot_nn(shift[...], column[2]).astype(BF16)
+    move = shift[...]
+    near_site = ordered(
+        half,
+        half_site(move, jnp.where(first, crossed[...], got1[got1.shape[0] - each :, :])),
+        half_site(move, one[:each]),
+    )
+    long_site = ordered(
+        half,
+        half_site(move, jnp.where(first, cross[2 * each :, :], far[...])),
+        half_site(move, one[each:]),
+    )
+    mid_site = ordered(0, half_site(move, two[:each]), half_site(move, two[each:]))
     sites = {1: long_site, 4: long_site, 2: mid_site, 5: mid_site, 3: near_site, 6: near_site}
     for k, ref in enumerate(times):
         sites[7 + k] = ref[...]
@@ -291,9 +303,9 @@
     for r in range(2):
         span = pl.ds(r * step, step)
         part = total[span, :]
-        for i in range(len(order)):
-            source = hops if i < hops.shape[0] else more
-            part = part + dot_nn(source[i % hops.shape[0], span, :], mixed[i])
+        for i, hop in enumerate(order):
+            group, at = spots_of[hop]
+            part = part + dot_nn((None, hops, more)[group][at, span, :], mixed[i])
         row = lax.broadcasted_iota(jnp.int32, (step, wide), 0)
         col = lax.broadcasted_iota(jnp.int32, (step, wide), 1)
         chosen = jnp.where(lax.rem(row, nb) == lax.div(col, blk), part, 0.0).astype(BF16)
@@ -357,27 +369,35 @@
     out[4 * n : 4 * n + blk, :], out[4 * n + blk :, :] = split(new)
 
 
-def final_kernel(n, blk, scale, pay, got, far, held, sems):
+def early_kernel(n, pay, far, held, sem):
+    core = place()[0]
+    width = held.shape[1]
+    held[...] = pay[:n, :width].astype(F32)
+    copy = pltpu.make_async_copy(held, far.at[rows_at(core, n), :width], sem)
+    copy.start()
+    copy.wait()
+
+
+def final_kernel(n, blk, scale, pay, got, begun, far, held, edge, sems):
     nvec = far.shape[1]
     core = place()[0]
+    width = nvec - LANES
     new = (value(pay, n, blk) + value(got, n, blk)) * scale
     tall = jnp.concatenate([jnp.zeros((LANES - blk, nvec), F32), new], axis=0)
-    held[:, nvec - LANES :] = tall.T
     step = n // 2
-    lane = lax.broadcasted_iota(jnp.int32, (step, LANES), 1)
     copies = []
-    for i in range(4):
-        side = core if i < 2 else 1 - core
-        source = pay if i < 2 else got
-        part = source[(i % 2) * step : (i % 2 + 1) * step, :].astype(F32)
-        span = pl.ds(pl.multiple_of(side * n + (i % 2) * step, step), step)
-        held[span, : nvec - LANES] = part[:, : nvec - LANES]
-        held[span, nvec - LANES :] = jnp.where(
-            lane < LANES - blk, part[:, nvec - LANES :], held[span, nvec - LANES :]
-        )
-        copy = pltpu.make_async_copy(held.at[span], far.at[span], sems.at[i])
-        copy.start()
-        copies.append(copy)
+    for i in range(2):
+        held[i * step : (i + 1) * step, :width] = got[i * step : (i + 1) * step, :width].astype(F32)
+        span = pl.ds(pl.multiple_of((1 - core) * n + i * step, step), step)
+        copies.append(pltpu.make_async_copy(held.at[pl.ds(i * step, step)], far.at[span, :width], sems.at[i]))
+        copies[-1].start()
+    lane = lax.broadcasted_iota(jnp.int32, (n, LANES), 1)
+    edge[...] = tall.T
+    for source, side in ((pay, core), (got, 1 - core)):
+        span = rows_at(side, n)
+        edge[span, :] = jnp.where(lane < LANES - blk, source[:n, width:].astype(F32), edge[span, :])
+    copies.append(pltpu.make_async_copy(edge, far.at[:, width:], sems.at[2]))
+    copies[-1].start()
     for copy in copies:
         copy.wait()
 
@@ -408,28 +428,24 @@
     n = half // 8
     near_order = [0] if sites > 8 else [0, 7, 8]
     far_order = [hop for hop in range(hops.shape[1]) if hop not in near_order]
-    pay0, basis_here, images_here, shift, perms, near_hops = call(
+    pay0, basis_here, images_here, shift, perms = call(
         functools.partial(open_kernel, nb, spots, near_order),
         (
             shaped(nvec + chunk, nvec, BF16),
             shaped(rows, nvec, BF16),
             shaped(rows, old, BF16),
-            shaped(coarse, spots * LANES, BF16),
+            shaped(coarse // 2, spots * LANES // 2, BF16),
             jax.ShapeDtypeStruct((hops.shape[1], 2 * wide, wide), BF16),
-            jax.ShapeDtypeStruct((len(near_order), rows, coarse), BF16),
         ),
         stay(flat_basis),
         stay(flat_images),
         stay(neighbours),
-        stay(flat_hops),
-        far=(0, 1, 2, 3),
+        far=(0, 1, 2),
         scratch=[
             pltpu.VMEM(neighbours.shape, jnp.int32),
-            pltpu.SemaphoreType.DMA((2 * PIECES + 1 + len(near_order),)),
+            pltpu.SemaphoreType.DMA((2 * PIECES + 1,)),
         ],
     )
-    got0 = send(pay0, core_hop, core_hop)
-    kept0 = call(keep_kernel, shaped(half, nvec, F32), basis_here, images_here)
 
     def fetched(order):
         return call(
@@ -440,9 +456,14 @@
             scratch=[pltpu.SemaphoreType.DMA((len(order),))],
         )
 
+    got0 = send(pay0, core_hop, core_hop)
     middle = len(far_order) // 2
-    far_hops = fetched(far_order[:middle])
-    more_hops = fetched(far_order[middle:])
+    groups = (near_order[:2], near_order[2:] + far_order[:middle], far_order[middle:])
+    spots_of = {hop: (g, i) for g, group in enumerate(groups) for i, hop in enumerate(group)}
+    near_hops = fetched(groups[0])
+    kept0 = call(keep_kernel, shaped(half, nvec, F32), basis_here, images_here)
+    far_hops = fetched(groups[1])
+    more_hops = fetched(groups[2])
     pay1, kept1, pair = call(
         second_kernel,
         (shaped(half + 2 * chunk, nvec, BF16), shaped(half // 2, nvec, F32), shaped(2 * chunk, nvec, BF16)),
@@ -463,15 +484,15 @@
     got2 = send(pay2, z0_hop, x_hop)
     crossed = send(got1[half:, :], core_hop, core_hop)
     total, own = call(
-        functools.partial(near_kernel, near_order),
+        functools.partial(near_kernel, near_order, spots_of),
         (shaped(rows, wide, F32), shaped(coarse, wide, BF16)),
         pair,
         got1,
         crossed,
         near_hops,
+        far_hops,
         perms,
         shift,
-        scratch=[pltpu.VMEM((spots * LANES, wide), BF16)],
     )
     times = []
     if sites > 8:
@@ -487,7 +508,7 @@
     cross = send(cross_pay, core_hop, core_hop)
     got3 = send(pay3, y_hop, z1_hop)
     masked, new = call(
-        functools.partial(far_kernel, nb, blk),
+        functools.partial(far_kernel, nb, blk, spots_of),
         (shaped(rows, wide, BF16), shaped(2 * blk, nvec, BF16)),
         own,
         got2,
@@ -502,7 +523,6 @@
         perms,
         shift,
         *times,
-        scratch=[pltpu.VMEM((3, spots * LANES, wide), BF16)],
     )
     payc = call(join_kernel, shaped(2 * n + 2 * blk, nvec, BF16), kept3, got3, new)
     turned = [pltpu.VMEM((rows, nvec), BF16), pltpu.SemaphoreType.DMA((PIECES,))]
@@ -552,13 +572,27 @@
     )
     n *= 4
     gotc = send(payc, core_hop, core_hop)
+    begun = call(
+        functools.partial(early_kernel, n),
+        shaped(nvec, nvec, F32),
+        payc,
+        out_far=True,
+        scratch=[pltpu.VMEM((n, nvec - LANES), F32), pltpu.SemaphoreType.DMA],
+    )
     projected = call(
         functools.partial(final_kernel, n, blk, scale),
         shaped(nvec, nvec, F32),
         payc,
         gotc,
+        begun,
+        far=(2,),
         out_far=True,
-        scratch=[pltpu.VMEM((nvec, nvec), F32), pltpu.SemaphoreType.DMA((4,))],
+        alias={2: 0},
+        scratch=[
+            pltpu.VMEM((n, nvec - LANES), F32),
+            pltpu.VMEM((nvec, LANES), F32),
+            pltpu.SemaphoreType.DMA((3,)),
+        ],
     )
 
     def back(x):

time: 54.8 us -> 56.4 us (1.029)
  Pallas kernels: 14.6 us -> 16.1 us
    pallas_call x16 -> x18, Pallas kernels: 14.6 us -> 16.1 us  [call(): pl.pallas_call(kernel, out_shape=outs, in_specs=[scalars if i in smem els...]
  transfers between devices with their start and end apart: 13 -> 13, of which waited for: 8 -> 8; matrix products, arithmetic and copies ran while one was open for 0% -> 0% of each run, Pallas kernels for 20% -> 23%
where the time goes in v5:
time: 56.4 us; the launch traced here: 55.7 us
  waiting for transfers between devices  22 us (39%)
  starting transfers between devices  16.8 us (30%)
  Pallas kernels  16.1 us (29%)
  between operations  0.83 us (1%)
    ppermute x13, waiting for transfers between devices, send(): return lax.ppermute(x, BOTH, pairs)  22 us
    ppermute x13, starting transfers between devices, send(): return lax.ppermute(x, BOTH, pairs)  16.8 us
    pallas_call x18, Pallas kernels, call(): pl.pallas_call(kernel, out_shape=outs, in_specs=[scalars if i in smem els...  16.1 us
  transfers between devices with their start and end apart: 13, of which 8 were waited for; matrix products, arithmetic and copies ran while one was open for 0% of the time, Pallas kernels for 23%

profile of v5, /device:TPU:0, one launch (start us, length us, event | category | flops | bytes accessed | tf_op | source)
XLA Modules:
  0.0 55.7 jit_solution(15838346404221471778)
XLA Ops:
  0.6 2.1 %shard_map.76 = (bf16[544,512]{1,0:T(8,128)(2,1)S(1)}, bf16[800,512]{1,0:T(8,128)(2,1)S(1)}, bf16[800,496]{1,0:T(8,128)(2,1)S(1)}, bf16[200,256]{1,0:T(8,128)(2,1)S(1)}, bf16[9,256,128]{2,1,0:T(8,128)(2,1)S(1)}) custom-call(bf16[800,512]{1,0:T(8,128)(2,1)} %bitcast.18, bf16[800,496]{1,0:T(8,128)(2,1)} %bitcast.19, s32[8,8]{1,0:T(8,128)} %table_far.1), custom_call_target="tpu_custom_call" | custom-call | flops 100000000 | bytes 2000000 | tf_op jit(solution)/shard_map/pallas_call | solution.py:62
  2.7 0.6 collective-permute-start
  3.3 0.5 shard_map.77.kept
  3.8 1.1 %collective-permute-done.got = bf16[544,512]{1,0:T(8,128)(2,1)S(1)} collective-permute-done((bf16[544,512]{1,0:T(8,128)(2,1)S(1)}, bf16[544,512]{1,0:T(8,128)(2,1)S(1)}, u32[]{:S(2)}, u32[]{:S(2)}) %collective-permute-start) | collective-permute-done | bytes 557088 | tf_op jit(solution)/shard_map/ppermute | solution.py:420
  4.9 0.2 shard_map.78
  5.1 2.9 %collective-permute-start.1 = (bf16[320,512]{1,0:T(8,128)(2,1)S(1)}, bf16[320,512]{1,0:T(8,128)(2,1)S(1)}, u32[]{:S(2)}, u32[]{:S(2)}) collective-permute-start(bf16[320,512]{1,0:T(8,128)(2,1)S(1)} %get-tuple-element.24), channel_id=1, source_target_pairs={{0,2},{1,5},{2,0},{3,7},{4,6},{5,1},{6,4},{7,3},{8,10},{9,13},{10,... | collective-permute-start | bytes 983048 | tf_op jit(solution)/shard_map/ppermute | solution.py:420
  8.0 0.7 %collective-permute-start.2 = (bf16[64,512]{1,0:T(8,128)(2,1)S(1)}, bf16[64,512]{1,0:T(8,128)(2,1)S(1)}, u32[]{:S(2)}, u32[]{:S(2)}) collective-permute-start(bf16[64,512]{1,0:T(8,128)(2,1)S(1)} %get-tuple-element.25.pair), channel_id=1, source_target_pairs={{1,17},{3,19},{5,21},{7,23},{9,25},{11,27},{13,29},{15,31},{17,1},... | collective-permute-start | bytes 196616 | tf_op jit(solution)/shard_map/ppermute | solution.py:420
  8.6 4.4 %collective-permute-done.1.got.got1 = bf16[320,512]{1,0:T(8,128)(2,1)S(1)} collective-permute-done((bf16[320,512]{1,0:T(8,128)(2,1)S(1)}, bf16[320,512]{1,0:T(8,128)(2,1)S(1)}, u32[]{:S(2)}, u32[]{:S(2)}) %collective-permute-start.1) | collective-permute-done | bytes 327712 | tf_op jit(solution)/shard_map/ppermute | solution.py:420
  13.0 0.1 shard_map.79
  13.1 2.2 %collective-permute-start.3 = (bf16[256,512]{1,0:T(8,128)(2,1)S(1)}, bf16[256,512]{1,0:T(8,128)(2,1)S(1)}, u32[]{:S(2)}, u32[]{:S(2)}) collective-permute-start(bf16[256,512]{1,0:T(8,128)(2,1)S(1)} %get-tuple-element.27), channel_id=1, source_target_pairs={{0,8},{1,3},{2,10},{3,1},{4,12},{5,7},{6,14},{7,5},{8,0},{9,11},{1... | collective-permute-start | bytes 786440 | tf_op jit(solution)/shard_map/ppermute | solution.py:420
  15.3 4.4 %collective-permute-done.3.got.got2 = bf16[256,512]{1,0:T(8,128)(2,1)S(1)} collective-permute-done((bf16[256,512]{1,0:T(8,128)(2,1)S(1)}, bf16[256,512]{1,0:T(8,128)(2,1)S(1)}, u32[]{:S(2)}, u32[]{:S(2)}) %collective-permute-start.3) | collective-permute-done | bytes 262176 | tf_op jit(solution)/shard_map/ppermute | solution.py:420
  19.7 0.1 collective-permute-start.6
  19.8 0.5 collective-permute-start.5
  20.3 2.0 %collective-permute-start.4 = (bf16[64,512]{1,0:T(8,128)(2,1)S(1)}, bf16[64,512]{1,0:T(8,128)(2,1)S(1)}, u32[]{:S(2)}, u32[]{:S(2)}) collective-permute-start(bf16[64,512]{1,0:T(8,128)(2,1)S(1)} %get-tuple-element.29), channel_id=1, source_target_pairs={{0,4},{1,17},{2,6},{3,19},{4,0},{5,21},{6,2},{7,23},{8,12},{9,25},... | collective-permute-start | bytes 196616 | tf_op jit(solution)/shard_map/ppermute | solution.py:420
  22.2 1.4 %shard_map.81.hops = bf16[2,800,400]{2,1,0:T(8,128)(2,1)S(1)} custom-call(bf16[9,800,400]{2,1,0:T(8,128)(2,1)} %bitcast.15), custom_call_target="tpu_custom_call" | custom-call | flops 100000000 | bytes 2000000 | tf_op jit(solution)/shard_map/pallas_call | solution.py:62
  23.6 1.9 %shard_map.82.more.hops = bf16[4,800,400]{2,1,0:T(8,128)(2,1)S(1)} custom-call(bf16[9,800,400]{2,1,0:T(8,128)(2,1)} %bitcast.16), custom_call_target="tpu_custom_call" | custom-call | flops 100000000 | bytes 2000000 | tf_op jit(solution)/shard_map/pallas_call | solution.py:62
  25.6 1.7 %shard_map.84.more = bf16[3,800,400]{2,1,0:T(8,128)(2,1)S(1)} custom-call(bf16[9,800,400]{2,1,0:T(8,128)(2,1)} %bitcast.17), custom_call_target="tpu_custom_call" | custom-call | flops 100000000 | bytes 2000000 | tf_op jit(solution)/shard_map/pallas_call | solution.py:62
  27.3 1.2 %shard_map.83 = (f32[800,128]{1,0:T(8,128)S(1)}, bf16[400,128]{1,0:T(8,128)(2,1)S(1)}) custom-call(bf16[64,512]{1,0:T(8,128)(2,1)S(1)} %get-tuple-element.25.pair, bf16[320,512]{1,0:T(8,128)(2,1)S(1)} %collective-permute-done.1.got.got1, bf16[64,512]{1,0:T(8,128)(2,1)S(1)} %collective-permute-done.5.crossed, bf16[2,800,400]{2,1,0:T(8,128)(2,1)S(1)} %shard_map.81.hops, ...), custom_call_target="tpu_custom_call" | custom-call | flops 100000000 | bytes 2000000 | tf_op jit(solution)/shard_map/pallas_call | solution.py:62
  28.5 2.3 %shard_map.85 = (bf16[800,128]{1,0:T(8,128)(2,1)S(1)}, bf16[32,512]{1,0:T(8,128)(2,1)S(1)}) custom-call(bf16[400,128]{1,0:T(8,128)(2,1)S(1)} %get-tuple-element.32.own, bf16[256,512]{1,0:T(8,128)(2,1)S(1)} %collective-permute-done.3.got.got2, bf16[192,512]{1,0:T(8,128)(2,1)S(1)} %collective-permute-done.6.cross, ...), custom_call_target="tpu_custom_call" | custom-call | flops 100000000 | bytes 2000000 | tf_op jit(solution)/shard_map/pallas_call | solution.py:62
  30.8 2.7 %collective-permute-start.7 = (bf16[96,512]{1,0:T(8,128)(2,1)S(1)}, bf16[96,512]{1,0:T(8,128)(2,1)S(1)}, u32[]{:S(2)}, u32[]{:S(2)}) collective-permute-start(bf16[96,512]{1,0:T(8,128)(2,1)S(1)} %shard_map.86.pay), channel_id=1, source_target_pairs={{0,16},{1,9},{2,18},{3,11},{4,20},{5,13},{6,22},{7,15},{8,24},{9,1... | collective-permute-start | bytes 294920 | tf_op jit(solution)/shard_map/ppermute | solution.py:420
  33.5 3.0 %collective-permute-done.7.got = bf16[96,512]{1,0:T(8,128)(2,1)S(1)} collective-permute-done((bf16[96,512]{1,0:T(8,128)(2,1)S(1)}, bf16[96,512]{1,0:T(8,128)(2,1)S(1)}, u32[]{:S(2)}, u32[]{:S(2)}) %collective-permute-start.7) | collective-permute-done | bytes 98336 | tf_op jit(solution)/shard_map/ppermute | solution.py:420
  36.5 0.7 %collective-permute-start.8 = (bf16[64,512]{1,0:T(8,128)(2,1)S(1)}, bf16[64,512]{1,0:T(8,128)(2,1)S(1)}, u32[]{:S(2)}, u32[]{:S(2)}) collective-permute-start(bf16[64,512]{1,0:T(8,128)(2,1)S(1)} %shard_map.87.pay), channel_id=1, source_target_pairs={{0,4},{1,17},{2,6},{3,19},{4,0},{5,21},{6,2},{7,23},{8,12},{9,25},... | collective-permute-start | bytes 196616 | tf_op jit(solution)/shard_map/ppermute | solution.py:420
  37.2 3.7 %collective-permute-done.8.got = bf16[64,512]{1,0:T(8,128)(2,1)S(1)} collective-permute-done((bf16[64,512]{1,0:T(8,128)(2,1)S(1)}, bf16[64,512]{1,0:T(8,128)(2,1)S(1)}, u32[]{:S(2)}, u32[]{:S(2)}) %collective-permute-start.8) | collective-permute-done | bytes 65568 | tf_op jit(solution)/shard_map/ppermute | solution.py:420
  40.9 3.1 %collective-permute-start.9 = (bf16[96,512]{1,0:T(8,128)(2,1)S(1)}, bf16[96,512]{1,0:T(8,128)(2,1)S(1)}, u32[]{:S(2)}, u32[]{:S(2)}) collective-permute-start(bf16[96,512]{1,0:T(8,128)(2,1)S(1)} %shard_map.88.pay), channel_id=1, source_target_pairs={{0,8},{1,3},{2,10},{3,1},{4,12},{5,7},{6,14},{7,5},{8,0},{9,11},{1... | collective-permute-start | bytes 294920 | tf_op jit(solution)/shard_map/ppermute | solution.py:420
  43.9 1.5 %collective-permute-start.10 = (bf16[96,512]{1,0:T(8,128)(2,1)S(1)}, bf16[96,512]{1,0:T(8,128)(2,1)S(1)}, u32[]{:S(2)}, u32[]{:S(2)}) collective-permute-start(bf16[96,512]{1,0:T(8,128)(2,1)S(1)} %shard_map.88.pay), channel_id=1, source_target_pairs={{0,2},{1,5},{2,0},{3,7},{4,6},{5,1},{6,4},{7,3},{8,10},{9,13},{10,... | collective-permute-start | bytes 294920 | tf_op jit(solution)/shard_map/ppermute | solution.py:420
  45.5 1.1 %collective-permute-done.9.got_a = bf16[96,512]{1,0:T(8,128)(2,1)S(1)} collective-permute-done((bf16[96,512]{1,0:T(8,128)(2,1)S(1)}, bf16[96,512]{1,0:T(8,128)(2,1)S(1)}, u32[]{:S(2)}, u32[]{:S(2)}) %collective-permute-start.9) | collective-permute-done | bytes 98336 | tf_op jit(solution)/shard_map/ppermute | solution.py:420
  46.5 2.0 %collective-permute-done.10.got_b = bf16[96,512]{1,0:T(8,128)(2,1)S(1)} collective-permute-done((bf16[96,512]{1,0:T(8,128)(2,1)S(1)}, bf16[96,512]{1,0:T(8,128)(2,1)S(1)}, u32[]{:S(2)}, u32[]{:S(2)}) %collective-permute-start.10) | collective-permute-done | bytes 98336 | tf_op jit(solution)/shard_map/ppermute | solution.py:420
  48.5 2.4 %collective-permute-done.11.got_ab = bf16[96,512]{1,0:T(8,128)(2,1)S(1)} collective-permute-done((bf16[96,512]{1,0:T(8,128)(2,1)S(1)}, bf16[96,512]{1,0:T(8,128)(2,1)S(1)}, u32[]{:S(2)}, u32[]{:S(2)}) %collective-permute-start.11) | collective-permute-done | bytes 98336 | tf_op jit(solution)/shard_map/ppermute | solution.py:420
  51.1 1.4 %shard_map.92 = bf16[800,512]{1,0:T(8,128)(2,1)} custom-call(bf16[800,512]{1,0:T(8,128)(2,1)S(1)} %get-tuple-element.20.basis, bf16[512,512]{1,0:T(8,128)(2,1)S(1)} %copy-done), custom_call_target="tpu_custom_call" | custom-call | flops 100000000 | bytes 2000000 | tf_op jit(solution)/shard_map/pallas_call | solution.py:62
  52.4 1.6 %shard_map.93 = bf16[800,512]{1,0:T(8,128)(2,1)} custom-call(bf16[800,496]{1,0:T(8,128)(2,1)S(1)} %get-tuple-element.21.images, bf16[800,128]{1,0:T(8,128)(2,1)S(1)} %get-tuple-element.36.masked, bf16[512,512]{1,0:T(8,128)(2,1)S(1)} %copy-done), custom_call_target="tpu_custom_call" | custom-call | flops 100000000 | bytes 2000000 | tf_op jit(solution)/shard_map/pallas_call | solution.py:62
  54.0 0.8 %shard_map.90.begun = f32[512,512]{1,0:T(8,128)} custom-call(bf16[288,512]{1,0:T(8,128)(2,1)S(1)} %shard_map.89.pay), custom_call_target="tpu_custom_call" | custom-call | flops 100000000 | bytes 2000000 | tf_op jit(solution)/shard_map/pallas_call | solution.py:62
  54.8 0.9 %shard_map.91 = f32[512,512]{1,0:T(8,128)} custom-call(bf16[288,512]{1,0:T(8,128)(2,1)S(1)} %shard_map.89.pay, bf16[288,512]{1,0:T(8,128)(2,1)S(1)} %collective-permute-done.12.got, f32[512,512]{1,0:T(8,128)} %shard_map.90.begun), custom_call_target="tpu_custom_call", output_to_operand_aliasing={{}: (2, {})} | custom-call | flops 100000000 | bytes 2000000 | tf_op jit(solution)/shard_map/pallas_call | solution.py:62
  (15 shorter events, 0.3 us)
Async XLA Ops:
  2.7 2.1 %collective-permute-start = (bf16[544,512]{1,0:T(8,128)(2,1)S(1)}, bf16[544,512]{1,0:T(8,128)(2,1)S(1)}, u32[]{:S(2)}, u32[]{:S(2)}) collective-permute-start(bf16[544,512]{1,0:T(8,128)(2,1)S(1)} %get-tuple-element.22.pay), channel_id=1, source_target_pairs={{0,1},{1,0},{2,3},{3,2},{4,5},{5,4},{6,7},{7,6},{8,9},{9,8},{10,11... | collective-permute-start | bytes 1671176 | tf_op jit(solution)/shard_map/ppermute | solution.py:420
  5.1 8.0 %collective-permute-start.1 = (bf16[320,512]{1,0:T(8,128)(2,1)S(1)}, bf16[320,512]{1,0:T(8,128)(2,1)S(1)}, u32[]{:S(2)}, u32[]{:S(2)}) collective-permute-start(bf16[320,512]{1,0:T(8,128)(2,1)S(1)} %get-tuple-element.24), channel_id=1, source_target_pairs={{0,2},{1,5},{2,0},{3,7},{4,6},{5,1},{6,4},{7,3},{8,10},{9,13},{10,... | collective-permute-start | bytes 983048 | tf_op jit(solution)/shard_map/ppermute | solution.py:420
  8.0 0.7 %collective-permute-start.2 = (bf16[64,512]{1,0:T(8,128)(2,1)S(1)}, bf16[64,512]{1,0:T(8,128)(2,1)S(1)}, u32[]{:S(2)}, u32[]{:S(2)}) collective-permute-start(bf16[64,512]{1,0:T(8,128)(2,1)S(1)} %get-tuple-element.25.pair), channel_id=1, source_target_pairs={{1,17},{3,19},{5,21},{7,23},{9,25},{11,27},{13,29},{15,31},{17,1},... | collective-permute-start | bytes 196616 | tf_op jit(solution)/shard_map/ppermute | solution.py:420
  13.1 6.5 %collective-permute-start.3 = (bf16[256,512]{1,0:T(8,128)(2,1)S(1)}, bf16[256,512]{1,0:T(8,128)(2,1)S(1)}, u32[]{:S(2)}, u32[]{:S(2)}) collective-permute-start(bf16[256,512]{1,0:T(8,128)(2,1)S(1)} %get-tuple-element.27), channel_id=1, source_target_pairs={{0,8},{1,3},{2,10},{3,1},{4,12},{5,7},{6,14},{7,5},{8,0},{9,11},{1... | collective-permute-start | bytes 786440 | tf_op jit(solution)/shard_map/ppermute | solution.py:420
  19.7 8.8 %collective-permute-start.6 = (bf16[192,512]{1,0:T(8,128)(2,1)S(1)}, bf16[192,512]{1,0:T(8,128)(2,1)S(1)}, u32[]{:S(2)}, u32[]{:S(2)}) collective-permute-start(bf16[192,512]{1,0:T(8,128)(2,1)S(1)} %get-tuple-element.33), channel_id=1, source_target_pairs={{0,1},{1,0},{2,3},{3,2},{4,5},{5,4},{6,7},{7,6},{8,9},{9,8},{10,11... | collective-permute-start | bytes 589832 | tf_op jit(solution)/shard_map/ppermute | solution.py:420
  19.8 7.5 %collective-permute-start.5 = (bf16[64,512]{1,0:T(8,128)(2,1)S(1)}, bf16[64,512]{1,0:T(8,128)(2,1)S(1)}, u32[]{:S(2)}, u32[]{:S(2)}) collective-permute-start(bf16[64,512]{1,0:T(8,128)(2,1)S(1)} %slice.4), channel_id=1, source_target_pairs={{0,1},{1,0},{2,3},{3,2},{4,5},{5,4},{6,7},{7,6},{8,9},{9,8},{10,11... | collective-permute-start | bytes 196616 | tf_op jit(solution)/shard_map/ppermute | solution.py:420
  20.3 10.5 %collective-permute-start.4 = (bf16[64,512]{1,0:T(8,128)(2,1)S(1)}, bf16[64,512]{1,0:T(8,128)(2,1)S(1)}, u32[]{:S(2)}, u32[]{:S(2)}) collective-permute-start(bf16[64,512]{1,0:T(8,128)(2,1)S(1)} %get-tuple-element.29), channel_id=1, source_target_pairs={{0,4},{1,17},{2,6},{3,19},{4,0},{5,21},{6,2},{7,23},{8,12},{9,25},... | collective-permute-start | bytes 196616 | tf_op jit(solution)/shard_map/ppermute | solution.py:420
  28.4 22.6 %copy-start = (bf16[512,512]{1,0:T(8,128)(2,1)S(1)}, bf16[512,512]{1,0:T(8,128)(2,1)}, u32[]{:S(2)}) copy-start(bf16[512,512]{1,0:T(8,128)(2,1)} %rotation.3) | copy-start | bytes 1572868
  30.8 5.6 %collective-permute-start.7 = (bf16[96,512]{1,0:T(8,128)(2,1)S(1)}, bf16[96,512]{1,0:T(8,128)(2,1)S(1)}, u32[]{:S(2)}, u32[]{:S(2)}) collective-permute-start(bf16[96,512]{1,0:T(8,128)(2,1)S(1)} %shard_map.86.pay), channel_id=1, source_target_pairs={{0,16},{1,9},{2,18},{3,11},{4,20},{5,13},{6,22},{7,15},{8,24},{9,1... | collective-permute-start | bytes 294920 | tf_op jit(solution)/shard_map/ppermute | solution.py:420
  36.5 4.3 %collective-permute-start.8 = (bf16[64,512]{1,0:T(8,128)(2,1)S(1)}, bf16[64,512]{1,0:T(8,128)(2,1)S(1)}, u32[]{:S(2)}, u32[]{:S(2)}) collective-permute-start(bf16[64,512]{1,0:T(8,128)(2,1)S(1)} %shard_map.87.pay), channel_id=1, source_target_pairs={{0,4},{1,17},{2,6},{3,19},{4,0},{5,21},{6,2},{7,23},{8,12},{9,25},... | collective-permute-start | bytes 196616 | tf_op jit(solution)/shard_map/ppermute | solution.py:420
  40.9 5.7 %collective-permute-start.9 = (bf16[96,512]{1,0:T(8,128)(2,1)S(1)}, bf16[96,512]{1,0:T(8,128)(2,1)S(1)}, u32[]{:S(2)}, u32[]{:S(2)}) collective-permute-start(bf16[96,512]{1,0:T(8,128)(2,1)S(1)} %shard_map.88.pay), channel_id=1, source_target_pairs={{0,8},{1,3},{2,10},{3,1},{4,12},{5,7},{6,14},{7,5},{8,0},{9,11},{1... | collective-permute-start | bytes 294920 | tf_op jit(solution)/shard_map/ppermute | solution.py:420
  43.9 4.6 %collective-permute-start.10 = (bf16[96,512]{1,0:T(8,128)(2,1)S(1)}, bf16[96,512]{1,0:T(8,128)(2,1)S(1)}, u32[]{:S(2)}, u32[]{:S(2)}) collective-permute-start(bf16[96,512]{1,0:T(8,128)(2,1)S(1)} %shard_map.88.pay), channel_id=1, source_target_pairs={{0,2},{1,5},{2,0},{3,7},{4,6},{5,1},{6,4},{7,3},{8,10},{9,13},{10,... | collective-permute-start | bytes 294920 | tf_op jit(solution)/shard_map/ppermute | solution.py:420
  45.4 5.5 %collective-permute-start.11 = (bf16[96,512]{1,0:T(8,128)(2,1)S(1)}, bf16[96,512]{1,0:T(8,128)(2,1)S(1)}, u32[]{:S(2)}, u32[]{:S(2)}) collective-permute-start(bf16[96,512]{1,0:T(8,128)(2,1)S(1)} %shard_map.88.pay), channel_id=1, source_target_pairs={{0,10},{1,7},{2,8},{3,5},{4,14},{5,3},{6,12},{7,1},{8,2},{9,15},{1... | collective-permute-start | bytes 294920 | tf_op jit(solution)/shard_map/ppermute | solution.py:420
  51.0 3.8 %collective-permute-start.12 = (bf16[288,512]{1,0:T(8,128)(2,1)S(1)}, bf16[288,512]{1,0:T(8,128)(2,1)S(1)}, u32[]{:S(2)}, u32[]{:S(2)}) collective-permute-start(bf16[288,512]{1,0:T(8,128)(2,1)S(1)} %shard_map.89.pay), channel_id=1, source_target_pairs={{0,1},{1,0},{2,3},{3,2},{4,5},{5,4},{6,7},{7,6},{8,9},{9,8},{10,11... | collective-permute-start | bytes 884744 | tf_op jit(solution)/shard_map/ppermute | solution.py:420

commit v6 on v5

--- a/solution.py
+++ b/solution.py
@@ -185,13 +185,14 @@
     out[2 * n :, :] = pair[...]
 
 
-def third_kernel(kept, got, pair, far, out, rest):
-    core, half, _, z0, _ = place()
+def third_kernel(kept, got, pair, far, out, side_out, both_out, rest):
+    core, half, y, z0, z1 = place()
     whole = kept.shape[0]
-    n = whole // 2
-    bit = pick(core, z0, half)
-    out[:n, :], out[n : 2 * n, :] = split(joined(kept, got, (1 - bit) * n, n))
-    rest[...] = joined(kept, got, bit * n, n)
+    n = whole // 4
+    b, a = pick(core, z0, half), pick(core, y, z1)
+    for target, spot in ((out, 2 * (1 - b) + a), (side_out, 2 * b + 1 - a), (both_out, 2 * (1 - b) + 1 - a)):
+        target[:n, :], target[n : 2 * n, :] = split(joined(kept, got, spot * n, n))
+    rest[...] = joined(kept, got, (2 * b + a) * n, n)
     each = pair.shape[0]
     at = pick(core, 1 - half, 0)
     out[pl.ds(pl.multiple_of(2 * n + at * each, each), each), :] = got[2 * whole :, :]
@@ -200,15 +201,9 @@
     )
 
 
-def fourth_kernel(kept, got, far, out, rest, cross):
-    core, _, y, _, z1 = place()
-    whole = kept.shape[0]
-    n = whole // 2
-    bit = pick(core, y, z1)
-    out[:n, :], out[n:, :] = split(joined(kept, got, (1 - bit) * n, n))
-    rest[...] = joined(kept, got, bit * n, n)
-    area = got.shape[0] - 2 * whole
-    cross[:area, :] = got[2 * whole :, :]
+def fourth_kernel(got, far, cross):
+    area = cross.shape[0] - far.shape[0]
+    cross[:area, :] = got[got.shape[0] - area :, :]
     cross[area:, :] = far[...]
 
 
@@ -245,7 +240,14 @@
     return jnp.concatenate([low, high], axis=0).astype(BF16)
 
 
-def near_kernel(order, spots_of, pair, got, crossed, hops, more, perms, shift, total, own_out):
+def pulled(order, far, near, sems):
+    copies = [pltpu.make_async_copy(far.at[hop], near.at[i], sems.at[i]) for i, hop in enumerate(order)]
+    for copy in copies:
+        copy.start()
+    return copies
+
+
+def near_kernel(here, later, pair, got, crossed, hops, more, perms, shift, total, own_out):
     core, half, _, _, _ = place()
     each = pair.shape[0]
     wide = own_out.shape[1]
@@ -254,19 +256,48 @@
     own = ordered(half, half_site(shift[...], pair[...]), half_site(shift[...], apart))
     own_out[...] = own
     rows = total.shape[0]
-    mixed = [dot_nn(own, perms[hop, :wide, :]).astype(BF16) for hop in order]
+    terms = [(hops, i, hop) for i, hop in enumerate(here)]
+    terms += [(more, more.shape[0] - len(later) + i, hop) for i, hop in enumerate(later)]
+    mixed = [dot_nn(own, perms[hop, :wide, :]).astype(BF16) for _, _, hop in terms]
     step = rows // 2
     for r in range(2):
         span = pl.ds(r * step, step)
         part = None
-        for i, hop in enumerate(order):
-            group, at = spots_of[hop]
-            piece = dot_nn((hops, more)[group][at, span, :], mixed[i])
+        for (source, at, _), term in zip(terms, mixed):
+            piece = dot_nn(source[at, span, :], term)
             part = piece if part is None else part + piece
         total[span, :] = part
 
 
-def far_kernel(nb, blk, spots_of, own, got2, cross, far, got1, crossed, total, basis, hops, more, perms, shift, *refs):
+def mixture(perms, own, site, hop):
+    return dot_nn(jnp.concatenate([own[...], site], axis=1), perms[hop]).astype(BF16)
+
+
+def middle_kernel(ahead, own, got2, got1, total, hops, hops_far, perms, shift, out, next_hops, sems):
+    copies = pulled(ahead, hops_far, next_hops, sems)
+    core, half, _, _, _ = place()
+    first = core == 0
+    each = 2 * LANES * LANES // got2.shape[1]
+    mine = got2[got2.shape[0] - 2 * each :, :]
+    move = shift[...]
+    site = ordered(
+        pick(core, 0, half),
+        half_site(move, jnp.where(first, mine[:each], got1[got1.shape[0] - each :, :])),
+        half_site(move, jnp.where(first, mine[each:], mine[:each])),
+    )
+    mixed = [mixture(perms, own, site, 2 + core + 3 * i) for i in range(2)]
+    step = out.shape[0] // 2
+    for r in range(2):
+        span = pl.ds(r * step, step)
+        part = total[span, :]
+        for i in range(2):
+            part = part + dot_nn(hops[2 * core + i, span, :], mixed[i])
+        out[span, :] = part
+    for copy in copies:
+        copy.wait()
+
+
+def far_kernel(nb, blk, order, own, got2, cross, far, crossed, total, basis, hops, more, perms, shift, *refs):
     times, (masked, new_out) = refs[:-2], refs[-2:]
     core, half, _, _, _ = place()
     each = far.shape[0]
@@ -276,36 +307,28 @@
     first = core == 0
     mine = got2[got2.shape[0] - 2 * each :, :]
     theirs = cross[: 2 * each, :]
-    sites = []
-    one = jnp.where(first, theirs, mine)
-    two = jnp.where(first, mine, theirs)
     move = shift[...]
-    near_site = ordered(
-        half,
-        half_site(move, jnp.where(first, crossed[...], got1[got1.shape[0] - each :, :])),
-        half_site(move, one[:each]),
+    site = ordered(
+        pick(core, half, 0),
+        half_site(move, jnp.where(first, crossed[...], theirs[:each])),
+        half_site(move, jnp.where(first, theirs[:each], theirs[each:])),
     )
     long_site = ordered(
         half,
         half_site(move, jnp.where(first, cross[2 * each :, :], far[...])),
-        half_site(move, one[each:]),
-    )
-    mid_site = ordered(0, half_site(move, two[:each]), half_site(move, two[each:]))
-    sites = {1: long_site, 4: long_site, 2: mid_site, 5: mid_site, 3: near_site, 6: near_site}
-    for k, ref in enumerate(times):
-        sites[7 + k] = ref[...]
-    order = sorted(sites)
-    mixed = [
-        dot_nn(jnp.concatenate([own[...], sites[hop]], axis=1), perms[hop]).astype(BF16) for hop in order
-    ]
+        half_site(move, jnp.where(first, theirs[each:], mine[each:])),
+    )
+    terms = [(more, 2 * (1 - core) + i, mixture(perms, own, site, 3 - core + 3 * i)) for i in range(2)]
+    for i, hop in enumerate(order):
+        term = long_site if hop in (1, 4) else times[hop - 7][...]
+        terms.append((hops, i, mixture(perms, own, term, hop)))
     step = rows // 2
     sums = jnp.zeros((wide, nvec), F32)
     for r in range(2):
         span = pl.ds(r * step, step)
         part = total[span, :]
-        for i, hop in enumerate(order):
-            group, at = spots_of[hop]
-            part = part + dot_nn((None, hops, more)[group][at, span, :], mixed[i])
+        for source, at, mixed in terms:
+            part = part + dot_nn(source[at, span, :], mixed)
         row = lax.broadcasted_iota(jnp.int32, (step, wide), 0)
         col = lax.broadcasted_iota(jnp.int32, (step, wide), 1)
         chosen = jnp.where(lax.rem(row, nb) == lax.div(col, blk), part, 0.0).astype(BF16)
@@ -317,9 +340,9 @@
     new_out[:blk, :], new_out[blk:, :] = split(new)
 
 
-def join_kernel(kept, got, new, out):
+def join_kernel(kept, got_b, got_a, got_ab, new, out):
     n = kept.shape[0]
-    total = kept[...] + (got[:n, :].astype(F32) + got[n:, :].astype(F32))
+    total = kept[...] + value(got_b, 0, n) + (value(got_a, 0, n) + value(got_ab, 0, n))
     out[:n, :], out[n : 2 * n, :] = split(total)
     out[2 * n :, :] = new[...]
 
@@ -457,13 +480,10 @@
         )
 
     got0 = send(pay0, core_hop, core_hop)
-    middle = len(far_order) // 2
-    groups = (near_order[:2], near_order[2:] + far_order[:middle], far_order[middle:])
-    spots_of = {hop: (g, i) for g, group in enumerate(groups) for i, hop in enumerate(group)}
+    groups = (near_order[:2], [2, 5, 3, 6] + near_order[2:], near_order[2:], [hop for hop in far_order if hop in (1, 4, 7, 8)])
     near_hops = fetched(groups[0])
     kept0 = call(keep_kernel, shaped(half, nvec, F32), basis_here, images_here)
-    far_hops = fetched(groups[1])
-    more_hops = fetched(groups[2])
+    more_hops = fetched(groups[1])
     pay1, kept1, pair = call(
         second_kernel,
         (shaped(half + 2 * chunk, nvec, BF16), shaped(half // 2, nvec, F32), shaped(2 * chunk, nvec, BF16)),
@@ -473,9 +493,14 @@
     )
     got1 = send(pay1, x_hop, y_hop)
     far = send(pair, 0, z1_hop)
-    pay2, kept2 = call(
+    pay2, pay_a, pay_ab, kept2 = call(
         third_kernel,
-        (shaped(half // 2 + 4 * chunk, nvec, BF16), shaped(half // 4, nvec, F32)),
+        (
+            shaped(2 * n + 4 * chunk, nvec, BF16),
+            shaped(2 * n, nvec, BF16),
+            shaped(2 * n, nvec, BF16),
+            shaped(n, nvec, F32),
+        ),
         kept1,
         got1,
         pair,
@@ -484,13 +509,16 @@
     got2 = send(pay2, z0_hop, x_hop)
     crossed = send(got1[half:, :], core_hop, core_hop)
     total, own = call(
-        functools.partial(near_kernel, near_order, spots_of),
-        (shaped(rows, wide, F32), shaped(coarse, wide, BF16)),
+        functools.partial(near_kernel, groups[0], groups[2]),
+        (
+            shaped(rows, wide, F32),
+            shaped(coarse, wide, BF16),
+        ),
         pair,
         got1,
         crossed,
         near_hops,
-        far_hops,
+        more_hops,
         perms,
         shift,
     )
@@ -498,33 +526,41 @@
     if sites > 8:
         gap = 8 * spots
         times = [lax.ppermute(own, BOTH, [((d + sign * gap) % count, d) for d in range(count)]) for sign in (1, -1)]
-    pay3, kept3, cross_pay = call(
-        fourth_kernel,
-        (shaped(half // 4, nvec, BF16), shaped(half // 8, nvec, F32), shaped(6 * chunk, nvec, BF16)),
-        kept2,
+    got_a = send(pay_a, y_hop, z1_hop)
+    got_ab = send(pay_ab, y_hop + z0_hop, z1_hop + x_hop)
+    cross_pay = call(fourth_kernel, shaped(6 * chunk, nvec, BF16), got2, far)
+    cross = send(cross_pay, core_hop, core_hop)
+    total, next_hops = call(
+        functools.partial(middle_kernel, groups[3]),
+        (shaped(rows, wide, F32), jax.ShapeDtypeStruct((len(groups[3]), rows, coarse), BF16)),
+        own,
         got2,
-        far,
-    )
-    cross = send(cross_pay, core_hop, core_hop)
-    got3 = send(pay3, y_hop, z1_hop)
+        got1,
+        total,
+        more_hops,
+        stay(flat_hops),
+        perms,
+        shift,
+        far=(5,),
+        scratch=[pltpu.SemaphoreType.DMA((len(groups[3]),))],
+    )
     masked, new = call(
-        functools.partial(far_kernel, nb, blk, spots_of),
+        functools.partial(far_kernel, nb, blk, groups[3]),
         (shaped(rows, wide, BF16), shaped(2 * blk, nvec, BF16)),
         own,
         got2,
         cross,
         far,
-        got1,
         crossed,
         total,
         basis_here,
-        far_hops,
+        next_hops,
         more_hops,
         perms,
         shift,
         *times,
     )
-    payc = call(join_kernel, shaped(2 * n + 2 * blk, nvec, BF16), kept3, got3, new)
+    payc = call(join_kernel, shaped(2 * n + 2 * blk, nvec, BF16), kept2, got2, got_a, got_ab, new)
     turned = [pltpu.VMEM((rows, nvec), BF16), pltpu.SemaphoreType.DMA((PIECES,))]
     gotc = send(payc, z1_hop, z0_hop)
     turned_images = call(

time: 56.4 us -> 54.3 us (0.963)
  waiting for transfers between devices: 22 us -> 19.3 us
  starting transfers between devices: 16.8 us -> 18.5 us
  Pallas kernels: 16.1 us -> 15.5 us
    ppermute x13 -> x14, waiting for transfers between devices: 22 us -> 19.3 us  [send(): return lax.ppermute(x, BOTH, pairs)]
    ppermute x13 -> x14, starting transfers between devices: 16.8 us -> 18.5 us  [send(): return lax.ppermute(x, BOTH, pairs)]
    pallas_call x18, Pallas kernels: 16.1 us -> 15.5 us  [call(): pl.pallas_call(kernel, out_shape=outs, in_specs=[scalars if i in smem els...]
  transfers between devices with their start and end apart: 13 -> 14, of which waited for: 8 -> 8; matrix products, arithmetic and copies ran while one was open for 0% -> 0% of each run, Pallas kernels for 23% -> 22%
where the time goes in v6:
time: 54.3 us; the launch traced here: 54.1 us
  waiting for transfers between devices  19.3 us (36%)
  starting transfers between devices  18.5 us (34%)
  Pallas kernels  15.5 us (29%)
  between operations  0.84 us (2%)
    ppermute x14, waiting for transfers between devices, send(): return lax.ppermute(x, BOTH, pairs)  19.3 us
    ppermute x14, starting transfers between devices, send(): return lax.ppermute(x, BOTH, pairs)  18.5 us
    pallas_call x18, Pallas kernels, call(): pl.pallas_call(kernel, out_shape=outs, in_specs=[scalars if i in smem els...  15.5 us
  transfers between devices with their start and end apart: 14, of which 8 were waited for; matrix products, arithmetic and copies ran while one was open for 0% of the time, Pallas kernels for 22%

profile of v6, /device:TPU:0, one launch (start us, length us, event | category | flops | bytes accessed | tf_op | source)
XLA Modules:
  0.0 54.1 jit_solution(15334933124633802230)
XLA Ops:
  0.6 2.1 %shard_map.76 = (bf16[544,512]{1,0:T(8,128)(2,1)S(1)}, bf16[800,512]{1,0:T(8,128)(2,1)S(1)}, bf16[800,496]{1,0:T(8,128)(2,1)S(1)}, bf16[200,256]{1,0:T(8,128)(2,1)S(1)}, bf16[9,256,128]{2,1,0:T(8,128)(2,1)S(1)}) custom-call(bf16[800,512]{1,0:T(8,128)(2,1)} %bitcast.18, bf16[800,496]{1,0:T(8,128)(2,1)} %bitcast.19, s32[8,8]{1,0:T(8,128)} %table_far.1), custom_call_target="tpu_custom_call" | custom-call | flops 100000000 | bytes 2000000 | tf_op jit(solution)/shard_map/pallas_call | solution.py:62
  2.7 0.6 %collective-permute-start = (bf16[544,512]{1,0:T(8,128)(2,1)S(1)}, bf16[544,512]{1,0:T(8,128)(2,1)S(1)}, u32[]{:S(2)}, u32[]{:S(2)}) collective-permute-start(bf16[544,512]{1,0:T(8,128)(2,1)S(1)} %get-tuple-element.23.pay), channel_id=1, source_target_pairs={{0,1},{1,0},{2,3},{3,2},{4,5},{5,4},{6,7},{7,6},{8,9},{9,8},{10,11... | collective-permute-start | bytes 1671176 | tf_op jit(solution)/shard_map/ppermute | solution.py:443
  3.3 0.5 shard_map.77.kept
  3.8 1.1 %collective-permute-done.got = bf16[544,512]{1,0:T(8,128)(2,1)S(1)} collective-permute-done((bf16[544,512]{1,0:T(8,128)(2,1)S(1)}, bf16[544,512]{1,0:T(8,128)(2,1)S(1)}, u32[]{:S(2)}, u32[]{:S(2)}) %collective-permute-start) | collective-permute-done | bytes 557088 | tf_op jit(solution)/shard_map/ppermute | solution.py:443
  4.9 0.2 shard_map.78
  5.1 2.9 %collective-permute-start.1 = (bf16[320,512]{1,0:T(8,128)(2,1)S(1)}, bf16[320,512]{1,0:T(8,128)(2,1)S(1)}, u32[]{:S(2)}, u32[]{:S(2)}) collective-permute-start(bf16[320,512]{1,0:T(8,128)(2,1)S(1)} %get-tuple-element.25), channel_id=1, source_target_pairs={{0,2},{1,5},{2,0},{3,7},{4,6},{5,1},{6,4},{7,3},{8,10},{9,13},{10,... | collective-permute-start | bytes 983048 | tf_op jit(solution)/shard_map/ppermute | solution.py:443
  8.0 0.7 %collective-permute-start.2 = (bf16[64,512]{1,0:T(8,128)(2,1)S(1)}, bf16[64,512]{1,0:T(8,128)(2,1)S(1)}, u32[]{:S(2)}, u32[]{:S(2)}) collective-permute-start(bf16[64,512]{1,0:T(8,128)(2,1)S(1)} %get-tuple-element.26.pair), channel_id=1, source_target_pairs={{1,17},{3,19},{5,21},{7,23},{9,25},{11,27},{13,29},{15,31},{17,1},... | collective-permute-start | bytes 196616 | tf_op jit(solution)/shard_map/ppermute | solution.py:443
  8.6 4.4 %collective-permute-done.1.got.got1 = bf16[320,512]{1,0:T(8,128)(2,1)S(1)} collective-permute-done((bf16[320,512]{1,0:T(8,128)(2,1)S(1)}, bf16[320,512]{1,0:T(8,128)(2,1)S(1)}, u32[]{:S(2)}, u32[]{:S(2)}) %collective-permute-start.1) | collective-permute-done | bytes 327712 | tf_op jit(solution)/shard_map/ppermute | solution.py:443
  13.0 0.1 shard_map.79
  13.1 2.2 %collective-permute-start.3 = (bf16[192,512]{1,0:T(8,128)(2,1)S(1)}, bf16[192,512]{1,0:T(8,128)(2,1)S(1)}, u32[]{:S(2)}, u32[]{:S(2)}) collective-permute-start(bf16[192,512]{1,0:T(8,128)(2,1)S(1)} %get-tuple-element.28), channel_id=1, source_target_pairs={{0,8},{1,3},{2,10},{3,1},{4,12},{5,7},{6,14},{7,5},{8,0},{9,11},{1... | collective-permute-start | bytes 589832 | tf_op jit(solution)/shard_map/ppermute | solution.py:443
  15.3 3.6 %collective-permute-done.3.got.got2.got_b = bf16[192,512]{1,0:T(8,128)(2,1)S(1)} collective-permute-done((bf16[192,512]{1,0:T(8,128)(2,1)S(1)}, bf16[192,512]{1,0:T(8,128)(2,1)S(1)}, u32[]{:S(2)}, u32[]{:S(2)}) %collective-permute-start.3) | collective-permute-done | bytes 196640 | tf_op jit(solution)/shard_map/ppermute | solution.py:443
  19.0 0.5 collective-permute-start.6
  19.5 2.0 %collective-permute-start.4 = (bf16[64,512]{1,0:T(8,128)(2,1)S(1)}, bf16[64,512]{1,0:T(8,128)(2,1)S(1)}, u32[]{:S(2)}, u32[]{:S(2)}) collective-permute-start(bf16[64,512]{1,0:T(8,128)(2,1)S(1)} %get-tuple-element.29), channel_id=1, source_target_pairs={{0,4},{1,17},{2,6},{3,19},{4,0},{5,21},{6,2},{7,23},{8,12},{9,25},... | collective-permute-start | bytes 196616 | tf_op jit(solution)/shard_map/ppermute | solution.py:443
  21.5 1.5 %collective-permute-start.5 = (bf16[64,512]{1,0:T(8,128)(2,1)S(1)}, bf16[64,512]{1,0:T(8,128)(2,1)S(1)}, u32[]{:S(2)}, u32[]{:S(2)}) collective-permute-start(bf16[64,512]{1,0:T(8,128)(2,1)S(1)} %get-tuple-element.30), channel_id=1, source_target_pairs={{0,12},{1,19},{2,14},{3,17},{4,8},{5,23},{6,10},{7,21},{8,4},{9,27... | collective-permute-start | bytes 196616 | tf_op jit(solution)/shard_map/ppermute | solution.py:443
  23.0 2.2 %shard_map.81.more.hops = bf16[5,800,400]{2,1,0:T(8,128)(2,1)S(1)} custom-call(bf16[9,800,400]{2,1,0:T(8,128)(2,1)} %bitcast.15), custom_call_target="tpu_custom_call" | custom-call | flops 100000000 | bytes 2000000 | tf_op jit(solution)/shard_map/pallas_call | solution.py:62
  25.2 1.4 %shard_map.80.hops = bf16[2,800,400]{2,1,0:T(8,128)(2,1)S(1)} custom-call(bf16[9,800,400]{2,1,0:T(8,128)(2,1)} %bitcast.16), custom_call_target="tpu_custom_call" | custom-call | flops 100000000 | bytes 2000000 | tf_op jit(solution)/shard_map/pallas_call | solution.py:62
  26.6 1.2 %shard_map.82 = (f32[800,128]{1,0:T(8,128)S(1)}, bf16[400,128]{1,0:T(8,128)(2,1)S(1)}) custom-call(bf16[64,512]{1,0:T(8,128)(2,1)S(1)} %get-tuple-element.26.pair, bf16[320,512]{1,0:T(8,128)(2,1)S(1)} %collective-permute-done.1.got.got1, bf16[64,512]{1,0:T(8,128)(2,1)S(1)} %collective-permute-done.6.crossed, bf16[2,800,400]{2,1,0:T(8,128)(2,1)S(1)} %shard_map.80.hops, ...), custom_call_target="tpu_custom_call" | custom-call | flops 100000000 | bytes 2000000 | tf_op jit(solution)/shard_map/pallas_call | solution.py:62
  27.8 1.4 %shard_map.84 = (f32[800,128]{1,0:T(8,128)S(1)}, bf16[2,800,400]{2,1,0:T(8,128)(2,1)S(1)}) custom-call(bf16[400,128]{1,0:T(8,128)(2,1)S(1)} %get-tuple-element.33.own, bf16[192,512]{1,0:T(8,128)(2,1)S(1)} %collective-permute-done.3.got.got2.got_b, bf16[320,512]{1,0:T(8,128)(2,1)S(1)} %collective-permute-done.1.got.got1, ...), custom_call_target="tpu_custom_call" | custom-call | flops 100000000 | bytes 2000000 | tf_op jit(solution)/shard_map/pallas_call | solution.py:62
  29.3 1.7 %shard_map.85 = (bf16[800,128]{1,0:T(8,128)(2,1)S(1)}, bf16[32,512]{1,0:T(8,128)(2,1)S(1)}) custom-call(bf16[400,128]{1,0:T(8,128)(2,1)S(1)} %get-tuple-element.33.own, bf16[192,512]{1,0:T(8,128)(2,1)S(1)} %collective-permute-done.3.got.got2.got_b, bf16[192,512]{1,0:T(8,128)(2,1)S(1)} %collective-permute-done.7.cross, ...), custom_call_target="tpu_custom_call" | custom-call | flops 100000000 | bytes 2000000 | tf_op jit(solution)/shard_map/pallas_call | solution.py:62
  31.0 2.7 %collective-permute-start.8 = (bf16[96,512]{1,0:T(8,128)(2,1)S(1)}, bf16[96,512]{1,0:T(8,128)(2,1)S(1)}, u32[]{:S(2)}, u32[]{:S(2)}) collective-permute-start(bf16[96,512]{1,0:T(8,128)(2,1)S(1)} %shard_map.86.pay), channel_id=1, source_target_pairs={{0,16},{1,9},{2,18},{3,11},{4,20},{5,13},{6,22},{7,15},{8,24},{9,1... | collective-permute-start | bytes 294920 | tf_op jit(solution)/shard_map/ppermute | solution.py:443
  33.7 3.5 %collective-permute-done.8.got = bf16[96,512]{1,0:T(8,128)(2,1)S(1)} collective-permute-done((bf16[96,512]{1,0:T(8,128)(2,1)S(1)}, bf16[96,512]{1,0:T(8,128)(2,1)S(1)}, u32[]{:S(2)}, u32[]{:S(2)}) %collective-permute-start.8) | collective-permute-done | bytes 98336 | tf_op jit(solution)/shard_map/ppermute | solution.py:443
  37.3 1.9 %collective-permute-start.9 = (bf16[64,512]{1,0:T(8,128)(2,1)S(1)}, bf16[64,512]{1,0:T(8,128)(2,1)S(1)}, u32[]{:S(2)}, u32[]{:S(2)}) collective-permute-start(bf16[64,512]{1,0:T(8,128)(2,1)S(1)} %shard_map.87.pay), channel_id=1, source_target_pairs={{0,4},{1,17},{2,6},{3,19},{4,0},{5,21},{6,2},{7,23},{8,12},{9,25},... | collective-permute-start | bytes 196616 | tf_op jit(solution)/shard_map/ppermute | solution.py:443
  39.2 2.4 %collective-permute-done.9.got = bf16[64,512]{1,0:T(8,128)(2,1)S(1)} collective-permute-done((bf16[64,512]{1,0:T(8,128)(2,1)S(1)}, bf16[64,512]{1,0:T(8,128)(2,1)S(1)}, u32[]{:S(2)}, u32[]{:S(2)}) %collective-permute-start.9) | collective-permute-done | bytes 65568 | tf_op jit(solution)/shard_map/ppermute | solution.py:443
  41.7 2.1 %collective-permute-start.11 = (bf16[96,512]{1,0:T(8,128)(2,1)S(1)}, bf16[96,512]{1,0:T(8,128)(2,1)S(1)}, u32[]{:S(2)}, u32[]{:S(2)}) collective-permute-start(bf16[96,512]{1,0:T(8,128)(2,1)S(1)} %shard_map.88.pay), channel_id=1, source_target_pairs={{0,2},{1,5},{2,0},{3,7},{4,6},{5,1},{6,4},{7,3},{8,10},{9,13},{10,... | collective-permute-start | bytes 294920 | tf_op jit(solution)/shard_map/ppermute | solution.py:443
  43.8 1.4 %collective-permute-start.12 = (bf16[96,512]{1,0:T(8,128)(2,1)S(1)}, bf16[96,512]{1,0:T(8,128)(2,1)S(1)}, u32[]{:S(2)}, u32[]{:S(2)}) collective-permute-start(bf16[96,512]{1,0:T(8,128)(2,1)S(1)} %shard_map.88.pay), channel_id=1, source_target_pairs={{0,10},{1,7},{2,8},{3,5},{4,14},{5,3},{6,12},{7,1},{8,2},{9,15},{1... | collective-permute-start | bytes 294920 | tf_op jit(solution)/shard_map/ppermute | solution.py:443
  45.2 1.1 %collective-permute-done.10.got_a = bf16[96,512]{1,0:T(8,128)(2,1)S(1)} collective-permute-done((bf16[96,512]{1,0:T(8,128)(2,1)S(1)}, bf16[96,512]{1,0:T(8,128)(2,1)S(1)}, u32[]{:S(2)}, u32[]{:S(2)}) %collective-permute-start.10) | collective-permute-done | bytes 98336 | tf_op jit(solution)/shard_map/ppermute | solution.py:443
  46.3 0.3 collective-permute-done.11.got_b
  46.6 2.7 %collective-permute-done.12.got_ab = bf16[96,512]{1,0:T(8,128)(2,1)S(1)} collective-permute-done((bf16[96,512]{1,0:T(8,128)(2,1)S(1)}, bf16[96,512]{1,0:T(8,128)(2,1)S(1)}, u32[]{:S(2)}, u32[]{:S(2)}) %collective-permute-start.12) | collective-permute-done | bytes 98336 | tf_op jit(solution)/shard_map/ppermute | solution.py:443
  49.5 1.4 %shard_map.92 = bf16[800,512]{1,0:T(8,128)(2,1)} custom-call(bf16[800,512]{1,0:T(8,128)(2,1)S(1)} %get-tuple-element.21.basis, bf16[512,512]{1,0:T(8,128)(2,1)S(1)} %copy-done), custom_call_target="tpu_custom_call" | custom-call | flops 100000000 | bytes 2000000 | tf_op jit(solution)/shard_map/pallas_call | solution.py:62
  50.8 1.6 %shard_map.93 = bf16[800,512]{1,0:T(8,128)(2,1)} custom-call(bf16[800,496]{1,0:T(8,128)(2,1)S(1)} %get-tuple-element.22.images, bf16[800,128]{1,0:T(8,128)(2,1)S(1)} %get-tuple-element.38.masked, bf16[512,512]{1,0:T(8,128)(2,1)S(1)} %copy-done), custom_call_target="tpu_custom_call" | custom-call | flops 100000000 | bytes 2000000 | tf_op jit(solution)/shard_map/pallas_call | solution.py:62
  52.4 0.8 %shard_map.90.begun = f32[512,512]{1,0:T(8,128)} custom-call(bf16[288,512]{1,0:T(8,128)(2,1)S(1)} %shard_map.89.pay), custom_call_target="tpu_custom_call" | custom-call | flops 100000000 | bytes 2000000 | tf_op jit(solution)/shard_map/pallas_call | solution.py:62
  53.2 0.9 %shard_map.91 = f32[512,512]{1,0:T(8,128)} custom-call(bf16[288,512]{1,0:T(8,128)(2,1)S(1)} %shard_map.89.pay, bf16[288,512]{1,0:T(8,128)(2,1)S(1)} %collective-permute-done.13.got, f32[512,512]{1,0:T(8,128)} %shard_map.90.begun), custom_call_target="tpu_custom_call", output_to_operand_aliasing={{}: (2, {})} | custom-call | flops 100000000 | bytes 2000000 | tf_op jit(solution)/shard_map/pallas_call | solution.py:62
  (17 shorter events, 0.4 us)
Async XLA Ops:
  2.7 2.1 %collective-permute-start = (bf16[544,512]{1,0:T(8,128)(2,1)S(1)}, bf16[544,512]{1,0:T(8,128)(2,1)S(1)}, u32[]{:S(2)}, u32[]{:S(2)}) collective-permute-start(bf16[544,512]{1,0:T(8,128)(2,1)S(1)} %get-tuple-element.23.pay), channel_id=1, source_target_pairs={{0,1},{1,0},{2,3},{3,2},{4,5},{5,4},{6,7},{7,6},{8,9},{9,8},{10,11... | collective-permute-start | bytes 1671176 | tf_op jit(solution)/shard_map/ppermute | solution.py:443
  5.1 8.0 %collective-permute-start.1 = (bf16[320,512]{1,0:T(8,128)(2,1)S(1)}, bf16[320,512]{1,0:T(8,128)(2,1)S(1)}, u32[]{:S(2)}, u32[]{:S(2)}) collective-permute-start(bf16[320,512]{1,0:T(8,128)(2,1)S(1)} %get-tuple-element.25), channel_id=1, source_target_pairs={{0,2},{1,5},{2,0},{3,7},{4,6},{5,1},{6,4},{7,3},{8,10},{9,13},{10,... | collective-permute-start | bytes 983048 | tf_op jit(solution)/shard_map/ppermute | solution.py:443
  8.0 0.7 %collective-permute-start.2 = (bf16[64,512]{1,0:T(8,128)(2,1)S(1)}, bf16[64,512]{1,0:T(8,128)(2,1)S(1)}, u32[]{:S(2)}, u32[]{:S(2)}) collective-permute-start(bf16[64,512]{1,0:T(8,128)(2,1)S(1)} %get-tuple-element.26.pair), channel_id=1, source_target_pairs={{1,17},{3,19},{5,21},{7,23},{9,25},{11,27},{13,29},{15,31},{17,1},... | collective-permute-start | bytes 196616 | tf_op jit(solution)/shard_map/ppermute | solution.py:443
  13.1 5.8 %collective-permute-start.3 = (bf16[192,512]{1,0:T(8,128)(2,1)S(1)}, bf16[192,512]{1,0:T(8,128)(2,1)S(1)}, u32[]{:S(2)}, u32[]{:S(2)}) collective-permute-start(bf16[192,512]{1,0:T(8,128)(2,1)S(1)} %get-tuple-element.28), channel_id=1, source_target_pairs={{0,8},{1,3},{2,10},{3,1},{4,12},{5,7},{6,14},{7,5},{8,0},{9,11},{1... | collective-permute-start | bytes 589832 | tf_op jit(solution)/shard_map/ppermute | solution.py:443
  18.9 10.3 %collective-permute-start.7 = (bf16[192,512]{1,0:T(8,128)(2,1)S(1)}, bf16[192,512]{1,0:T(8,128)(2,1)S(1)}, u32[]{:S(2)}, u32[]{:S(2)}) collective-permute-start(bf16[192,512]{1,0:T(8,128)(2,1)S(1)} %shard_map.83), channel_id=1, source_target_pairs={{0,1},{1,0},{2,3},{3,2},{4,5},{5,4},{6,7},{7,6},{8,9},{9,8},{10,11... | collective-permute-start | bytes 589832 | tf_op jit(solution)/shard_map/ppermute | solution.py:443
  19.0 7.6 %collective-permute-start.6 = (bf16[64,512]{1,0:T(8,128)(2,1)S(1)}, bf16[64,512]{1,0:T(8,128)(2,1)S(1)}, u32[]{:S(2)}, u32[]{:S(2)}) collective-permute-start(bf16[64,512]{1,0:T(8,128)(2,1)S(1)} %slice.4), channel_id=1, source_target_pairs={{0,1},{1,0},{2,3},{3,2},{4,5},{5,4},{6,7},{7,6},{8,9},{9,8},{10,11... | collective-permute-start | bytes 196616 | tf_op jit(solution)/shard_map/ppermute | solution.py:443
  19.5 11.4 %collective-permute-start.4 = (bf16[64,512]{1,0:T(8,128)(2,1)S(1)}, bf16[64,512]{1,0:T(8,128)(2,1)S(1)}, u32[]{:S(2)}, u32[]{:S(2)}) collective-permute-start(bf16[64,512]{1,0:T(8,128)(2,1)S(1)} %get-tuple-element.29), channel_id=1, source_target_pairs={{0,4},{1,17},{2,6},{3,19},{4,0},{5,21},{6,2},{7,23},{8,12},{9,25},... | collective-permute-start | bytes 196616 | tf_op jit(solution)/shard_map/ppermute | solution.py:443
  21.5 9.5 %collective-permute-start.5 = (bf16[64,512]{1,0:T(8,128)(2,1)S(1)}, bf16[64,512]{1,0:T(8,128)(2,1)S(1)}, u32[]{:S(2)}, u32[]{:S(2)}) collective-permute-start(bf16[64,512]{1,0:T(8,128)(2,1)S(1)} %get-tuple-element.30), channel_id=1, source_target_pairs={{0,12},{1,19},{2,14},{3,17},{4,8},{5,23},{6,10},{7,21},{8,4},{9,27... | collective-permute-start | bytes 196616 | tf_op jit(solution)/shard_map/ppermute | solution.py:443
  29.3 20.2 %copy-start = (bf16[512,512]{1,0:T(8,128)(2,1)S(1)}, bf16[512,512]{1,0:T(8,128)(2,1)}, u32[]{:S(2)}) copy-start(bf16[512,512]{1,0:T(8,128)(2,1)} %rotation.3) | copy-start | bytes 1572868
  31.0 6.2 %collective-permute-start.8 = (bf16[96,512]{1,0:T(8,128)(2,1)S(1)}, bf16[96,512]{1,0:T(8,128)(2,1)S(1)}, u32[]{:S(2)}, u32[]{:S(2)}) collective-permute-start(bf16[96,512]{1,0:T(8,128)(2,1)S(1)} %shard_map.86.pay), channel_id=1, source_target_pairs={{0,16},{1,9},{2,18},{3,11},{4,20},{5,13},{6,22},{7,15},{8,24},{9,1... | collective-permute-start | bytes 294920 | tf_op jit(solution)/shard_map/ppermute | solution.py:443
  37.3 4.3 %collective-permute-start.9 = (bf16[64,512]{1,0:T(8,128)(2,1)S(1)}, bf16[64,512]{1,0:T(8,128)(2,1)S(1)}, u32[]{:S(2)}, u32[]{:S(2)}) collective-permute-start(bf16[64,512]{1,0:T(8,128)(2,1)S(1)} %shard_map.87.pay), channel_id=1, source_target_pairs={{0,4},{1,17},{2,6},{3,19},{4,0},{5,21},{6,2},{7,23},{8,12},{9,25},... | collective-permute-start | bytes 196616 | tf_op jit(solution)/shard_map/ppermute | solution.py:443
  41.6 4.7 %collective-permute-start.10 = (bf16[96,512]{1,0:T(8,128)(2,1)S(1)}, bf16[96,512]{1,0:T(8,128)(2,1)S(1)}, u32[]{:S(2)}, u32[]{:S(2)}) collective-permute-start(bf16[96,512]{1,0:T(8,128)(2,1)S(1)} %shard_map.88.pay), channel_id=1, source_target_pairs={{0,8},{1,3},{2,10},{3,1},{4,12},{5,7},{6,14},{7,5},{8,0},{9,11},{1... | collective-permute-start | bytes 294920 | tf_op jit(solution)/shard_map/ppermute | solution.py:443
  41.7 4.9 %collective-permute-start.11 = (bf16[96,512]{1,0:T(8,128)(2,1)S(1)}, bf16[96,512]{1,0:T(8,128)(2,1)S(1)}, u32[]{:S(2)}, u32[]{:S(2)}) collective-permute-start(bf16[96,512]{1,0:T(8,128)(2,1)S(1)} %shard_map.88.pay), channel_id=1, source_target_pairs={{0,2},{1,5},{2,0},{3,7},{4,6},{5,1},{6,4},{7,3},{8,10},{9,13},{10,... | collective-permute-start | bytes 294920 | tf_op jit(solution)/shard_map/ppermute | solution.py:443
  43.8 5.5 %collective-permute-start.12 = (bf16[96,512]{1,0:T(8,128)(2,1)S(1)}, bf16[96,512]{1,0:T(8,128)(2,1)S(1)}, u32[]{:S(2)}, u32[]{:S(2)}) collective-permute-start(bf16[96,512]{1,0:T(8,128)(2,1)S(1)} %shard_map.88.pay), channel_id=1, source_target_pairs={{0,10},{1,7},{2,8},{3,5},{4,14},{5,3},{6,12},{7,1},{8,2},{9,15},{1... | collective-permute-start | bytes 294920 | tf_op jit(solution)/shard_map/ppermute | solution.py:443
  49.4 3.8 %collective-permute-start.13 = (bf16[288,512]{1,0:T(8,128)(2,1)S(1)}, bf16[288,512]{1,0:T(8,128)(2,1)S(1)}, u32[]{:S(2)}, u32[]{:S(2)}) collective-permute-start(bf16[288,512]{1,0:T(8,128)(2,1)S(1)} %shard_map.89.pay), channel_id=1, source_target_pairs={{0,1},{1,0},{2,3},{3,2},{4,5},{5,4},{6,7},{7,6},{8,9},{9,8},{10,11... | collective-permute-start | bytes 884744 | tf_op jit(solution)/shard_map/ppermute | solution.py:443

commit v7 on v6

--- a/solution.py
+++ b/solution.py
@@ -247,7 +247,7 @@
     return copies
 
 
-def near_kernel(here, later, pair, got, crossed, hops, more, perms, shift, total, own_out):
+def near_kernel(here, pair, got, crossed, hops, perms, shift, total, own_out):
     core, half, _, _, _ = place()
     each = pair.shape[0]
     wide = own_out.shape[1]
@@ -257,7 +257,6 @@
     own_out[...] = own
     rows = total.shape[0]
     terms = [(hops, i, hop) for i, hop in enumerate(here)]
-    terms += [(more, more.shape[0] - len(later) + i, hop) for i, hop in enumerate(later)]
     mixed = [dot_nn(own, perms[hop, :wide, :]).astype(BF16) for _, _, hop in terms]
     step = rows // 2
     for r in range(2):
@@ -273,7 +272,7 @@
     return dot_nn(jnp.concatenate([own[...], site], axis=1), perms[hop]).astype(BF16)
 
 
-def middle_kernel(ahead, own, got2, got1, total, hops, hops_far, perms, shift, out, next_hops, sems):
+def middle_kernel(ahead, later, own, got2, got1, total, hops, hops_far, perms, shift, out, next_hops, sems):
     copies = pulled(ahead, hops_far, next_hops, sems)
     core, half, _, _, _ = place()
     first = core == 0
@@ -286,12 +285,16 @@
         half_site(move, jnp.where(first, mine[each:], mine[:each])),
     )
     mixed = [mixture(perms, own, site, 2 + core + 3 * i) for i in range(2)]
+    wide = own.shape[1]
+    plain = [dot_nn(own[...], perms[hop, :wide, :]).astype(BF16) for hop in later]
     step = out.shape[0] // 2
     for r in range(2):
         span = pl.ds(r * step, step)
         part = total[span, :]
         for i in range(2):
             part = part + dot_nn(hops[2 * core + i, span, :], mixed[i])
+        for i, term in enumerate(plain):
+            part = part + dot_nn(hops[4 + i, span, :], term)
         out[span, :] = part
     for copy in copies:
         copy.wait()
@@ -509,7 +512,7 @@
     got2 = send(pay2, z0_hop, x_hop)
     crossed = send(got1[half:, :], core_hop, core_hop)
     total, own = call(
-        functools.partial(near_kernel, groups[0], groups[2]),
+        functools.partial(near_kernel, groups[0]),
         (
             shaped(rows, wide, F32),
             shaped(coarse, wide, BF16),
@@ -518,7 +521,6 @@
         got1,
         crossed,
         near_hops,
-        more_hops,
         perms,
         shift,
     )
@@ -531,7 +533,7 @@
     cross_pay = call(fourth_kernel, shaped(6 * chunk, nvec, BF16), got2, far)
     cross = send(cross_pay, core_hop, core_hop)
     total, next_hops = call(
-        functools.partial(middle_kernel, groups[3]),
+        functools.partial(middle_kernel, groups[3], groups[2]),
         (shaped(rows, wide, F32), jax.ShapeDtypeStruct((len(groups[3]), rows, coarse), BF16)),
         own,
         got2,

time: 54.3 us -> 54.1 us (level)
  no operation moved by 1% of the time
where the time goes in v7:
time: 54.1 us; the launch traced here: 53.8 us
  waiting for transfers between devices  19.3 us (36%)
  starting transfers between devices  18.5 us (34%)
  Pallas kernels  15.2 us (28%)
  between operations  0.84 us (2%)
    ppermute x14, waiting for transfers between devices, send(): return lax.ppermute(x, BOTH, pairs)  19.3 us
    ppermute x14, starting transfers between devices, send(): return lax.ppermute(x, BOTH, pairs)  18.5 us
    pallas_call x18, Pallas kernels, call(): pl.pallas_call(kernel, out_shape=outs, in_specs=[scalars if i in smem els...  15.2 us
  transfers between devices with their start and end apart: 14, of which 8 were waited for; matrix products, arithmetic and copies ran while one was open for 0% of the time, Pallas kernels for 22%

profile of v7, /device:TPU:0, one launch (start us, length us, event | category | flops | bytes accessed | tf_op | source)
XLA Modules:
  0.0 53.8 jit_solution(3398949346654574664)
XLA Ops:
  0.6 2.1 %shard_map.76 = (bf16[544,512]{1,0:T(8,128)(2,1)S(1)}, bf16[800,512]{1,0:T(8,128)(2,1)S(1)}, bf16[800,496]{1,0:T(8,128)(2,1)S(1)}, bf16[200,256]{1,0:T(8,128)(2,1)S(1)}, bf16[9,256,128]{2,1,0:T(8,128)(2,1)S(1)}) custom-call(bf16[800,512]{1,0:T(8,128)(2,1)} %bitcast.18, bf16[800,496]{1,0:T(8,128)(2,1)} %bitcast.19, s32[8,8]{1,0:T(8,128)} %table_far.1), custom_call_target="tpu_custom_call" | custom-call | flops 100000000 | bytes 2000000 | tf_op jit(solution)/shard_map/pallas_call | solution.py:62
  2.7 0.6 %collective-permute-start = (bf16[544,512]{1,0:T(8,128)(2,1)S(1)}, bf16[544,512]{1,0:T(8,128)(2,1)S(1)}, u32[]{:S(2)}, u32[]{:S(2)}) collective-permute-start(bf16[544,512]{1,0:T(8,128)(2,1)S(1)} %get-tuple-element.23.pay), channel_id=1, source_target_pairs={{0,1},{1,0},{2,3},{3,2},{4,5},{5,4},{6,7},{7,6},{8,9},{9,8},{10,11... | collective-permute-start | bytes 1671176 | tf_op jit(solution)/shard_map/ppermute | solution.py:446
  3.3 0.5 shard_map.77.kept
  3.8 1.1 %collective-permute-done.got = bf16[544,512]{1,0:T(8,128)(2,1)S(1)} collective-permute-done((bf16[544,512]{1,0:T(8,128)(2,1)S(1)}, bf16[544,512]{1,0:T(8,128)(2,1)S(1)}, u32[]{:S(2)}, u32[]{:S(2)}) %collective-permute-start) | collective-permute-done | bytes 557088 | tf_op jit(solution)/shard_map/ppermute | solution.py:446
  4.9 0.2 shard_map.78
  5.1 2.9 %collective-permute-start.1 = (bf16[320,512]{1,0:T(8,128)(2,1)S(1)}, bf16[320,512]{1,0:T(8,128)(2,1)S(1)}, u32[]{:S(2)}, u32[]{:S(2)}) collective-permute-start(bf16[320,512]{1,0:T(8,128)(2,1)S(1)} %get-tuple-element.25), channel_id=1, source_target_pairs={{0,2},{1,5},{2,0},{3,7},{4,6},{5,1},{6,4},{7,3},{8,10},{9,13},{10,... | collective-permute-start | bytes 983048 | tf_op jit(solution)/shard_map/ppermute | solution.py:446
  8.0 0.7 %collective-permute-start.2 = (bf16[64,512]{1,0:T(8,128)(2,1)S(1)}, bf16[64,512]{1,0:T(8,128)(2,1)S(1)}, u32[]{:S(2)}, u32[]{:S(2)}) collective-permute-start(bf16[64,512]{1,0:T(8,128)(2,1)S(1)} %get-tuple-element.26.pair), channel_id=1, source_target_pairs={{1,17},{3,19},{5,21},{7,23},{9,25},{11,27},{13,29},{15,31},{17,1},... | collective-permute-start | bytes 196616 | tf_op jit(solution)/shard_map/ppermute | solution.py:446
  8.6 4.4 %collective-permute-done.1.got.got1 = bf16[320,512]{1,0:T(8,128)(2,1)S(1)} collective-permute-done((bf16[320,512]{1,0:T(8,128)(2,1)S(1)}, bf16[320,512]{1,0:T(8,128)(2,1)S(1)}, u32[]{:S(2)}, u32[]{:S(2)}) %collective-permute-start.1) | collective-permute-done | bytes 327712 | tf_op jit(solution)/shard_map/ppermute | solution.py:446
  13.0 0.1 shard_map.79
  13.1 2.2 %collective-permute-start.3 = (bf16[192,512]{1,0:T(8,128)(2,1)S(1)}, bf16[192,512]{1,0:T(8,128)(2,1)S(1)}, u32[]{:S(2)}, u32[]{:S(2)}) collective-permute-start(bf16[192,512]{1,0:T(8,128)(2,1)S(1)} %get-tuple-element.28), channel_id=1, source_target_pairs={{0,8},{1,3},{2,10},{3,1},{4,12},{5,7},{6,14},{7,5},{8,0},{9,11},{1... | collective-permute-start | bytes 589832 | tf_op jit(solution)/shard_map/ppermute | solution.py:446
  15.3 3.6 %collective-permute-done.3.got.got2.got_b = bf16[192,512]{1,0:T(8,128)(2,1)S(1)} collective-permute-done((bf16[192,512]{1,0:T(8,128)(2,1)S(1)}, bf16[192,512]{1,0:T(8,128)(2,1)S(1)}, u32[]{:S(2)}, u32[]{:S(2)}) %collective-permute-start.3) | collective-permute-done | bytes 196640 | tf_op jit(solution)/shard_map/ppermute | solution.py:446
  19.0 0.5 collective-permute-start.6
  19.5 2.0 %collective-permute-start.4 = (bf16[64,512]{1,0:T(8,128)(2,1)S(1)}, bf16[64,512]{1,0:T(8,128)(2,1)S(1)}, u32[]{:S(2)}, u32[]{:S(2)}) collective-permute-start(bf16[64,512]{1,0:T(8,128)(2,1)S(1)} %get-tuple-element.29), channel_id=1, source_target_pairs={{0,4},{1,17},{2,6},{3,19},{4,0},{5,21},{6,2},{7,23},{8,12},{9,25},... | collective-permute-start | bytes 196616 | tf_op jit(solution)/shard_map/ppermute | solution.py:446
  21.5 1.5 %collective-permute-start.5 = (bf16[64,512]{1,0:T(8,128)(2,1)S(1)}, bf16[64,512]{1,0:T(8,128)(2,1)S(1)}, u32[]{:S(2)}, u32[]{:S(2)}) collective-permute-start(bf16[64,512]{1,0:T(8,128)(2,1)S(1)} %get-tuple-element.30), channel_id=1, source_target_pairs={{0,12},{1,19},{2,14},{3,17},{4,8},{5,23},{6,10},{7,21},{8,4},{9,27... | collective-permute-start | bytes 196616 | tf_op jit(solution)/shard_map/ppermute | solution.py:446
  23.0 1.4 %shard_map.80.hops = bf16[2,800,400]{2,1,0:T(8,128)(2,1)S(1)} custom-call(bf16[9,800,400]{2,1,0:T(8,128)(2,1)} %bitcast.15), custom_call_target="tpu_custom_call" | custom-call | flops 100000000 | bytes 2000000 | tf_op jit(solution)/shard_map/pallas_call | solution.py:62
  24.4 2.2 %shard_map.83.hops.more = bf16[5,800,400]{2,1,0:T(8,128)(2,1)S(1)} custom-call(bf16[9,800,400]{2,1,0:T(8,128)(2,1)} %bitcast.16), custom_call_target="tpu_custom_call" | custom-call | flops 100000000 | bytes 2000000 | tf_op jit(solution)/shard_map/pallas_call | solution.py:62
  26.6 0.9 %shard_map.81 = (f32[800,128]{1,0:T(8,128)S(1)}, bf16[400,128]{1,0:T(8,128)(2,1)S(1)}) custom-call(bf16[64,512]{1,0:T(8,128)(2,1)S(1)} %get-tuple-element.26.pair, bf16[320,512]{1,0:T(8,128)(2,1)S(1)} %collective-permute-done.1.got.got1, bf16[64,512]{1,0:T(8,128)(2,1)S(1)} %collective-permute-done.6.crossed, bf16[2,800,400]{2,1,0:T(8,128)(2,1)S(1)} %shard_map.80.hops, ...), custom_call_target="tpu_custom_call" | custom-call | flops 100000000 | bytes 2000000 | tf_op jit(solution)/shard_map/pallas_call | solution.py:62
  27.5 1.4 %shard_map.84 = (f32[800,128]{1,0:T(8,128)S(1)}, bf16[2,800,400]{2,1,0:T(8,128)(2,1)S(1)}) custom-call(bf16[400,128]{1,0:T(8,128)(2,1)S(1)} %get-tuple-element.33.own, bf16[192,512]{1,0:T(8,128)(2,1)S(1)} %collective-permute-done.3.got.got2.got_b, bf16[320,512]{1,0:T(8,128)(2,1)S(1)} %collective-permute-done.1.got.got1, ...), custom_call_target="tpu_custom_call" | custom-call | flops 100000000 | bytes 2000000 | tf_op jit(solution)/shard_map/pallas_call | solution.py:62
  29.0 1.7 %shard_map.85 = (bf16[800,128]{1,0:T(8,128)(2,1)S(1)}, bf16[32,512]{1,0:T(8,128)(2,1)S(1)}) custom-call(bf16[400,128]{1,0:T(8,128)(2,1)S(1)} %get-tuple-element.33.own, bf16[192,512]{1,0:T(8,128)(2,1)S(1)} %collective-permute-done.3.got.got2.got_b, bf16[192,512]{1,0:T(8,128)(2,1)S(1)} %collective-permute-done.7.cross, ...), custom_call_target="tpu_custom_call" | custom-call | flops 100000000 | bytes 2000000 | tf_op jit(solution)/shard_map/pallas_call | solution.py:62
  30.7 2.6 %collective-permute-start.8 = (bf16[96,512]{1,0:T(8,128)(2,1)S(1)}, bf16[96,512]{1,0:T(8,128)(2,1)S(1)}, u32[]{:S(2)}, u32[]{:S(2)}) collective-permute-start(bf16[96,512]{1,0:T(8,128)(2,1)S(1)} %shard_map.86.pay), channel_id=1, source_target_pairs={{0,16},{1,9},{2,18},{3,11},{4,20},{5,13},{6,22},{7,15},{8,24},{9,1... | collective-permute-start | bytes 294920 | tf_op jit(solution)/shard_map/ppermute | solution.py:446
  33.4 3.5 %collective-permute-done.8.got = bf16[96,512]{1,0:T(8,128)(2,1)S(1)} collective-permute-done((bf16[96,512]{1,0:T(8,128)(2,1)S(1)}, bf16[96,512]{1,0:T(8,128)(2,1)S(1)}, u32[]{:S(2)}, u32[]{:S(2)}) %collective-permute-start.8) | collective-permute-done | bytes 98336 | tf_op jit(solution)/shard_map/ppermute | solution.py:446
  37.0 1.9 %collective-permute-start.9 = (bf16[64,512]{1,0:T(8,128)(2,1)S(1)}, bf16[64,512]{1,0:T(8,128)(2,1)S(1)}, u32[]{:S(2)}, u32[]{:S(2)}) collective-permute-start(bf16[64,512]{1,0:T(8,128)(2,1)S(1)} %shard_map.87.pay), channel_id=1, source_target_pairs={{0,4},{1,17},{2,6},{3,19},{4,0},{5,21},{6,2},{7,23},{8,12},{9,25},... | collective-permute-start | bytes 196616 | tf_op jit(solution)/shard_map/ppermute | solution.py:446
  38.9 2.4 %collective-permute-done.9.got = bf16[64,512]{1,0:T(8,128)(2,1)S(1)} collective-permute-done((bf16[64,512]{1,0:T(8,128)(2,1)S(1)}, bf16[64,512]{1,0:T(8,128)(2,1)S(1)}, u32[]{:S(2)}, u32[]{:S(2)}) %collective-permute-start.9) | collective-permute-done | bytes 65568 | tf_op jit(solution)/shard_map/ppermute | solution.py:446
  41.4 2.1 %collective-permute-start.11 = (bf16[96,512]{1,0:T(8,128)(2,1)S(1)}, bf16[96,512]{1,0:T(8,128)(2,1)S(1)}, u32[]{:S(2)}, u32[]{:S(2)}) collective-permute-start(bf16[96,512]{1,0:T(8,128)(2,1)S(1)} %shard_map.88.pay), channel_id=1, source_target_pairs={{0,2},{1,5},{2,0},{3,7},{4,6},{5,1},{6,4},{7,3},{8,10},{9,13},{10,... | collective-permute-start | bytes 294920 | tf_op jit(solution)/shard_map/ppermute | solution.py:446
  43.5 1.3 %collective-permute-start.12 = (bf16[96,512]{1,0:T(8,128)(2,1)S(1)}, bf16[96,512]{1,0:T(8,128)(2,1)S(1)}, u32[]{:S(2)}, u32[]{:S(2)}) collective-permute-start(bf16[96,512]{1,0:T(8,128)(2,1)S(1)} %shard_map.88.pay), channel_id=1, source_target_pairs={{0,10},{1,7},{2,8},{3,5},{4,14},{5,3},{6,12},{7,1},{8,2},{9,15},{1... | collective-permute-start | bytes 294920 | tf_op jit(solution)/shard_map/ppermute | solution.py:446
  44.9 1.1 %collective-permute-done.10.got_a = bf16[96,512]{1,0:T(8,128)(2,1)S(1)} collective-permute-done((bf16[96,512]{1,0:T(8,128)(2,1)S(1)}, bf16[96,512]{1,0:T(8,128)(2,1)S(1)}, u32[]{:S(2)}, u32[]{:S(2)}) %collective-permute-start.10) | collective-permute-done | bytes 98336 | tf_op jit(solution)/shard_map/ppermute | solution.py:446
  46.0 0.3 collective-permute-done.11.got_b
  46.3 2.7 %collective-permute-done.12.got_ab = bf16[96,512]{1,0:T(8,128)(2,1)S(1)} collective-permute-done((bf16[96,512]{1,0:T(8,128)(2,1)S(1)}, bf16[96,512]{1,0:T(8,128)(2,1)S(1)}, u32[]{:S(2)}, u32[]{:S(2)}) %collective-permute-start.12) | collective-permute-done | bytes 98336 | tf_op jit(solution)/shard_map/ppermute | solution.py:446
  49.2 1.4 %shard_map.92 = bf16[800,512]{1,0:T(8,128)(2,1)} custom-call(bf16[800,512]{1,0:T(8,128)(2,1)S(1)} %get-tuple-element.21.basis, bf16[512,512]{1,0:T(8,128)(2,1)S(1)} %copy-done), custom_call_target="tpu_custom_call" | custom-call | flops 100000000 | bytes 2000000 | tf_op jit(solution)/shard_map/pallas_call | solution.py:62
  50.6 1.6 %shard_map.93 = bf16[800,512]{1,0:T(8,128)(2,1)} custom-call(bf16[800,496]{1,0:T(8,128)(2,1)S(1)} %get-tuple-element.22.images, bf16[800,128]{1,0:T(8,128)(2,1)S(1)} %get-tuple-element.38.masked, bf16[512,512]{1,0:T(8,128)(2,1)S(1)} %copy-done), custom_call_target="tpu_custom_call" | custom-call | flops 100000000 | bytes 2000000 | tf_op jit(solution)/shard_map/pallas_call | solution.py:62
  52.1 0.8 %shard_map.90.begun = f32[512,512]{1,0:T(8,128)} custom-call(bf16[288,512]{1,0:T(8,128)(2,1)S(1)} %shard_map.89.pay), custom_call_target="tpu_custom_call" | custom-call | flops 100000000 | bytes 2000000 | tf_op jit(solution)/shard_map/pallas_call | solution.py:62
  52.9 0.9 %shard_map.91 = f32[512,512]{1,0:T(8,128)} custom-call(bf16[288,512]{1,0:T(8,128)(2,1)S(1)} %shard_map.89.pay, bf16[288,512]{1,0:T(8,128)(2,1)S(1)} %collective-permute-done.13.got, f32[512,512]{1,0:T(8,128)} %shard_map.90.begun), custom_call_target="tpu_custom_call", output_to_operand_aliasing={{}: (2, {})} | custom-call | flops 100000000 | bytes 2000000 | tf_op jit(solution)/shard_map/pallas_call | solution.py:62
  (17 shorter events, 0.4 us)
Async XLA Ops:
  2.7 2.1 %collective-permute-start = (bf16[544,512]{1,0:T(8,128)(2,1)S(1)}, bf16[544,512]{1,0:T(8,128)(2,1)S(1)}, u32[]{:S(2)}, u32[]{:S(2)}) collective-permute-start(bf16[544,512]{1,0:T(8,128)(2,1)S(1)} %get-tuple-element.23.pay), channel_id=1, source_target_pairs={{0,1},{1,0},{2,3},{3,2},{4,5},{5,4},{6,7},{7,6},{8,9},{9,8},{10,11... | collective-permute-start | bytes 1671176 | tf_op jit(solution)/shard_map/ppermute | solution.py:446
  5.1 8.0 %collective-permute-start.1 = (bf16[320,512]{1,0:T(8,128)(2,1)S(1)}, bf16[320,512]{1,0:T(8,128)(2,1)S(1)}, u32[]{:S(2)}, u32[]{:S(2)}) collective-permute-start(bf16[320,512]{1,0:T(8,128)(2,1)S(1)} %get-tuple-element.25), channel_id=1, source_target_pairs={{0,2},{1,5},{2,0},{3,7},{4,6},{5,1},{6,4},{7,3},{8,10},{9,13},{10,... | collective-permute-start | bytes 983048 | tf_op jit(solution)/shard_map/ppermute | solution.py:446
  8.0 0.7 %collective-permute-start.2 = (bf16[64,512]{1,0:T(8,128)(2,1)S(1)}, bf16[64,512]{1,0:T(8,128)(2,1)S(1)}, u32[]{:S(2)}, u32[]{:S(2)}) collective-permute-start(bf16[64,512]{1,0:T(8,128)(2,1)S(1)} %get-tuple-element.26.pair), channel_id=1, source_target_pairs={{1,17},{3,19},{5,21},{7,23},{9,25},{11,27},{13,29},{15,31},{17,1},... | collective-permute-start | bytes 196616 | tf_op jit(solution)/shard_map/ppermute | solution.py:446
  13.1 5.8 %collective-permute-start.3 = (bf16[192,512]{1,0:T(8,128)(2,1)S(1)}, bf16[192,512]{1,0:T(8,128)(2,1)S(1)}, u32[]{:S(2)}, u32[]{:S(2)}) collective-permute-start(bf16[192,512]{1,0:T(8,128)(2,1)S(1)} %get-tuple-element.28), channel_id=1, source_target_pairs={{0,8},{1,3},{2,10},{3,1},{4,12},{5,7},{6,14},{7,5},{8,0},{9,11},{1... | collective-permute-start | bytes 589832 | tf_op jit(solution)/shard_map/ppermute | solution.py:446
  18.9 10.0 %collective-permute-start.7 = (bf16[192,512]{1,0:T(8,128)(2,1)S(1)}, bf16[192,512]{1,0:T(8,128)(2,1)S(1)}, u32[]{:S(2)}, u32[]{:S(2)}) collective-permute-start(bf16[192,512]{1,0:T(8,128)(2,1)S(1)} %shard_map.82), channel_id=1, source_target_pairs={{0,1},{1,0},{2,3},{3,2},{4,5},{5,4},{6,7},{7,6},{8,9},{9,8},{10,11... | collective-permute-start | bytes 589832 | tf_op jit(solution)/shard_map/ppermute | solution.py:446
  19.0 7.6 %collective-permute-start.6 = (bf16[64,512]{1,0:T(8,128)(2,1)S(1)}, bf16[64,512]{1,0:T(8,128)(2,1)S(1)}, u32[]{:S(2)}, u32[]{:S(2)}) collective-permute-start(bf16[64,512]{1,0:T(8,128)(2,1)S(1)} %slice.4), channel_id=1, source_target_pairs={{0,1},{1,0},{2,3},{3,2},{4,5},{5,4},{6,7},{7,6},{8,9},{9,8},{10,11... | collective-permute-start | bytes 196616 | tf_op jit(solution)/shard_map/ppermute | solution.py:446
  19.5 11.1 %collective-permute-start.4 = (bf16[64,512]{1,0:T(8,128)(2,1)S(1)}, bf16[64,512]{1,0:T(8,128)(2,1)S(1)}, u32[]{:S(2)}, u32[]{:S(2)}) collective-permute-start(bf16[64,512]{1,0:T(8,128)(2,1)S(1)} %get-tuple-element.29), channel_id=1, source_target_pairs={{0,4},{1,17},{2,6},{3,19},{4,0},{5,21},{6,2},{7,23},{8,12},{9,25},... | collective-permute-start | bytes 196616 | tf_op jit(solution)/shard_map/ppermute | solution.py:446
  21.5 9.2 %collective-permute-start.5 = (bf16[64,512]{1,0:T(8,128)(2,1)S(1)}, bf16[64,512]{1,0:T(8,128)(2,1)S(1)}, u32[]{:S(2)}, u32[]{:S(2)}) collective-permute-start(bf16[64,512]{1,0:T(8,128)(2,1)S(1)} %get-tuple-element.30), channel_id=1, source_target_pairs={{0,12},{1,19},{2,14},{3,17},{4,8},{5,23},{6,10},{7,21},{8,4},{9,27... | collective-permute-start | bytes 196616 | tf_op jit(solution)/shard_map/ppermute | solution.py:446
  29.0 20.2 %copy-start = (bf16[512,512]{1,0:T(8,128)(2,1)S(1)}, bf16[512,512]{1,0:T(8,128)(2,1)}, u32[]{:S(2)}) copy-start(bf16[512,512]{1,0:T(8,128)(2,1)} %rotation.3) | copy-start | bytes 1572868
  30.7 6.2 %collective-permute-start.8 = (bf16[96,512]{1,0:T(8,128)(2,1)S(1)}, bf16[96,512]{1,0:T(8,128)(2,1)S(1)}, u32[]{:S(2)}, u32[]{:S(2)}) collective-permute-start(bf16[96,512]{1,0:T(8,128)(2,1)S(1)} %shard_map.86.pay), channel_id=1, source_target_pairs={{0,16},{1,9},{2,18},{3,11},{4,20},{5,13},{6,22},{7,15},{8,24},{9,1... | collective-permute-start | bytes 294920 | tf_op jit(solution)/shard_map/ppermute | solution.py:446
  37.0 4.3 %collective-permute-start.9 = (bf16[64,512]{1,0:T(8,128)(2,1)S(1)}, bf16[64,512]{1,0:T(8,128)(2,1)S(1)}, u32[]{:S(2)}, u32[]{:S(2)}) collective-permute-start(bf16[64,512]{1,0:T(8,128)(2,1)S(1)} %shard_map.87.pay), channel_id=1, source_target_pairs={{0,4},{1,17},{2,6},{3,19},{4,0},{5,21},{6,2},{7,23},{8,12},{9,25},... | collective-permute-start | bytes 196616 | tf_op jit(solution)/shard_map/ppermute | solution.py:446
  41.3 4.7 %collective-permute-start.10 = (bf16[96,512]{1,0:T(8,128)(2,1)S(1)}, bf16[96,512]{1,0:T(8,128)(2,1)S(1)}, u32[]{:S(2)}, u32[]{:S(2)}) collective-permute-start(bf16[96,512]{1,0:T(8,128)(2,1)S(1)} %shard_map.88.pay), channel_id=1, source_target_pairs={{0,8},{1,3},{2,10},{3,1},{4,12},{5,7},{6,14},{7,5},{8,0},{9,11},{1... | collective-permute-start | bytes 294920 | tf_op jit(solution)/shard_map/ppermute | solution.py:446
  41.4 4.9 %collective-permute-start.11 = (bf16[96,512]{1,0:T(8,128)(2,1)S(1)}, bf16[96,512]{1,0:T(8,128)(2,1)S(1)}, u32[]{:S(2)}, u32[]{:S(2)}) collective-permute-start(bf16[96,512]{1,0:T(8,128)(2,1)S(1)} %shard_map.88.pay), channel_id=1, source_target_pairs={{0,2},{1,5},{2,0},{3,7},{4,6},{5,1},{6,4},{7,3},{8,10},{9,13},{10,... | collective-permute-start | bytes 294920 | tf_op jit(solution)/shard_map/ppermute | solution.py:446
  43.5 5.5 %collective-permute-start.12 = (bf16[96,512]{1,0:T(8,128)(2,1)S(1)}, bf16[96,512]{1,0:T(8,128)(2,1)S(1)}, u32[]{:S(2)}, u32[]{:S(2)}) collective-permute-start(bf16[96,512]{1,0:T(8,128)(2,1)S(1)} %shard_map.88.pay), channel_id=1, source_target_pairs={{0,10},{1,7},{2,8},{3,5},{4,14},{5,3},{6,12},{7,1},{8,2},{9,15},{1... | collective-permute-start | bytes 294920 | tf_op jit(solution)/shard_map/ppermute | solution.py:446
  49.1 3.8 %collective-permute-start.13 = (bf16[288,512]{1,0:T(8,128)(2,1)S(1)}, bf16[288,512]{1,0:T(8,128)(2,1)S(1)}, u32[]{:S(2)}, u32[]{:S(2)}) collective-permute-start(bf16[288,512]{1,0:T(8,128)(2,1)S(1)} %shard_map.89.pay), channel_id=1, source_target_pairs={{0,1},{1,0},{2,3},{3,2},{4,5},{5,4},{6,7},{7,6},{8,9},{9,8},{10,11... | collective-permute-start | bytes 884744 | tf_op jit(solution)/shard_map/ppermute | solution.py:446
